TPU v7x, 32 devices: a whole 2x2x4 slice. The times are simulated.
32 devices in a mesh: seq: 4 (over x, core), chan: 8 (over z, y).
Axes of the slice: x: 2, y: 2, z: 4, core: 2. Of those that a mesh axis runs over, the one named last changes fastest.
Arguments:
- frames_in: bfloat16 [8192, 4096], P('seq', 'chan'), may hold values from -6 to 6
- gate_in: bfloat16 [8192, 4096], P('seq', 'chan'), may hold values from -6 to 6
- in_keys: bfloat16 [8192, 128], P('seq'), may hold values from -6 to 6
- out_keys: bfloat16 [8192, 128], P('seq'), may hold values from -6 to 6
- step_size: float32 [8192, 64], P('seq', 'chan'), may hold values from 0 to 1.6
- decay_rate: float32 [64], P('chan'), may hold values from 0.5 to 2
- skip_gain: float32 [64], P('chan'), may hold values from 0.5 to 2
- out_weight: bfloat16 [4096, 2048], P('chan'), may hold values from -0.09375 to 0.09375
- codebook: bfloat16 [65536, 512], P('chan'), may hold values from -6 to 6
- code_index: int32 [8192, 4], P(('seq', 'chan')), may hold values from 0 to 65535, as said below
- upstream: bfloat16 [8192, 2048], P(('seq', 'chan')), may hold values from -6 to 6
Outputs:
- latent: bfloat16 [8192, 2048], P(('seq', 'chan'))
- latent_grad: float32 [8192, 2048], P(('seq', 'chan'))
- codebook_grad: float32 [65536, 512], P('chan')
Inputs may be any that keep to these rules, and one draw needn't show every extreme that they name: `code_index`: the codebook's entries fall into 8 shards of 65536 / 8 consecutive entries. Among the codes of the frames of one device (one index of seq+chan, 4 codes a frame), each shard is named at most 128 times and at least 128 - 1 times.
All inputs are finite; a program needn't handle non-finite values.
Results may differ from a plain program's by a relative error of at most 0.009.
Values may be sent and summed in bfloat16 or wider, within the bound.
No kernel may reach another device: no remote copies, remote signals or barrier semaphores. Data moves between devices by JAX's collectives and lax.ppermute only.
A program may use at most 128 MiB of HBM per device.

v0:
```python
import jax
import jax.numpy as jnp
from jax import lax
from jax.sharding import PartitionSpec as P

BLOCK = 256


commit_weight = 0.25


def carried_in(part, axis, combine, identity):
    place = lax.axis_index(axis)
    gathered = jax.tree.map(lambda a: lax.all_gather(a, axis), part)
    state = jax.tree.map(lambda a, e: jnp.zeros_like(a) + jnp.asarray(e, a.dtype), part, identity)

    def one(hop, state):
        return combine(
            state, jax.tree.map(lambda a: lax.dynamic_index_in_dim(a, hop, 0, False), gathered)
        )

    return lax.fori_loop(0, place, one, state)


def group_norm(v):
    return jnp.sqrt(jnp.sum(v * v, axis=-1, keepdims=True) + 1e-06)


def rotate_back(e, q, g):
    ne = group_norm(e)
    nq = group_norm(q)
    eh = e / ne
    qh = q / nq
    summed = eh + qh
    unit = summed / group_norm(summed)
    scale = nq / ne
    along = jnp.sum(unit * g, axis=-1, keepdims=True)
    toward = jnp.sum(qh * g, axis=-1, keepdims=True)
    return scale * (g - 2.0 * unit * along + 2.0 * eh * toward) + 2.0 * commit_weight * (e - q)


def link_states(earlier, later):
    return (earlier[0] * later[0], later[0][:, None, None] * earlier[1] + later[1])


def body(
    frames_in,
    gate_in,
    in_keys,
    out_keys,
    step_size,
    decay_rate,
    skip_gain,
    out_weight,
    codebook,
    code_index,
    upstream,
):
    highest = lax.Precision.HIGHEST
    chan_count = lax.axis_size("chan")
    frames_dev = frames_in.shape[0]
    heads = decay_rate.shape[0]
    head_dim = frames_in.shape[1] // heads
    nstate = in_keys.shape[1]
    blocks = frames_dev // BLOCK
    owned_rows = frames_dev // chan_count
    codes_dev = codebook.shape[0]
    code_dim = codebook.shape[1]
    groups = code_index.shape[1]
    xs = frames_in.astype(jnp.float32).reshape(blocks, BLOCK, heads, head_dim)
    dts = step_size.reshape(blocks, BLOCK, heads)
    bks = in_keys.astype(jnp.float32).reshape(blocks, BLOCK, nstate)
    cks = out_keys.astype(jnp.float32).reshape(blocks, BLOCK, nstate)
    lower = jnp.arange(BLOCK)[:, None] >= jnp.arange(BLOCK)[None, :]
    cums = jnp.cumsum(-dts * decay_rate[None, None, :], axis=1)
    trans = jnp.swapaxes(cums, 1, 2)
    spread = jnp.where(lower[None, None], trans[:, :, :, None] - trans[:, :, None, :], 0.0)
    masks = jnp.where(lower[None, None], jnp.exp(spread), 0.0)
    gram = jnp.einsum("bin,bjn->bij", cks, bks, precision=highest)
    scaled = dts[..., None] * xs
    intra = jnp.einsum("bhij,bjhp->bihp", masks * gram[:, None], scaled, precision=highest)
    weight = jnp.exp(cums[:, -1:, :] - cums)
    local_states = jnp.einsum("bjh,bjhp,bjn->bhpn", weight, scaled, bks, precision=highest)
    totals = cums[:, -1, :]
    block_decay = jnp.exp(totals)

    def chain(state, item):
        decay_now, fresh = item
        return (decay_now[:, None, None] * state + fresh, state)

    empty_state = jnp.zeros((heads, head_dim, nstate), jnp.float32)
    dev_state, starts = lax.scan(chain, empty_state, (block_decay, local_states))
    dev_decay = jnp.exp(jnp.sum(totals, axis=0))
    carried = carried_in(
        (dev_decay, dev_state),
        "seq",
        link_states,
        (jnp.ones_like(dev_decay), jnp.zeros_like(dev_state)),
    )
    incoming = carried[1]
    before = jnp.exp(jnp.cumsum(totals, axis=0) - totals)
    full_starts = starts + before[:, :, None, None] * incoming[None]
    inter = jnp.exp(cums)[..., None] * jnp.einsum(
        "bin,bhpn->bihp", cks, full_starts, precision=highest
    )
    mixed = intra + inter + skip_gain[None, None, :, None] * xs
    gated = (
        mixed.reshape(frames_dev, heads * head_dim) * jax.nn.silu(gate_in.astype(jnp.float32))
    ).astype(jnp.bfloat16)
    summed = lax.psum_scatter(
        jnp.dot(gated, out_weight, preferred_element_type=jnp.float32),
        "chan",
        scatter_dimension=0,
        tiled=True,
    )
    latent = summed.astype(jnp.bfloat16)
    e = latent.astype(jnp.float32).reshape(owned_rows, groups, code_dim)
    g = upstream.astype(jnp.float32).reshape(owned_rows, groups, code_dim)
    entries = owned_rows * groups
    slots = max(1, (entries + chan_count - 1) // chan_count)
    flat_index = code_index.reshape(entries)
    owner = flat_index // codes_dev
    within = flat_index - owner * codes_dev
    one_hot = (owner[:, None] == jnp.arange(chan_count, dtype=jnp.int32)[None, :]).astype(jnp.int32)
    rank = jnp.sum(jnp.cumsum(one_hot, axis=0) * one_hot, axis=1) - 1
    requests = jnp.full((chan_count, slots), codes_dev, jnp.int32).at[owner, rank].set(within)
    received = lax.all_to_all(requests, "chan", split_axis=0, concat_axis=0, tiled=True)
    picked = jnp.take(codebook, jnp.minimum(received, codes_dev - 1), axis=0)
    returned = lax.all_to_all(picked, "chan", split_axis=0, concat_axis=0, tiled=True)
    position = owner * slots + rank
    q = jnp.take(returned.reshape(chan_count * slots, code_dim), position, axis=0).astype(
        jnp.float32
    )
    q = q.reshape(owned_rows, groups, code_dim)
    latent_grad = rotate_back(e, q, g).reshape(owned_rows, groups * code_dim)
    diff = (q - e).astype(jnp.bfloat16).reshape(entries, code_dim)
    outgoing = jnp.zeros((chan_count, slots, code_dim), jnp.bfloat16).at[owner, rank].set(diff)
    incoming_diff = lax.all_to_all(outgoing, "chan", split_axis=0, concat_axis=0, tiled=True)
    diff_every, asked_every = (
        lax.all_gather(incoming_diff, "seq", axis=0, tiled=True),
        lax.all_gather(received, "seq", axis=0, tiled=True),
    )
    desired_quantity = asked_every.reshape(-1)
    values = diff_every.reshape(-1, code_dim).astype(jnp.float32)
    table = (
        jnp.zeros((codes_dev, code_dim), jnp.float32).at[desired_quantity].add(values, mode="drop")
    )
    codebook_grad = 2.0 * table
    return (latent, latent_grad, codebook_grad)


def solution(mesh):
    placed = (
        P("seq", "chan"),
        P("seq", "chan"),
        P("seq", None),
        P("seq", None),
        P("seq", "chan"),
        P("chan"),
        P("chan"),
        P("chan", None),
        P("chan", None),
        P(("seq", "chan"), None),
        P(("seq", "chan"), None),
    )
    return jax.shard_map(
        body,
        mesh=mesh,
        in_specs=placed,
        out_specs=(P(("seq", "chan"), None), P(("seq", "chan"), None), P("chan", None)),
        check_vma=False,
    )
```

profile of v0, /device:TPU:0, one launch (start us, length us, event | category | flops | bytes accessed | tf_op | source)
XLA Modules:
  0.0 541.8 jit_solution(2735800479278983932)
XLA Ops:
  9.2 4.5 reduce-window.14
  14.5 4.1 copy.84
  18.5 6.1 %copy.112 = f32[64,8,8,256]{3,2,1,0:T(8,128)} copy(f32[64,8,8,256]{3,1,2,0:T(8,128)} %bitcast.127) | data formatting | bytes 8388608
  24.6 4.8 broadcast_multiply_fusion.1
  29.4 4.4 fusion.21
  33.8 14.3 %while.26 = (s32[]{:T(128)}, f32[8,64,128]{2,1,0:T(8,128)S(1)}, f32[8,8,64,128]{3,2,1,0:T(8,128)}, f32[8,8]{1,0:T(8,128)S(1)}, f32[8,8,64,128]{3,2,1,0:T(8,128)}, /*index=5*/s32[]{:T(128)}, s32[]{:T(128)}) while((s32[]{:T(128)}, f32[8,64,128]{2,1,0:T(8,128)S(1)}, f32[8,8,64,128]{3,2,1,0:T(8,128)}, f32[8,8]{1,0:T(8,128)S(1)}, ...), condition=%wide.region_3.4_spmd.clone, body=%wide.region_2.3_spmd.clone.sunk | while | flops 262147 | bytes 1310924 | solution.py:92
  50.3 8.8 %all-reduce = f32[32]{0:T(128)S(1)} all-reduce(f32[32]{0:T(128)S(1)} %exponential_dynamic-update-slice_fusion), channel_id=2, replica_groups=mesh['seq'=4,'chan'=8] {'seq'}, use_global_device_ids=true, to_apply=%add | all-reduce | flops 32 | bytes 256
  59.2 4.0 copy.92
  63.8 22.5 %fusion.1 = f32[8,8,64,256]{3,2,1,0:T(8,128)} fusion(f32[8,256,256]{2,1,0:T(8,128)S(1)} %fusion.66, f32[8,8,256]{2,1,0:T(8,128)S(1)} %add_bitcast_fusion.1, pred[256,256]{1,0:T(8,128)(4,1)S(1)} %iota_compare_fusion, f32[8,256,8,64]{1,0,3,2:T(8,128)} %get-tuple-element.127), kind=kOutput, calls=%fused_computation.11 | convolution fusion | flops 3238002688 | bytes 10616832 | tf_op jit(solution)/shard_map/bhij,bjhp->bihp/dot_general | solution.py:81
  87.0 7.3 %fusion.20 = f32[8,256,8,64]{1,3,2,0:T(8,128)S(1)} fusion(f32[8,8,64,256]{3,2,1,0:T(8,128)} %fusion.1, f32[8,256,8,64]{1,0,3,2:T(8,128)} %bitcast.125, bf16[8,256,128,1]{2,1,3,0:T(8,128)(2,1)S(1)} %bitcast.146, f32[8]{0:T(128)S(1)} %copy-done.16, f32[8,8,64,128]{3,2,1,0:T(8,128)} %get-tuple-element.75, f32[8,256,8]{1,2,0:T(8,128)S(1)} %get-tuple-element.124, ...), kind=kOutput, calls=%fused_computation.34 | convolution fusion | flops 1615855616 | bytes 15532320 | tf_op jit(solution)/shard_map/bin,bhpn->bihp/dot_general | solution.py:103
  98.7 8.7 %fusion.33 = f32[2048,2048]{1,0:T(8,128)} fusion(bf16[512,2048]{1,0:T(8,128)(2,1)S(1)} %copy-done, f32[2048,512]{0,1:T(8,128)S(1)} %bitcast.141, bf16[2048,512]{0,1:T(8,128)(2,1)S(1)} %copy-done.12), kind=kOutput, calls=%fused_computation.52 | convolution fusion | flops 4302307328 | bytes 25165824 | tf_op jit(solution)/shard_map/dot_general | solution.py:111
  111.7 4.3 scatter_custom_fusion.1
  116.0 12.8 %all_to_all.22 = s32[8,1,128]{2,1,0:T(1,128)S(1)} all-to-all(s32[8,1,128]{2,1,0:T(1,128)S(1)} %bitcast.159), channel_id=1, replica_groups=mesh['seq'=4,'chan'=8] {'chan'}, dimensions={0} | all-to-all | bytes 8192 | tf_op jit(solution)/shard_map/all_to_all | solution.py:127
  128.8 8.5 %gather_fusion = bf16[1024,512]{1,0:T(8,128)(2,1)S(1)} fusion(bf16[8192,512]{1,0:T(8,128)(2,1)} %param.23, s32[1024]{0:T(1024)S(1)} %fusion.58), kind=kCustom, calls=%fused_computation | custom fusion | bytes 2101248 | tf_op jit(solution)/shard_map/jit(_take)/gather | solution.py:128
  138.5 3.6 all-to-all-start.1
  142.2 51.7 %all-to-all-done.1 = bf16[8,128,512]{2,1,0:T(8,128)(2,1)S(1)} async-done(((bf16[8,128,512]{2,1,0:T(8,128)(2,1)}), bf16[8,128,512]{2,1,0:T(8,128)(2,1)S(1)}, u32[]{:S(2)}, u32[]{:S(2)}) %all-to-all-start.1) | async-done | bytes 1048608 | tf_op jit(solution)/shard_map/all_to_all | solution.py:129
  193.9 4.0 gather_fusion.1
  197.8 216.7 %reduce-scatter.2.cloned.1.call-done = f32[256,2048]{1,0:T(8,128)} async-done(((f32[2048,2048]{1,0:T(8,128)}), f32[256,2048]{1,0:T(8,128)}) %reduce-scatter.2.cloned.1.call-update) | async-done | bytes 2097168 | tf_op jit(solution)/shard_map/reduce_scatter | solution.py:110
  417.9 7.3 %scatter_custom_fusion.2 = bf16[1024,512]{1,0:T(8,128)(2,1)} fusion(s32[1024]{0:T(1024)S(1)} %broadcast_select_fusion.1, f32[1024,512]{1,0:T(8,128)} %reshape.416, bf16[1024,512]{1,0:T(8,128)(2,1)S(1)} %gather_fusion.1, pred[1024]{0:T(1024)(128)(4,1)S(1)} %compare_and_fusion.1, bf16[]{:T(256)} %constant.117.clone.1, bf16[]{:T(256)} %constant.113.clone.1), kind=kCustom, calls=%fused_computation.65 | custom fusion | flops 2097152 | bytes 4195332
  425.2 30.1 %all_to_all.23 = bf16[8,128,512]{2,1,0:T(8,128)(2,1)} all-to-all(bf16[8,128,512]{2,1,0:T(8,128)(2,1)} %bitcast.142), channel_id=1, replica_groups=mesh['seq'=4,'chan'=8] {'chan'}, dimensions={0} | all-to-all | bytes 2097152 | tf_op jit(solution)/shard_map/all_to_all | solution.py:138
  460.2 5.2 all-gather.2
  487.1 3.3 fusion.31
  490.4 32.7 %scatter_custom_fusion = f32[8192,512]{1,0:T(8,128)} fusion(s32[4096]{0:T(1024)S(1)} %bitcast.157, bf16[4096,512]{1,0:T(8,128)(2,1)} %bitcast.143, f32[]{:T(128)} %constant.70.clone.1), kind=kCustom, calls=%fused_computation.17 | custom fusion | flops 4194304 | bytes 20971524 | tf_op jit(solution)/shard_map/scatter-add | solution.py:146
  523.1 12.0 %broadcast_multiply_fusion = f32[8192,512]{1,0:T(8,128)} fusion(f32[8192,512]{1,0:T(8,128)} %scatter_custom_fusion), kind=kLoop, calls=%fused_computation.19 | loop fusion | flops 4194304 | bytes 33554432 | tf_op jit(solution)/shard_map/mul | solution.py:148
  (156 shorter events, 59.2 us)
Async XLA Ops:
  7.2 91.5 %copy-start = (bf16[512,2048]{1,0:T(8,128)(2,1)S(1)}, bf16[512,2048]{1,0:T(8,128)(2,1)}, u32[]{:S(2)}) copy-start(bf16[512,2048]{1,0:T(8,128)(2,1)} %param.22) | copy-start | bytes 6291460
  7.2 79.1 %all-gather.8.cloned.1.call-start = ((), (), s32[]{:S(2)}) async-start(), calls=%async_computation.6 | async-start | bytes 1310720 | tf_op jit(solution)/shard_map/all_gather | solution.py:14
  24.6 4.8 copy-start.14
  33.8 15.2 %copy-start.19 = (u32[32]{0:T(128)S(1)}, u32[32]{0:T(128)}, u32[]{:S(2)}) copy-start(u32[32]{0:T(128)} %constant.135) | copy-start | bytes 388
  48.2 0.7 copy-start.2
  48.9 365.6 %reduce-scatter.2.cloned.1.call-start = ((), (), s32[]{:S(2)}) async-start(), calls=%async_computation.4 | async-start | bytes 18874368 | tf_op jit(solution)/shard_map/reduce_scatter | solution.py:110
  59.2 4.1 copy-start.13
  86.3 0.7 copy-start.16
  96.7 2.0 copy-start.12
  107.4 0.7 copy-start.15
  107.4 4.1 copy-start.18
  107.4 4.2 copy-start.17
  138.5 55.3 %all-to-all-start.1 = ((bf16[8,128,512]{2,1,0:T(8,128)(2,1)}), bf16[8,128,512]{2,1,0:T(8,128)(2,1)S(1)}, u32[]{:S(2)}, u32[]{:S(2)}) async-start(bf16[8,128,512]{2,1,0:T(8,128)(2,1)} %broadcast_select_fusion), calls=%async_computation.2 | async-start | bytes 2097152 | tf_op jit(solution)/shard_map/all_to_all | solution.py:129
  142.1 348.3 %all-gather.6.cloned.1.call-start = ((), (), s32[]{:S(2)}) async-start(), calls=%async_computation.5 | async-start | bytes 5242880 | tf_op jit(solution)/shard_map/all_gather | solution.py:140
  416.3 55.1 %copy-start.3 = (bf16[256,2048]{1,0:T(8,128)(2,1)}, bf16[256,2048]{1,0:T(8,128)(2,1)S(1)}, u32[]{:S(2)}) copy-start(bf16[256,2048]{1,0:T(8,128)(2,1)S(1)} %convert_element_type.48) | copy-start | bytes 3145732
  425.2 30.8 %copy-start.8 = (bf16[256,2048]{1,0:T(8,128)(2,1)S(1)}, bf16[256,2048]{1,0:T(8,128)(2,1)}, u32[]{:S(2)}) copy-start(bf16[256,2048]{1,0:T(8,128)(2,1)} %param.25) | copy-start | bytes 3145732
  473.9 1.3 copy-start.4
  475.2 2.1 copy-start.7
  483.2 2.2 copy-start.11
  484.1 1.3 copy-start.9
  484.1 1.6 copy-start.10
  484.5 2.0 copy-start.5
  484.5 2.6 copy-start.6
  523.1 12.0 %copy-start.1 = (bf16[512,2048]{1,0:T(8,128)(2,1)S(1)}, bf16[512,2048]{1,0:T(8,128)(2,1)}, u32[]{:S(2)}) copy-start(bf16[512,2048]{1,0:T(8,128)(2,1)} %param.22) | copy-start | bytes 6291460
Sparse Core Ops, SparseCore 0:
  49.0 19.4 all-gather.7
  107.5 306.9 reduce-scatter.1
  455.5 33.4 all-gather.5
where the time goes:
time: 548 us; the launch traced here: 542 us
  waiting for transfers between devices  268 us (49%)
  other arithmetic  92.4 us (17%)
  local copies, waits for them, and re-layouts  61.6 us (11%)
  blocking collectives  56.9 us (10%)
  matrix products  43.3 us (8%)
  between operations  15.2 us (3%)
    reduce_scatter x1, waiting for transfers between devices, body(): lax.psum_scatter(jnp.dot(gated, out_weight, preferred_element_type=jnp.fl...  217 us
    all_to_all x1, waiting for transfers between devices, body(): lax.all_to_all(picked, 'chan', split_axis=0, concat_axis=0, tiled=True)  51.7 us
    scatter-add x1, other arithmetic, body(): jnp.zeros((codes_dev, code_dim), jnp.float32).at[desired_quantity]  32.7 us
    all_to_all x1, blocking collectives, body(): lax.all_to_all(outgoing, 'chan', split_axis=0, concat_axis=0, tiled=True)  30.1 us
    unnamed x55, local copies, waits for them, and re-layouts  28.9 us
    dot_general x1, matrix products, body(): jnp.einsum('bhij,bjhp->bihp', masks * gram[:, None], scaled, precision=hi...  22.5 us
    all_to_all x1, blocking collectives, body(): lax.all_to_all(requests, 'chan', split_axis=0, concat_axis=0, tiled=True)  12.8 us
    mul x1, other arithmetic, body(): codebook_grad = 2.0 * table  12 us
  transfers between devices with their start and end apart: 4, of which 2 were waited for; matrix products, arithmetic and copies ran while one was open for 14% of the time, Pallas kernels for 0%

commit v1 on v0

v1 whole, which is shorter than its diff:
```python
import functools

import jax
import jax.numpy as jnp
from jax import lax
from jax.experimental import pallas as pl
from jax.experimental.pallas import tpu as pltpu
from jax.sharding import PartitionSpec as P

COMMIT = 0.25
CODE_BLOCK = 256
F32 = jnp.float32
BF16 = jnp.bfloat16
HIGHEST = lax.Precision.HIGHEST


def flip(x, axis, bit):
    n = lax.axis_size(axis)
    return lax.ppermute(x, axis, [(i, i ^ bit) for i in range(n)])


def dot_nt(a, b):
    return lax.dot_general(a, b, (((1,), (1,)), ((), ())), preferred_element_type=F32)


def dot_tn(a, b):
    return lax.dot_general(a, b, (((0,), (0,)), ((), ())), preferred_element_type=F32)


def per_head(values, heads, width):
    rows = values.shape[0]
    return jnp.concatenate(
        [jnp.broadcast_to(values[:, h : h + 1], (rows, width)) for h in range(heads)], axis=1
    )


def states_kernel(
    x_ref, b_ref, dt_ref, rate_ref,
    starts_ref, cums_ref, cums_t_ref, before_ref, final_ref, total_ref,
    state, seen,
):
    step = pl.program_id(0)
    rows, width = x_ref.shape
    heads = dt_ref.shape[1]
    head_dim = width // heads

    @pl.when(step == 0)
    def _():
        state[...] = jnp.zeros_like(state)
        seen[...] = jnp.zeros_like(seen)

    dt = dt_ref[...]
    logs = -dt * rate_ref[...]
    lower = (
        lax.broadcasted_iota(jnp.int32, (rows, rows), 0)
        >= lax.broadcasted_iota(jnp.int32, (rows, rows), 1)
    ).astype(F32)
    cums = jnp.dot(lower, logs, precision=HIGHEST, preferred_element_type=F32)
    cums_ref[...] = cums
    cums_t_ref[0] = cums.T
    before_ref[0] = seen[...]
    total = cums[rows - 1 : rows, :]
    weight = dt * jnp.exp(total - cums)
    xw = (x_ref[...].astype(F32) * per_head(weight, heads, head_dim)).astype(BF16)
    fresh = dot_tn(xw, b_ref[...])
    starts_ref[0] = state[...]
    keep = jnp.exp(total)
    for h in range(heads):
        rs = slice(h * head_dim, (h + 1) * head_dim)
        state[rs, :] = state[rs, :] * keep[:, h : h + 1] + fresh[rs, :]
    seen[...] = seen[...] + total

    @pl.when(step == pl.num_programs(0) - 1)
    def _():
        final_ref[...] = state[...]
        total_ref[...] = seen[...]


def block_states(frames_in, in_keys, step_size, rate, rows):
    frames, width = frames_in.shape
    nstate = in_keys.shape[1]
    heads = step_size.shape[1]
    nb = frames // rows
    return pl.pallas_call(
        states_kernel,
        grid=(nb,),
        in_specs=[
            pl.BlockSpec((rows, width), lambda i: (i, 0)),
            pl.BlockSpec((rows, nstate), lambda i: (i, 0)),
            pl.BlockSpec((rows, heads), lambda i: (i, 0)),
            pl.BlockSpec((1, heads), lambda i: (0, 0)),
        ],
        out_specs=[
            pl.BlockSpec((1, width, nstate), lambda i: (i, 0, 0)),
            pl.BlockSpec((rows, heads), lambda i: (i, 0)),
            pl.BlockSpec((1, heads, rows), lambda i: (i, 0, 0)),
            pl.BlockSpec((1, 1, heads), lambda i: (i, 0, 0)),
            pl.BlockSpec((width, nstate), lambda i: (0, 0)),
            pl.BlockSpec((1, heads), lambda i: (0, 0)),
        ],
        out_shape=[
            jax.ShapeDtypeStruct((nb, width, nstate), F32),
            jax.ShapeDtypeStruct((frames, heads), F32),
            jax.ShapeDtypeStruct((nb, heads, rows), F32),
            jax.ShapeDtypeStruct((nb, 1, heads), F32),
            jax.ShapeDtypeStruct((width, nstate), F32),
            jax.ShapeDtypeStruct((1, heads), F32),
        ],
        scratch_shapes=[pltpu.VMEM((width, nstate), F32), pltpu.VMEM((1, heads), F32)],
        name="block_states",
    )(frames_in, in_keys, step_size, rate)


def intra_kernel(x_ref, b_ref, c_ref, dt_ref, cums_ref, cums_t_ref, skip_ref, out_ref):
    rows, width = x_ref.shape
    heads = dt_ref.shape[1]
    head_dim = width // heads
    tile = min(rows, 128)
    cums = cums_ref[...]
    cums_t = cums_t_ref[0]
    x = x_ref[...].astype(F32)
    xdt = (x * per_head(dt_ref[...], heads, head_dim)).astype(BF16)
    skipped = x * per_head(skip_ref[...], heads, head_dim)
    for t in range(rows // tile):
        rs = slice(t * tile, (t + 1) * tile)
        n = (t + 1) * tile
        gram = dot_nt(c_ref[rs, :], b_ref[0:n, :])
        allowed = (
            lax.broadcasted_iota(jnp.int32, (tile, n), 0) + t * tile
            >= lax.broadcasted_iota(jnp.int32, (tile, n), 1)
        )
        parts = []
        for h in range(heads):
            spread = cums[rs, h : h + 1] - cums_t[h : h + 1, 0:n]
            mask = jnp.exp(jnp.where(allowed, spread, -1e30))
            parts.append(
                jnp.dot(
                    (mask * gram).astype(BF16),
                    xdt[0:n, h * head_dim : (h + 1) * head_dim],
                    preferred_element_type=F32,
                )
            )
        out_ref[rs, :] = jnp.concatenate(parts, axis=1) + skipped[rs, :]


def intra_block(frames_in, in_keys, out_keys, step_size, cums, cums_t, skip, rows):
    frames, width = frames_in.shape
    nstate = in_keys.shape[1]
    heads = step_size.shape[1]
    return pl.pallas_call(
        intra_kernel,
        grid=(frames // rows,),
        in_specs=[
            pl.BlockSpec((rows, width), lambda i: (i, 0)),
            pl.BlockSpec((rows, nstate), lambda i: (i, 0)),
            pl.BlockSpec((rows, nstate), lambda i: (i, 0)),
            pl.BlockSpec((rows, heads), lambda i: (i, 0)),
            pl.BlockSpec((rows, heads), lambda i: (i, 0)),
            pl.BlockSpec((1, heads, rows), lambda i: (i, 0, 0)),
            pl.BlockSpec((1, heads), lambda i: (0, 0)),
        ],
        out_specs=pl.BlockSpec((rows, width), lambda i: (i, 0)),
        out_shape=jax.ShapeDtypeStruct((frames, width), F32),
        name="intra_block",
    )(frames_in, in_keys, out_keys, step_size, cums, cums_t, skip)


def gate_kernel(
    order_ref, mixed_ref, gate_ref, c_ref, cums_ref, starts_ref, before_ref, incoming_ref, out_ref
):
    rows, width = mixed_ref.shape
    heads = cums_ref.shape[1]
    head_dim = width // heads
    carry = jnp.exp(before_ref[0])
    parts = []
    for h in range(heads):
        rs = slice(h * head_dim, (h + 1) * head_dim)
        parts.append(starts_ref[0, rs, :] + incoming_ref[rs, :] * carry[:, h : h + 1])
    start = jnp.concatenate(parts, axis=0).astype(BF16)
    inter = dot_nt(c_ref[...], start)
    mixed = mixed_ref[...] + inter * per_head(jnp.exp(cums_ref[...]), heads, head_dim)
    gate = gate_ref[...].astype(F32)
    gated = (mixed * (gate / (1.0 + jnp.exp(-gate)))).astype(BF16)
    second = order_ref[order_ref.shape[0] - 1] == 1
    half = width // 2
    lo = gated[:, :half]
    hi = gated[:, half:]
    out_ref[0, :, :half] = jnp.where(second, hi, lo)
    out_ref[0, :, half:] = jnp.where(second, lo, hi)


def gated_blocks(order, count, mixed, gate_in, out_keys, cums, starts, before, incoming, rows):
    width = mixed.shape[1]
    nstate = out_keys.shape[1]
    heads = cums.shape[1]
    return pl.pallas_call(
        gate_kernel,
        grid_spec=pltpu.PrefetchScalarGridSpec(
            num_scalar_prefetch=1,
            grid=(count,),
            in_specs=[
                pl.BlockSpec((rows, width), lambda i, o: (o[i], 0)),
                pl.BlockSpec((rows, width), lambda i, o: (o[i], 0)),
                pl.BlockSpec((rows, nstate), lambda i, o: (o[i], 0)),
                pl.BlockSpec((rows, heads), lambda i, o: (o[i], 0)),
                pl.BlockSpec((1, width, nstate), lambda i, o: (o[i], 0, 0)),
                pl.BlockSpec((1, 1, heads), lambda i, o: (o[i], 0, 0)),
                pl.BlockSpec((width, nstate), lambda i, o: (0, 0)),
            ],
            out_specs=pl.BlockSpec((1, rows, width), lambda i, o: (i, 0, 0)),
        ),
        out_shape=jax.ShapeDtypeStruct((count, rows, width), BF16),
        name="gated_blocks",
    )(order, mixed, gate_in, out_keys, cums, starts, before, incoming)


def project_kernel(*refs, count, added):
    gs = refs[:count]
    firsts = refs[count : 2 * count]
    seconds = refs[2 * count : 3 * count]
    out_ref = refs[-1]
    half = firsts[0].shape[0]
    acc = None
    for g, a, b in zip(gs, firsts, seconds):
        part = jnp.dot(g[:, :half], a[...], preferred_element_type=F32)
        part = part + jnp.dot(g[:, half:], b[...], preferred_element_type=F32)
        acc = part if acc is None else acc + part
    if added:
        acc = acc + refs[3 * count][...].astype(F32)
    out_ref[...] = acc.astype(BF16)


def project(gs, firsts, seconds, add=None):
    count = len(gs)
    rows, width = gs[0].shape
    half, cols = firsts[0].shape
    tile = min(cols, 512)
    in_specs = [pl.BlockSpec((rows, width), lambda j: (0, 0))] * count
    in_specs += [pl.BlockSpec((half, tile), lambda j: (0, j))] * (2 * count)
    args = list(gs) + list(firsts) + list(seconds)
    if add is not None:
        in_specs.append(pl.BlockSpec((rows, tile), lambda j: (0, j)))
        args.append(add)
    return pl.pallas_call(
        functools.partial(project_kernel, count=count, added=add is not None),
        grid=(cols // tile,),
        in_specs=in_specs,
        out_specs=pl.BlockSpec((rows, tile), lambda j: (0, j)),
        out_shape=jax.ShapeDtypeStruct((rows, cols), BF16),
        name="project",
    )(*args)


def diff_kernel(pos_ref, latent_ref, q_ref, out_ref):
    _, slots, dim = out_ref.shape
    groups, rows = pos_ref.shape
    base = pl.program_id(0) * slots
    slot = lax.broadcasted_iota(jnp.int32, (slots, rows), 0) + base
    acc = None
    for g in range(groups):
        pick = jnp.where(slot == pos_ref[g : g + 1, :], 1.0, 0.0).astype(BF16)
        part = jnp.dot(
            pick, latent_ref[:, g * dim : (g + 1) * dim], preferred_element_type=F32
        )
        acc = part if acc is None else acc + part
    out_ref[0] = (q_ref[0].astype(F32) - acc).astype(BF16)


def diffs(pos, latent, q):
    count, slots, dim = q.shape
    return pl.pallas_call(
        diff_kernel,
        grid=(count,),
        in_specs=[
            pl.BlockSpec(pos.shape, lambda i: (0, 0)),
            pl.BlockSpec(latent.shape, lambda i: (0, 0)),
            pl.BlockSpec((1, slots, dim), lambda i: (i, 0, 0)),
        ],
        out_specs=pl.BlockSpec((1, slots, dim), lambda i: (i, 0, 0)),
        out_shape=jax.ShapeDtypeStruct(q.shape, BF16),
        name="diffs",
    )(pos, latent, q)


def norm_of(v):
    return jnp.sqrt(jnp.sum(v * v, axis=-1, keepdims=True) + 1e-06)


def grad_kernel(pos_ref, latent_ref, up_ref, q_ref, out_ref):
    entries, dim = q_ref.shape
    rows = latent_ref.shape[0]
    groups = latent_ref.shape[1] // dim
    slot = lax.broadcasted_iota(jnp.int32, (rows, entries), 1)
    for n in range(groups):
        cols = slice(n * dim, (n + 1) * dim)
        pick = jnp.where(slot == pos_ref[:, n : n + 1], 1.0, 0.0).astype(BF16)
        q = jnp.dot(pick, q_ref[...], preferred_element_type=F32)
        e = latent_ref[:, cols].astype(F32)
        g = up_ref[:, cols].astype(F32)
        ne = norm_of(e)
        nq = norm_of(q)
        eh = e / ne
        qh = q / nq
        summed = eh + qh
        unit = summed / norm_of(summed)
        along = jnp.sum(unit * g, axis=-1, keepdims=True)
        toward = jnp.sum(qh * g, axis=-1, keepdims=True)
        out_ref[:, cols] = (nq / ne) * (g - 2.0 * unit * along + 2.0 * eh * toward) + (
            2.0 * COMMIT
        ) * (e - q)


def latent_grads(pos_cols, latent, upstream, q):
    rows, width = latent.shape
    groups = pos_cols.shape[1]
    tile = min(rows, 64)
    return pl.pallas_call(
        grad_kernel,
        grid=(rows // tile,),
        in_specs=[
            pl.BlockSpec((tile, groups), lambda i: (i, 0)),
            pl.BlockSpec((tile, width), lambda i: (i, 0)),
            pl.BlockSpec((tile, width), lambda i: (i, 0)),
            pl.BlockSpec(q.shape, lambda i: (0, 0)),
        ],
        out_specs=pl.BlockSpec((tile, width), lambda i: (i, 0)),
        out_shape=jax.ShapeDtypeStruct((rows, width), F32),
        name="latent_grads",
    )(pos_cols, latent, upstream, q)


def order_kernel(*refs):
    place_ref = refs[0]
    chunks = refs[1:-1]
    out_ref = refs[-1]
    tile = out_ref.shape[0]
    slots = chunks[0].shape[0]
    slot = lax.broadcasted_iota(jnp.int32, (tile, slots), 0) + pl.program_id(0) * tile
    acc = None
    for n, chunk in enumerate(chunks):
        pick = jnp.where(slot == place_ref[:, n * slots : (n + 1) * slots], 1.0, 0.0).astype(BF16)
        part = jnp.dot(pick, chunk[...], preferred_element_type=F32)
        acc = part if acc is None else acc + part
    out_ref[...] = acc.astype(BF16)


def ordered(place, chunks):
    slots, dim = chunks[0].shape
    total = slots * len(chunks)
    tile = min(total, 256)
    return pl.pallas_call(
        order_kernel,
        grid=(total // tile,),
        in_specs=[pl.BlockSpec((1, total), lambda i: (0, 0))]
        + [pl.BlockSpec((slots, dim), lambda i: (0, 0))] * len(chunks),
        out_specs=pl.BlockSpec((tile, dim), lambda i: (i, 0)),
        out_shape=jax.ShapeDtypeStruct((total, dim), BF16),
        name="ordered",
    )(place, *chunks)


def table_kernel(bounds_ref, codes_ref, *refs, window):
    runs = refs[:-1]
    out_ref = refs[-1]
    codes, dim = out_ref.shape
    length = runs[0].shape[0]
    block = pl.program_id(0)
    base = block * codes
    lane = lax.broadcasted_iota(jnp.int32, (window, 128), 1) + base
    row = lax.broadcasted_iota(jnp.int32, (window, 128), 0)

    def gathered(turn):
        picks = []
        rows = []
        for r, run in enumerate(runs):
            first = (bounds_ref[r, block] // 16) * 16 + turn * window
            at = pl.multiple_of(jnp.minimum(first, length - window), 16)
            mine = codes_ref[r, pl.ds(at, window), :]
            mine = jnp.where(row + at >= first, mine, -1)
            picks.append(
                jnp.concatenate(
                    [
                        jnp.where(mine == lane + n * 128, 1.0, 0.0).astype(BF16)
                        for n in range(codes // 128)
                    ],
                    axis=1,
                )
            )
            rows.append(run[pl.ds(at, window), :])
        pick = jnp.concatenate(picks, axis=0)
        values = jnp.concatenate(rows, axis=0)
        return 2.0 * dot_tn(pick, values)

    out_ref[...] = gathered(0)
    turns = 0
    for r in range(len(runs)):
        lo = (bounds_ref[r, block] // 16) * 16
        hi = bounds_ref[r, block + 1]
        turns = jnp.maximum(turns, (hi - lo + window - 1) // window)

    def more(turn, carry):
        out_ref[...] += gathered(turn)
        return carry

    lax.fori_loop(1, turns, more, 0)


def table(bounds, codes, runs, codes_dev):
    length, dim = runs[0].shape
    block = min(CODE_BLOCK, codes_dev)
    blocks = codes_dev // block
    window = 16
    while window < length and window < 2 * length // blocks:
        window *= 2
    return pl.pallas_call(
        functools.partial(table_kernel, window=window),
        grid_spec=pltpu.PrefetchScalarGridSpec(
            num_scalar_prefetch=1,
            grid=(blocks,),
            in_specs=[pl.BlockSpec(codes.shape, lambda i, b: (0, 0, 0))]
            + [pl.BlockSpec((length, dim), lambda i, b: (0, 0))] * len(runs),
            out_specs=pl.BlockSpec((block, dim), lambda i, b: (i, 0)),
        ),
        out_shape=jax.ShapeDtypeStruct((codes_dev, dim), F32),
        name="table",
    )(bounds, codes, *runs)


def body(
    frames_in,
    gate_in,
    in_keys,
    out_keys,
    step_size,
    decay_rate,
    skip_gain,
    out_weight,
    codebook,
    code_index,
    upstream,
):
    chans = lax.axis_size("chan")
    seqs = lax.axis_size("seq")
    chan = lax.axis_index("chan")
    seq = lax.axis_index("seq")
    half = chans // 2
    core = seq % 2
    frames, width = frames_in.shape
    rows = frames // chans
    codes_dev, dim = codebook.shape
    groups = code_index.shape[1]
    heads = decay_rate.shape[0]
    nstate = in_keys.shape[1]

    wrows = out_weight.shape[0] // 2
    mine = lax.dynamic_slice_in_dim(out_weight, core * wrows, wrows, 0)
    other = lax.dynamic_slice_in_dim(out_weight, (1 - core) * wrows, wrows, 0)
    firsts = [mine] + [flip(mine, "chan", k) for k in range(1, half)]
    seconds = [other] + [flip(firsts[k], "seq", 1) for k in range(1, half)]

    rate = decay_rate.reshape(1, heads)
    starts, cums, cums_t, before, final, total = block_states(
        frames_in, in_keys, step_size, rate, rows
    )
    mixed = intra_block(
        frames_in, in_keys, out_keys, step_size, cums, cums_t, skip_gain.reshape(1, heads), rows
    )
    head_dim = width // heads
    held = final
    held_log = total
    incoming = jnp.zeros_like(final)
    lower_log = jnp.zeros_like(total)

    def rows_of(logs):
        return jnp.broadcast_to(
            jnp.exp(logs).reshape(heads, 1, 1), (heads, head_dim, 1)
        ).reshape(width, 1)

    bit = 1
    while bit < seqs:
        got = flip(held.astype(BF16), "seq", bit).astype(F32)
        got_log = flip(held_log, "seq", bit)
        after = (seq & bit) != 0
        incoming = jnp.where(after, incoming + rows_of(lower_log) * got, incoming)
        lower_log = jnp.where(after, lower_log + got_log, lower_log)
        held = jnp.where(
            after, rows_of(held_log) * got + held, rows_of(got_log) * held + got
        )
        held_log = held_log + got_log
        bit *= 2

    top = chan // half
    low = chan % half
    turn = jnp.arange(half, dtype=jnp.int32)
    near = top * half + (low ^ turn)
    far = (1 - top) * half + (low ^ turn)
    tail = core.astype(jnp.int32)[None]

    def gated_for(which):
        out = gated_blocks(
            jnp.concatenate([which.astype(jnp.int32), tail]),
            half, mixed, gate_in, out_keys, cums, starts, before, incoming, rows,
        )
        return [out[0]] + [flip(out[k], "chan", k) for k in range(1, half)]

    across = flip(project(gated_for(far), firsts, seconds), "chan", half)
    near_blocks = gated_for(near)

    entries = rows * groups
    slots = max(1, (entries + chans - 1) // chans)
    index_t = code_index.T
    flat = index_t.reshape(entries)
    owner = flat // codes_dev
    within = flat - owner * codes_dev
    hot = (owner[:, None] == jnp.arange(chans, dtype=jnp.int32)[None, :]).astype(BF16)
    entry = jnp.arange(entries, dtype=jnp.int32)
    earlier = (entry[:, None] > entry[None, :]).astype(BF16)
    counts = jnp.dot(earlier, hot, preferred_element_type=F32)
    rank = jnp.sum(counts * hot.astype(F32), axis=1).astype(jnp.int32)
    slot_of = owner * slots + rank
    place = (owner ^ chan) * slots + rank
    pos = place.reshape(groups, rows)
    wanted = jnp.sum(
        jnp.where(slot_of[None, :] == entry[:, None], within[None, :] + 1, 0), axis=1
    )
    wanted = jnp.where(wanted == 0, codes_dev, wanted - 1).reshape(chans, slots)
    received = lax.all_to_all(wanted, "chan", split_axis=0, concat_axis=0, tiled=True)
    lane = jnp.arange(chans, dtype=jnp.int32)
    turned = (lane[:, None] ^ chan) == lane[None, :]
    asked = jnp.sum(jnp.where(turned[:, :, None], received[None], 0), axis=1)
    picked = jnp.take(codebook, jnp.minimum(asked, codes_dev - 1), axis=0)
    q = jnp.stack([picked[0]] + [flip(picked[k], "chan", k) for k in range(1, chans)])

    asked_runs = asked.reshape(1, entries)
    bit = seqs // 2
    while bit > 1:
        asked_runs = jnp.concatenate([asked_runs, flip(asked_runs, "seq", bit)])
        bit //= 2
    keys = asked_runs * entries + entry[None, :]
    ranks = jnp.sum((keys[:, None, :] < keys[:, :, None]).astype(jnp.int32), axis=2)
    run_codes = jnp.sum(
        jnp.where(ranks[:, None, :] == entry[None, :, None], asked_runs[:, None, :], 0), axis=2
    )
    if seqs > 1:
        run_codes = jnp.concatenate([run_codes, flip(run_codes, "seq", 1)])
    block = min(CODE_BLOCK, codes_dev)
    edges = jnp.arange(codes_dev // block + 1, dtype=jnp.int32) * block
    bounds = jnp.sum((run_codes[:, None, :] < edges[None, :, None]).astype(jnp.int32), axis=2)
    codes_wide = jnp.broadcast_to(run_codes[:, :, None], run_codes.shape + (128,))

    latent = project(near_blocks, firsts, seconds, across)

    diff = diffs(pos, latent, q)
    chunks = []
    for k in range(chans):
        got = [diff[k] if k == 0 else flip(diff[k], "chan", k)]
        bit = seqs // 2
        while bit > 1:
            got = got + [flip(a, "seq", bit) for a in got]
            bit //= 2
        chunks.append(got)
    latent_grad = latent_grads(pos.T, latent, upstream, q.reshape(entries, dim))
    runs = [
        ordered(ranks[r : r + 1], [chunks[k][r] for k in range(chans)])
        for r in range(max(1, seqs // 2))
    ]
    if seqs > 1:
        runs = runs + [flip(a, "seq", 1) for a in runs]
    codebook_grad = table(bounds, codes_wide, runs, codes_dev)
    return (latent, latent_grad, codebook_grad)


def solution(mesh):
    placed = (
        P("seq", "chan"),
        P("seq", "chan"),
        P("seq", None),
        P("seq", None),
        P("seq", "chan"),
        P("chan"),
        P("chan"),
        P("chan", None),
        P("chan", None),
        P(("seq", "chan"), None),
        P(("seq", "chan"), None),
    )
    return jax.shard_map(
        body,
        mesh=mesh,
        in_specs=placed,
        out_specs=(P(("seq", "chan"), None), P(("seq", "chan"), None), P("chan", None)),
        check_vma=False,
    )
```

time: 548 us -> 274 us (0.50)
  waiting for transfers between devices: 268 us -> 65.2 us
  Pallas kernels: 0 us -> 94.3 us
  other arithmetic: 92.4 us -> 10.2 us
  starting transfers between devices: 3.68 us -> 65.8 us
  blocking collectives: 56.9 us -> 0 us
  matrix products: 43.3 us -> 0.48 us
  local copies, waits for them, and re-layouts: 61.6 us -> 35.4 us
  between operations: 15.2 us -> 1.17 us
    reduce_scatter x1 -> x0, waiting for transfers between devices: 217 us -> none  [body(): lax.psum_scatter(jnp.dot(gated, out_weight, preferred_element_type=jnp.fl...]
    pallas_call x0 -> x11, Pallas kernels: none -> 94.3 us  [the longest x1 21.2 us: table(): pl.pallas_call(functools.partial(table_kernel, window=window), grid_spec=...]
    ppermute x0 -> x42, starting transfers between devices: none -> 59.6 us  [flip(): return lax.ppermute(x, axis, [(i, i ^ bit) for i in range(n)])]
    ppermute x0 -> x42, waiting for transfers between devices: none -> 56 us  [flip(): return lax.ppermute(x, axis, [(i, i ^ bit) for i in range(n)])]
    all_to_all x2 -> x0, blocking collectives: 42.9 us -> none  [the longest x1 30.1 us: body(): lax.all_to_all(outgoing, 'chan', split_axis=0, concat_axis=0, tiled=True)]
    dot_general x5 -> x1, matrix products: 43.3 us -> 0.48 us  [body(): counts = jnp.dot(earlier, hot, preferred_element_type=F32)]
    all_to_all x1, waiting for transfers between devices: 51.7 us -> 9.13 us  [body(): lax.all_to_all(wanted, 'chan', split_axis=0, concat_axis=0, tiled=True)]
    scatter-add x1 -> x0, other arithmetic: 32.7 us -> none  [body(): jnp.zeros((codes_dev, code_dim), jnp.float32).at[desired_quantity]]
  transfers between devices with their start and end apart: 4 -> 43, of which waited for: 2 -> 15; matrix products, arithmetic and copies ran while one was open for 14% -> 14% of each run, Pallas kernels for 0% -> 27%
where the time goes in v1:
time: 274 us; the launch traced here: 273 us
  Pallas kernels  94.3 us (34%)
  starting transfers between devices  65.8 us (24%)
  waiting for transfers between devices  65.2 us (24%)
  local copies, waits for them, and re-layouts  35.4 us (13%)
  other arithmetic  10.2 us (4%)
    ppermute x42, starting transfers between devices, flip(): return lax.ppermute(x, axis, [(i, i ^ bit) for i in range(n)])  59.6 us
    ppermute x42, waiting for transfers between devices, flip(): return lax.ppermute(x, axis, [(i, i ^ bit) for i in range(n)])  56 us
    pallas_call x1, Pallas kernels, table(): pl.pallas_call(functools.partial(table_kernel, window=window), grid_spec=...  21.2 us
    pallas_call x2, Pallas kernels, project(): pl.pallas_call(functools.partial(project_kernel, count=count, added=add i...  13.9 us
    pallas_call x1, Pallas kernels, intra_block(): pl.pallas_call(intra_kernel, grid=(frames // rows,), in_specs=[pl.BlockSp...  12.2 us
    pallas_call x2, Pallas kernels, gated_blocks(): pl.pallas_call(gate_kernel, grid_spec=pltpu.PrefetchScalarGridSpec(num_sc...  11.8 us
    pallas_call x1, Pallas kernels, block_states(): pl.pallas_call(states_kernel, grid=(nb,), in_specs=[pl.BlockSpec((rows, w...  11.1 us
    pallas_call x2, Pallas kernels, ordered(): pl.pallas_call(order_kernel, grid=(total // tile,), in_specs=[pl.BlockSpe...  9.65 us
  transfers between devices with their start and end apart: 43, of which 15 were waited for; matrix products, arithmetic and copies ran while one was open for 14% of the time, Pallas kernels for 27%

profile of v1, /device:TPU:0, one launch (start us, length us, event | category | flops | bytes accessed | tf_op | source)
XLA Modules:
  0.0 272.6 jit_solution(5232016507382616111)
XLA Ops:
  0.7 2.8 %constant_dynamic-slice_fusion = (bf16[256,2048]{1,0:T(8,128)(2,1)}, bf16[256,2048]{1,0:T(8,128)(2,1)S(1)}) fusion(bf16[512,2048]{1,0:T(8,128)(2,1)} %param.18, s32[]{:T(128)S(6)} %select_n.124, s32[]{:T(128)S(6)} %select_n.123), kind=kLoop, calls=%fused_computation.97 | loop fusion | bytes 4194312 | tf_op jit(solution)/shard_map/dynamic_slice | solution.py:457
  3.4 3.1 %collective-permute-start.7 = (bf16[256,2048]{1,0:T(8,128)(2,1)S(1)}, bf16[256,2048]{1,0:T(8,128)(2,1)S(1)}, u32[]{:S(2)}, u32[]{:S(2)}) collective-permute-start(bf16[256,2048]{1,0:T(8,128)(2,1)S(1)} %get-tuple-element.16.refs_4_), channel_id=1, source_target_pairs={{0,2},{1,3},{2,0},{3,1},{4,6},{5,7},{6,4},{7,5},{8,10},{9,11},{10,... | collective-permute-start | bytes 3145736 | tf_op jit(solution)/shard_map/ppermute | solution.py:19
  9.6 6.2 %all-to-all-start = ((s32[8,1,128]{2,1,0:T(1,128)}), s32[8,1,128]{2,1,0:T(1,128)S(1)}, u32[]{:S(2)}, u32[]{:S(2)}) async-start(s32[8,1,128]{2,1,0:T(1,128)} %bitcast.16), calls=%async_computation | async-start | bytes 8192 | tf_op jit(solution)/shard_map/all_to_all | solution.py:527
  17.2 11.1 %block_states.1 = (f32[8,512,128]{2,1,0:T(8,128)}, f32[2048,8]{1,0:T(8,128)}, f32[8,8,256]{2,1,0:T(8,128)}, f32[8,1,8]{2,1,0:T(1,128)}, f32[512,128]{1,0:T(8,128)}, /*index=5*/f32[1,8]{1,0:T(1,128)}) custom-call(bf16[2048,512]{1,0:T(8,128)(2,1)} %x_ref.3, bf16[2048,128]{1,0:T(8,128)(2,1)} %b_ref.3, f32[2048,8]{1,0:T(8,128)} %copy.21.dt_ref, f32[1,8]{1,0:T(1,128)} %bitcast.109), custom_call_target="tpu_custom_call" | custom-call | tf_op jit(solution)/shard_map/block_states/pallas_call | solution.py:84
  32.6 12.2 %intra_block.1.mixed_ref = f32[2048,512]{1,0:T(8,128)} custom-call(bf16[2048,512]{1,0:T(8,128)(2,1)} %x_ref.3, bf16[2048,128]{1,0:T(8,128)(2,1)} %b_ref.3, bf16[2048,128]{1,0:T(8,128)(2,1)} %c_ref.5, f32[2048,8]{1,0:T(8,128)} %copy.21.dt_ref, f32[2048,8]{1,0:T(8,128)} %get-tuple-element.9.cums_ref, f32[8,8,256]{2,1,0:T(8,128)} %get-tuple-element.10.cums_t_ref, ...), custom_call_target="tpu_custom_call" | custom-call | tf_op jit(solution)/shard_map/intra_block/pallas_call | solution.py:150
  46.2 9.1 %all-to-all-done = s32[8,1,128]{2,1,0:T(1,128)S(1)} async-done(((s32[8,1,128]{2,1,0:T(1,128)}), s32[8,1,128]{2,1,0:T(1,128)S(1)}, u32[]{:S(2)}, u32[]{:S(2)}) %all-to-all-start) | async-done | bytes 4128 | tf_op jit(solution)/shard_map/all_to_all | solution.py:527
  56.1 8.5 %gather_fusion = bf16[1024,512]{1,0:T(8,128)(2,1)S(1)} fusion(bf16[8192,512]{1,0:T(8,128)(2,1)} %param.19, s32[1024]{0:T(1024)S(1)} %fusion.14), kind=kCustom, calls=%fused_computation | custom fusion | bytes 2101248 | tf_op jit(solution)/shard_map/jit(_take)/gather | solution.py:531
  73.3 6.0 %gated_blocks.3 = bf16[4,256,512]{2,1,0:T(8,128)(2,1)} custom-call(s32[5]{0:T(128)} %get-tuple-element.50.order_ref, f32[2048,512]{1,0:T(8,128)} %intra_block.1.mixed_ref, bf16[2048,512]{1,0:T(8,128)(2,1)} %gate_ref.3, bf16[2048,128]{1,0:T(8,128)(2,1)} %c_ref.5, f32[2048,8]{1,0:T(8,128)} %get-tuple-element.9.cums_ref, ...), custom_call_target="tpu_custom_call" | custom-call | tf_op jit(solution)/shard_map/gated_blocks/pallas_call | solution.py:196
  84.9 4.0 %collective-permute-done.18 = bf16[128,512]{1,0:T(8,128)(2,1)S(1)} collective-permute-done((bf16[128,512]{1,0:T(8,128)(2,1)}, bf16[128,512]{1,0:T(8,128)(2,1)S(1)}, u32[]{:S(2)}, u32[]{:S(2)}) %collective-permute-start.18) | collective-permute-done | bytes 131104 | tf_op jit(solution)/shard_map/ppermute | solution.py:19
  90.8 3.2 %collective-permute-done.12.refs_1_ = bf16[256,512]{1,0:T(8,128)(2,1)S(1)} collective-permute-done((bf16[256,512]{1,0:T(8,128)(2,1)S(1)}, bf16[256,512]{1,0:T(8,128)(2,1)S(1)}, u32[]{:S(2)}, u32[]{:S(2)}) %collective-permute-start.12) | collective-permute-done | bytes 262176 | tf_op jit(solution)/shard_map/ppermute | solution.py:19
  96.6 2.6 collective-permute-start.19
  99.2 6.3 %collective-permute-done.14.refs_3_ = bf16[256,512]{1,0:T(8,128)(2,1)S(1)} collective-permute-done((bf16[256,512]{1,0:T(8,128)(2,1)S(1)}, bf16[256,512]{1,0:T(8,128)(2,1)S(1)}, u32[]{:S(2)}, u32[]{:S(2)}) %collective-permute-start.14) | collective-permute-done | bytes 262176 | tf_op jit(solution)/shard_map/ppermute | solution.py:19
  112.9 6.8 %project.2 = bf16[256,2048]{1,0:T(8,128)(2,1)} custom-call(bf16[256,512]{1,0:T(8,128)(2,1)} %get-tuple-element.36.refs_0_, bf16[256,512]{1,0:T(8,128)(2,1)} %copy-done.10, bf16[256,512]{1,0:T(8,128)(2,1)} %copy-done.11, bf16[256,512]{1,0:T(8,128)(2,1)} %copy-done.14, bf16[256,2048]{1,0:T(8,128)(2,1)} %copy-done, ...), custom_call_target="tpu_custom_call" | custom-call | tf_op jit(solution)/shard_map/project/pallas_call | solution.py:244
  122.5 5.8 %gated_blocks.2 = bf16[4,256,512]{2,1,0:T(8,128)(2,1)} custom-call(s32[5]{0:T(128)} %get-tuple-element.49.order_ref, f32[2048,512]{1,0:T(8,128)} %intra_block.1.mixed_ref, bf16[2048,512]{1,0:T(8,128)(2,1)} %gate_ref.3, bf16[2048,128]{1,0:T(8,128)(2,1)} %c_ref.5, f32[2048,8]{1,0:T(8,128)} %get-tuple-element.9.cums_ref, ...), custom_call_target="tpu_custom_call" | custom-call | tf_op jit(solution)/shard_map/gated_blocks/pallas_call | solution.py:196
  133.2 10.9 %collective-permute-start.5 = (bf16[256,512]{1,0:T(8,128)(2,1)S(1)}, bf16[256,512]{1,0:T(8,128)(2,1)S(1)}, u32[]{:S(2)}, u32[]{:S(2)}) collective-permute-start(bf16[256,512]{1,0:T(8,128)(2,1)S(1)} %get-tuple-element.37), channel_id=1, source_target_pairs={{0,3},{1,2},{2,1},{3,0},{4,7},{5,6},{6,5},{7,4},{8,11},{9,10},{10,... | collective-permute-start | bytes 786440 | tf_op jit(solution)/shard_map/ppermute | solution.py:19
  150.1 22.7 %collective-permute-done.5.refs_3_ = bf16[256,512]{1,0:T(8,128)(2,1)S(1)} collective-permute-done((bf16[256,512]{1,0:T(8,128)(2,1)S(1)}, bf16[256,512]{1,0:T(8,128)(2,1)S(1)}, u32[]{:S(2)}, u32[]{:S(2)}) %collective-permute-start.5) | collective-permute-done | bytes 262176 | tf_op jit(solution)/shard_map/ppermute | solution.py:19
  173.8 7.1 %project.3.latent_ref = bf16[256,2048]{1,0:T(8,128)(2,1)} custom-call(bf16[256,512]{1,0:T(8,128)(2,1)} %get-tuple-element.40.refs_0_, bf16[256,512]{1,0:T(8,128)(2,1)} %copy-done.12, bf16[256,512]{1,0:T(8,128)(2,1)} %copy-done.13, bf16[256,512]{1,0:T(8,128)(2,1)} %copy-done.15, bf16[256,2048]{1,0:T(8,128)(2,1)} %copy-done, ...), custom_call_target="tpu_custom_call" | custom-call | tf_op jit(solution)/shard_map/project/pallas_call | solution.py:244
  180.9 6.8 %diffs.1 = bf16[8,128,512]{2,1,0:T(8,128)(2,1)} custom-call(s32[4,256]{1,0:T(4,128)} %fusion.11.pos_ref, bf16[256,2048]{1,0:T(8,128)(2,1)} %project.3.latent_ref, bf16[8,128,512]{2,1,0:T(8,128)(2,1)} %copy-done.1), custom_call_target="tpu_custom_call" | custom-call | tf_op jit(solution)/shard_map/diffs/pallas_call | solution.py:271
  194.3 2.6 collective-permute-start.29
  203.7 7.2 %collective-permute-done.28.refs_5_ = bf16[128,512]{1,0:T(8,128)(2,1)S(1)} collective-permute-done((bf16[128,512]{1,0:T(8,128)(2,1)S(1)}, bf16[128,512]{1,0:T(8,128)(2,1)S(1)}, u32[]{:S(2)}, u32[]{:S(2)}) %collective-permute-start.28) | collective-permute-done | bytes 131104 | tf_op jit(solution)/shard_map/ppermute | solution.py:19
  223.2 4.8 %ordered.2.refs_0_ = bf16[1024,512]{1,0:T(8,128)(2,1)} custom-call(s32[1,1024]{1,0:T(1,128)} %get-tuple-element.42.refs_0_, bf16[128,512]{1,0:T(8,128)(2,1)} %copy-done.9, bf16[128,512]{1,0:T(8,128)(2,1)} %copy-done.17, bf16[128,512]{1,0:T(8,128)(2,1)} %copy-done.19, bf16[128,512]{1,0:T(8,128)(2,1)} %copy-done.21, bf16[128,512]{1,0:T(8,128)(2,1)} %copy-done.18, ...), custom_call_target="tpu_custom_call" | custom-call | tf_op jit(solution)/shard_map/ordered/pallas_call | solution.py:351
  231.9 4.8 %ordered.3.refs_1_ = bf16[1024,512]{1,0:T(8,128)(2,1)} custom-call(s32[1,1024]{1,0:T(1,128)} %get-tuple-element.41.refs_0_, bf16[128,512]{1,0:T(8,128)(2,1)} %copy-done.24, bf16[128,512]{1,0:T(8,128)(2,1)} %copy-done.25, bf16[128,512]{1,0:T(8,128)(2,1)} %copy-done.26, bf16[128,512]{1,0:T(8,128)(2,1)} %copy-done.27, bf16[128,512]{1,0:T(8,128)(2,1)} %copy-done.28, ...), custom_call_target="tpu_custom_call" | custom-call | tf_op jit(solution)/shard_map/ordered/pallas_call | solution.py:351
  241.0 7.7 %latent_grads.1 = f32[256,2048]{1,0:T(8,128)} custom-call(s32[256,4]{1,0:T(8,128)} %copy.22.pos_ref, bf16[256,2048]{1,0:T(8,128)(2,1)} %project.3.latent_ref, bf16[256,2048]{1,0:T(8,128)(2,1)} %up_ref.1, bf16[1024,512]{1,0:T(8,128)(2,1)} %bitcast.99), custom_call_target="tpu_custom_call" | custom-call | tf_op jit(solution)/shard_map/latent_grads/pallas_call | solution.py:317
  251.3 21.2 %table.1 = f32[8192,512]{1,0:T(8,128)} custom-call(s32[4,33]{1,0:T(4,128)} %copy.23.bounds_ref, s32[4,1024,128]{2,1,0:T(8,128)} %broadcast_in_dim.137.codes_ref, bf16[1024,512]{1,0:T(8,128)(2,1)} %ordered.2.refs_0_, bf16[1024,512]{1,0:T(8,128)(2,1)} %ordered.3.refs_1_, bf16[1024,512]{1,0:T(8,128)(2,1)} %copy-done.5, bf16[1024,512]{1,0:T(8,128)(2,1)} %copy-done.6), custom_call_target="tpu_custom_call" | custom-call | tf_op jit(solution)/shard_map/table/pallas_call | solution.py:415
  (198 shorter events, 88.0 us)
Async XLA Ops:
  3.4 75.8 %collective-permute-start.7 = (bf16[256,2048]{1,0:T(8,128)(2,1)S(1)}, bf16[256,2048]{1,0:T(8,128)(2,1)S(1)}, u32[]{:S(2)}, u32[]{:S(2)}) collective-permute-start(bf16[256,2048]{1,0:T(8,128)(2,1)S(1)} %get-tuple-element.16.refs_4_), channel_id=1, source_target_pairs={{0,2},{1,3},{2,0},{3,1},{4,6},{5,7},{6,4},{7,5},{8,10},{9,11},{10,... | collective-permute-start | bytes 3145736 | tf_op jit(solution)/shard_map/ppermute | solution.py:19
  6.5 72.8 %collective-permute-start.8 = (bf16[256,2048]{1,0:T(8,128)(2,1)S(1)}, bf16[256,2048]{1,0:T(8,128)(2,1)}, u32[]{:S(2)}, u32[]{:S(2)}) collective-permute-start(bf16[256,2048]{1,0:T(8,128)(2,1)S(1)} %get-tuple-element.16.refs_4_), channel_id=1, source_target_pairs={{0,3},{1,2},{2,1},{3,0},{4,7},{5,6},{6,5},{7,4},{8,11},{9,10},{10,... | collective-permute-start | bytes 3145736 | tf_op jit(solution)/shard_map/ppermute | solution.py:19
  7.9 71.9 %collective-permute-start.6 = (bf16[256,2048]{1,0:T(8,128)(2,1)S(1)}, bf16[256,2048]{1,0:T(8,128)(2,1)}, u32[]{:S(2)}, u32[]{:S(2)}) collective-permute-start(bf16[256,2048]{1,0:T(8,128)(2,1)S(1)} %get-tuple-element.16.refs_4_), channel_id=1, source_target_pairs={{0,1},{1,0},{2,3},{3,2},{4,5},{5,4},{6,7},{7,6},{8,9},{9,8},{10,11... | collective-permute-start | bytes 3145736 | tf_op jit(solution)/shard_map/ppermute | solution.py:19
  9.6 45.7 %all-to-all-start = ((s32[8,1,128]{2,1,0:T(1,128)}), s32[8,1,128]{2,1,0:T(1,128)S(1)}, u32[]{:S(2)}, u32[]{:S(2)}) async-start(s32[8,1,128]{2,1,0:T(1,128)} %bitcast.16), calls=%async_computation | async-start | bytes 8192 | tf_op jit(solution)/shard_map/all_to_all | solution.py:527
  28.2 16.5 %collective-permute-start.1 = (f32[1,8]{1,0:T(1,128)}, f32[1,8]{1,0:T(1,128)S(1)}, u32[]{:S(2)}, u32[]{:S(2)}) collective-permute-start(f32[1,8]{1,0:T(1,128)} %get-tuple-element.14), channel_id=1, source_target_pairs={{0,8},{8,0},{16,24},{24,16},{1,9},{9,1},{17,25},{25,17},{2,10},{10... | collective-permute-start | bytes 104 | tf_op jit(solution)/shard_map/ppermute | solution.py:19
  29.9 35.5 %collective-permute-start = (bf16[512,128]{1,0:T(8,128)(2,1)}, bf16[512,128]{1,0:T(8,128)(2,1)S(1)}, u32[]{:S(2)}, u32[]{:S(2)}) collective-permute-start(bf16[512,128]{1,0:T(8,128)(2,1)} %convert_element_type.36), channel_id=1, source_target_pairs={{0,8},{8,0},{16,24},{24,16},{1,9},{9,1},{17,25},{25,17},{2,10},{10... | collective-permute-start | bytes 393224 | tf_op jit(solution)/shard_map/ppermute | solution.py:19
  79.2 27.8 %collective-permute-start.10 = (bf16[256,2048]{1,0:T(8,128)(2,1)S(1)}, bf16[256,2048]{1,0:T(8,128)(2,1)S(1)}, u32[]{:S(2)}, u32[]{:S(2)}) collective-permute-start(bf16[256,2048]{1,0:T(8,128)(2,1)S(1)} %collective-permute-done.7.refs_6_), channel_id=1, source_target_pairs={{0,8},{8,0},{16,24},{24,16},{1,9},{9,1},{17,25},{25,17},{2,10},{10... | collective-permute-start | bytes 3145736 | tf_op jit(solution)/shard_map/ppermute | solution.py:19
  79.3 30.6 %collective-permute-start.11 = (bf16[256,2048]{1,0:T(8,128)(2,1)}, bf16[256,2048]{1,0:T(8,128)(2,1)}, u32[]{:S(2)}, u32[]{:S(2)}) collective-permute-start(bf16[256,2048]{1,0:T(8,128)(2,1)} %collective-permute-done.8.refs_7_), channel_id=1, source_target_pairs={{0,8},{8,0},{16,24},{24,16},{1,9},{9,1},{17,25},{25,17},{2,10},{10... | collective-permute-start | bytes 3145736 | tf_op jit(solution)/shard_map/ppermute | solution.py:19
  79.8 32.1 %collective-permute-start.9 = (bf16[256,2048]{1,0:T(8,128)(2,1)}, bf16[256,2048]{1,0:T(8,128)(2,1)S(1)}, u32[]{:S(2)}, u32[]{:S(2)}) collective-permute-start(bf16[256,2048]{1,0:T(8,128)(2,1)} %collective-permute-done.6.refs_5_), channel_id=1, source_target_pairs={{0,8},{8,0},{16,24},{24,16},{1,9},{9,1},{17,25},{25,17},{2,10},{10... | collective-permute-start | bytes 3145736 | tf_op jit(solution)/shard_map/ppermute | solution.py:19
  96.6 24.0 %collective-permute-start.19 = (bf16[128,512]{1,0:T(8,128)(2,1)}, bf16[128,512]{1,0:T(8,128)(2,1)}, u32[]{:S(2)}, u32[]{:S(2)}) collective-permute-start(bf16[128,512]{1,0:T(8,128)(2,1)} %get-tuple-element.28), channel_id=1, source_target_pairs={{0,4},{1,5},{2,6},{3,7},{4,0},{5,1},{6,2},{7,3},{8,12},{9,13},{10,... | collective-permute-start | bytes 393224 | tf_op jit(solution)/shard_map/ppermute | solution.py:19
  105.5 16.1 %collective-permute-start.20 = (bf16[128,512]{1,0:T(8,128)(2,1)}, bf16[128,512]{1,0:T(8,128)(2,1)}, u32[]{:S(2)}, u32[]{:S(2)}) collective-permute-start(bf16[128,512]{1,0:T(8,128)(2,1)} %get-tuple-element.27), channel_id=1, source_target_pairs={{0,5},{1,4},{2,7},{3,6},{4,1},{5,0},{6,3},{7,2},{8,13},{9,12},{10,... | collective-permute-start | bytes 393224 | tf_op jit(solution)/shard_map/ppermute | solution.py:19
  108.1 25.1 %collective-permute-start.21 = (bf16[128,512]{1,0:T(8,128)(2,1)}, bf16[128,512]{1,0:T(8,128)(2,1)}, u32[]{:S(2)}, u32[]{:S(2)}) collective-permute-start(bf16[128,512]{1,0:T(8,128)(2,1)} %get-tuple-element.26), channel_id=1, source_target_pairs={{0,6},{1,7},{2,4},{3,5},{4,2},{5,3},{6,0},{7,1},{8,14},{9,15},{10,... | collective-permute-start | bytes 393224 | tf_op jit(solution)/shard_map/ppermute | solution.py:19
  110.0 35.1 %collective-permute-start.22 = (bf16[128,512]{1,0:T(8,128)(2,1)S(1)}, bf16[128,512]{1,0:T(8,128)(2,1)}, u32[]{:S(2)}, u32[]{:S(2)}) collective-permute-start(bf16[128,512]{1,0:T(8,128)(2,1)S(1)} %copy-done.16), channel_id=1, source_target_pairs={{0,7},{1,6},{2,5},{3,4},{4,3},{5,2},{6,1},{7,0},{8,15},{9,14},{10,... | collective-permute-start | bytes 393224 | tf_op jit(solution)/shard_map/ppermute | solution.py:19
  119.6 53.1 %collective-permute-start.15 = (bf16[256,2048]{1,0:T(8,128)(2,1)}, bf16[256,2048]{1,0:T(8,128)(2,1)S(1)}, u32[]{:S(2)}, u32[]{:S(2)}) collective-permute-start(bf16[256,2048]{1,0:T(8,128)(2,1)} %project.2), channel_id=1, source_target_pairs={{0,4},{1,5},{2,6},{3,7},{4,0},{5,1},{6,2},{7,3},{8,12},{9,13},{10,... | collective-permute-start | bytes 3145736 | tf_op jit(solution)/shard_map/ppermute | solution.py:19
  130.3 17.2 %collective-permute-start.3 = (bf16[256,512]{1,0:T(8,128)(2,1)S(1)}, bf16[256,512]{1,0:T(8,128)(2,1)S(1)}, u32[]{:S(2)}, u32[]{:S(2)}) collective-permute-start(bf16[256,512]{1,0:T(8,128)(2,1)S(1)} %get-tuple-element.39), channel_id=1, source_target_pairs={{0,1},{1,0},{2,3},{3,2},{4,5},{5,4},{6,7},{7,6},{8,9},{9,8},{10,11... | collective-permute-start | bytes 786440 | tf_op jit(solution)/shard_map/ppermute | solution.py:19
  131.2 18.8 %collective-permute-start.4 = (bf16[256,512]{1,0:T(8,128)(2,1)S(1)}, bf16[256,512]{1,0:T(8,128)(2,1)S(1)}, u32[]{:S(2)}, u32[]{:S(2)}) collective-permute-start(bf16[256,512]{1,0:T(8,128)(2,1)S(1)} %get-tuple-element.38), channel_id=1, source_target_pairs={{0,2},{1,3},{2,0},{3,1},{4,6},{5,7},{6,4},{7,5},{8,10},{9,11},{10,... | collective-permute-start | bytes 786440 | tf_op jit(solution)/shard_map/ppermute | solution.py:19
  133.2 39.5 %collective-permute-start.5 = (bf16[256,512]{1,0:T(8,128)(2,1)S(1)}, bf16[256,512]{1,0:T(8,128)(2,1)S(1)}, u32[]{:S(2)}, u32[]{:S(2)}) collective-permute-start(bf16[256,512]{1,0:T(8,128)(2,1)S(1)} %get-tuple-element.37), channel_id=1, source_target_pairs={{0,3},{1,2},{2,1},{3,0},{4,7},{5,6},{6,5},{7,4},{8,11},{9,10},{10,... | collective-permute-start | bytes 786440 | tf_op jit(solution)/shard_map/ppermute | solution.py:19
  145.0 49.3 %collective-permute-start.23 = (s32[1,1024]{1,0:T(1,128)S(1)}, s32[1,1024]{1,0:T(1,128)S(1)}, u32[]{:S(2)}, u32[]{:S(2)}) collective-permute-start(s32[1,1024]{1,0:T(1,128)S(1)} %bitcast.101), channel_id=1, source_target_pairs={{0,16},{8,24},{16,0},{24,8},{1,17},{9,25},{17,1},{25,9},{2,18},{10... | collective-permute-start | bytes 12296 | tf_op jit(solution)/shard_map/ppermute | solution.py:19
  192.6 18.3 %collective-permute-start.28 = (bf16[128,512]{1,0:T(8,128)(2,1)S(1)}, bf16[128,512]{1,0:T(8,128)(2,1)S(1)}, u32[]{:S(2)}, u32[]{:S(2)}) collective-permute-start(bf16[128,512]{1,0:T(8,128)(2,1)S(1)} %get-tuple-element.20), channel_id=1, source_target_pairs={{0,4},{1,5},{2,6},{3,7},{4,0},{5,1},{6,2},{7,3},{8,12},{9,13},{10,... | collective-permute-start | bytes 393224 | tf_op jit(solution)/shard_map/ppermute | solution.py:19
  194.3 20.4 %collective-permute-start.29 = (bf16[128,512]{1,0:T(8,128)(2,1)S(1)}, bf16[128,512]{1,0:T(8,128)(2,1)S(1)}, u32[]{:S(2)}, u32[]{:S(2)}) collective-permute-start(bf16[128,512]{1,0:T(8,128)(2,1)S(1)} %get-tuple-element.19), channel_id=1, source_target_pairs={{0,5},{1,4},{2,7},{3,6},{4,1},{5,0},{6,3},{7,2},{8,13},{9,12},{10,... | collective-permute-start | bytes 393224 | tf_op jit(solution)/shard_map/ppermute | solution.py:19
  196.9 20.4 %collective-permute-start.30 = (bf16[128,512]{1,0:T(8,128)(2,1)S(1)}, bf16[128,512]{1,0:T(8,128)(2,1)S(1)}, u32[]{:S(2)}, u32[]{:S(2)}) collective-permute-start(bf16[128,512]{1,0:T(8,128)(2,1)S(1)} %get-tuple-element.18), channel_id=1, source_target_pairs={{0,6},{1,7},{2,4},{3,5},{4,2},{5,3},{6,0},{7,1},{8,14},{9,15},{10,... | collective-permute-start | bytes 393224 | tf_op jit(solution)/shard_map/ppermute | solution.py:19
  200.1 17.8 %collective-permute-start.31 = (bf16[128,512]{1,0:T(8,128)(2,1)S(1)}, bf16[128,512]{1,0:T(8,128)(2,1)S(1)}, u32[]{:S(2)}, u32[]{:S(2)}) collective-permute-start(bf16[128,512]{1,0:T(8,128)(2,1)S(1)} %get-tuple-element.17), channel_id=1, source_target_pairs={{0,7},{1,6},{2,5},{3,4},{4,3},{5,2},{6,1},{7,0},{8,15},{9,14},{10,... | collective-permute-start | bytes 393224 | tf_op jit(solution)/shard_map/ppermute | solution.py:19
  202.2 17.3 %collective-permute-start.32 = (bf16[128,512]{1,0:T(8,128)(2,1)S(1)}, bf16[128,512]{1,0:T(8,128)(2,1)S(1)}, u32[]{:S(2)}, u32[]{:S(2)}) collective-permute-start(bf16[128,512]{1,0:T(8,128)(2,1)S(1)} %get-tuple-element.24.refs_1_), channel_id=1, source_target_pairs={{0,16},{8,24},{16,0},{24,8},{1,17},{9,25},{17,1},{25,9},{2,18},{10... | collective-permute-start | bytes 393224 | tf_op jit(solution)/shard_map/ppermute | solution.py:19
  228.1 20.7 %collective-permute-start.40 = (bf16[1024,512]{1,0:T(8,128)(2,1)}, bf16[1024,512]{1,0:T(8,128)(2,1)S(1)}, u32[]{:S(2)}, u32[]{:S(2)}) collective-permute-start(bf16[1024,512]{1,0:T(8,128)(2,1)} %ordered.2.refs_0_), channel_id=1, source_target_pairs={{0,8},{8,0},{16,24},{24,16},{1,9},{9,1},{17,25},{25,17},{2,10},{10... | collective-permute-start | bytes 3145736 | tf_op jit(solution)/shard_map/ppermute | solution.py:19
  (55 other events, 693.0 us)

commit v2 on v1

v2 whole, which is shorter than its diff:
```python
import functools

import jax
import jax.numpy as jnp
from jax import lax
from jax.experimental import pallas as pl
from jax.experimental.pallas import tpu as pltpu
from jax.sharding import PartitionSpec as P


COMMIT = 0.25
CODE_BLOCK = 256
F32 = jnp.float32
BF16 = jnp.bfloat16


def flip(x, axis, bit):
    n = lax.axis_size(axis)
    return lax.ppermute(x, axis, [(i, i ^ bit) for i in range(n)])


def dot_nt(a, b):
    return lax.dot_general(a, b, (((1,), (1,)), ((), ())), preferred_element_type=F32)


def per_head(values, heads, width):
    rows = values.shape[0]
    return jnp.concatenate(
        [jnp.broadcast_to(values[:, h : h + 1], (rows, width)) for h in range(heads)], axis=1
    )


def states_kernel(
    x_ref, b_ref, dt_ref, rate_ref, starts_ref, cums_ref, before_ref, final_ref, sent_ref,
    state, seen, upper,
):
    step = pl.program_id(0)
    rows, width = x_ref.shape
    heads = dt_ref.shape[0]
    head_dim = width // heads

    @pl.when(step == 0)
    def _():
        state[...] = jnp.zeros_like(state)
        seen[...] = jnp.zeros_like(seen)
        upper[...] = jnp.where(
            lax.broadcasted_iota(jnp.int32, (rows, rows), 0)
            <= lax.broadcasted_iota(jnp.int32, (rows, rows), 1),
            1.0,
            0.0,
        ).astype(BF16)

    dt = dt_ref[...]
    logs = -dt * rate_ref[...]
    one = logs.astype(BF16).astype(F32)
    two = (logs - one).astype(BF16).astype(F32)
    three = logs - one - two
    terms = jnp.concatenate([one, two, three, jnp.zeros_like(one)], axis=0).astype(BF16)
    sums = jnp.dot(terms, upper[...], preferred_element_type=F32)
    cums = sums[:heads] + sums[heads : 2 * heads] + sums[2 * heads : 3 * heads]
    cums_ref[...] = cums
    before_ref[0] = seen[...]
    total = cums[:, rows - 1 : rows]
    weight = dt * jnp.exp(total - cums)
    x_t = x_ref[...].T
    scaled = jnp.concatenate(
        [
            (x_t[h * head_dim : (h + 1) * head_dim, :].astype(F32) * weight[h : h + 1, :]).astype(
                BF16
            )
            for h in range(heads)
        ],
        axis=0,
    )
    fresh = jnp.dot(scaled, b_ref[...], preferred_element_type=F32)
    starts_ref[0] = state[...].astype(BF16)
    keep = jnp.exp(jnp.broadcast_to(total, seen.shape))
    for h in range(heads):
        rs = slice(h * head_dim, (h + 1) * head_dim)
        state[rs, :] = state[rs, :] * keep[h : h + 1, :] + fresh[rs, :]
    seen[...] = seen[...] + total

    @pl.when(step == pl.num_programs(0) - 1)
    def _():
        final_ref[...] = state[...]
        sent_ref[...] = state[...].astype(BF16)


def block_states(frames_in, in_keys, step_t, rate, rows):
    frames, width = frames_in.shape
    nstate = in_keys.shape[1]
    heads = step_t.shape[0]
    nb = frames // rows
    return pl.pallas_call(
        states_kernel,
        grid=(nb,),
        in_specs=[
            pl.BlockSpec((rows, width), lambda i: (i, 0)),
            pl.BlockSpec((rows, nstate), lambda i: (i, 0)),
            pl.BlockSpec((heads, rows), lambda i: (0, i)),
            pl.BlockSpec((heads, 1), lambda i: (0, 0)),
        ],
        out_specs=[
            pl.BlockSpec((1, width, nstate), lambda i: (i, 0, 0)),
            pl.BlockSpec((heads, rows), lambda i: (0, i)),
            pl.BlockSpec((1, heads, nstate), lambda i: (i, 0, 0)),
            pl.BlockSpec((width, nstate), lambda i: (0, 0)),
            pl.BlockSpec((width, nstate), lambda i: (0, 0)),
        ],
        out_shape=[
            jax.ShapeDtypeStruct((nb, width, nstate), BF16),
            jax.ShapeDtypeStruct((heads, frames), F32),
            jax.ShapeDtypeStruct((nb, heads, nstate), F32),
            jax.ShapeDtypeStruct((width, nstate), F32),
            jax.ShapeDtypeStruct((width, nstate), BF16),
        ],
        scratch_shapes=[
            pltpu.VMEM((width, nstate), F32),
            pltpu.VMEM((heads, nstate), F32),
            pltpu.VMEM((rows, rows), BF16),
        ],
        name="block_states",
    )(frames_in, in_keys, step_t, rate)


def intra_kernel(
    order_ref, x_ref, gate_ref, b_ref, c_ref, dt_ref, cums_ref, skip_ref, base_ref, slope_ref
):
    rows, width = x_ref.shape
    heads = dt_ref.shape[0]
    head_dim = width // heads
    tile = min(rows, 128)
    cums_t = cums_ref[...]
    cums = cums_t.T
    dt = dt_ref[...]
    for t in range(rows // tile):
        rs = slice(t * tile, (t + 1) * tile)
        n = (t + 1) * tile
        gram = dot_nt(c_ref[rs, :], b_ref[0:n, :])
        allowed = (
            lax.broadcasted_iota(jnp.int32, (tile, n), 0) + t * tile
            >= lax.broadcasted_iota(jnp.int32, (tile, n), 1)
        )
        parts = []
        for h in range(heads):
            spread = cums[rs, h : h + 1] - cums_t[h : h + 1, 0:n]
            mask = jnp.exp(jnp.where(allowed, spread, -1e30)) * dt[h : h + 1, 0:n]
            parts.append(
                jnp.dot(
                    (mask * gram).astype(BF16),
                    x_ref[0:n, h * head_dim : (h + 1) * head_dim],
                    preferred_element_type=F32,
                )
            )
        gate = gate_ref[rs, :].astype(F32)
        gate = gate / (1.0 + jnp.exp(-gate))
        mixed = jnp.concatenate(parts, axis=1) + x_ref[rs, :].astype(F32) * skip_ref[...]
        base_ref[0, rs, :] = mixed * gate
        slope_ref[0, rs, :] = (gate * per_head(jnp.exp(cums[rs, :]), heads, head_dim)).astype(BF16)


def intra_block(order, count, frames_in, gate_in, in_keys, out_keys, step_t, cums, skip, rows):
    width = frames_in.shape[1]
    nstate = in_keys.shape[1]
    heads = step_t.shape[0]
    return pl.pallas_call(
        intra_kernel,
        grid_spec=pltpu.PrefetchScalarGridSpec(
            num_scalar_prefetch=1,
            grid=(count,),
            in_specs=[
                pl.BlockSpec((rows, width), lambda i, o: (o[i], 0)),
                pl.BlockSpec((rows, width), lambda i, o: (o[i], 0)),
                pl.BlockSpec((rows, nstate), lambda i, o: (o[i], 0)),
                pl.BlockSpec((rows, nstate), lambda i, o: (o[i], 0)),
                pl.BlockSpec((heads, rows), lambda i, o: (0, o[i])),
                pl.BlockSpec((heads, rows), lambda i, o: (0, o[i])),
                pl.BlockSpec((1, width), lambda i, o: (0, 0)),
            ],
            out_specs=[pl.BlockSpec((1, rows, width), lambda i, o: (i, 0, 0))] * 2,
        ),
        out_shape=[
            jax.ShapeDtypeStruct((count, rows, width), F32),
            jax.ShapeDtypeStruct((count, rows, width), BF16),
        ],
        name="intra_block",
    )(order, frames_in, gate_in, in_keys, out_keys, step_t, cums, skip)


def gate_kernel(order_ref, base_ref, slope_ref, c_ref, starts_ref, before_ref, incoming_ref, *outs):
    width = base_ref.shape[2]
    heads = before_ref.shape[1]
    head_dim = width // heads
    carry = jnp.exp(before_ref[0])
    parts = []
    for h in range(heads):
        rs = slice(h * head_dim, (h + 1) * head_dim)
        parts.append(starts_ref[0, rs, :].astype(F32) + incoming_ref[rs, :] * carry[h : h + 1, :])
    start = jnp.concatenate(parts, axis=0).astype(BF16)
    inter = dot_nt(c_ref[...], start)
    gated = (base_ref[0] + inter * slope_ref[0].astype(F32)).astype(BF16)
    for k, out_ref in enumerate(outs):

        @pl.when(pl.program_id(0) == k)
        def _():
            out_ref[...] = gated


def gated_blocks(order, base, slope, out_keys, starts, before, incoming):
    count, rows, width = base.shape
    nstate = out_keys.shape[1]
    heads = before.shape[1]
    return pl.pallas_call(
        gate_kernel,
        grid_spec=pltpu.PrefetchScalarGridSpec(
            num_scalar_prefetch=1,
            grid=(count,),
            in_specs=[
                pl.BlockSpec((1, rows, width), lambda i, o: (i, 0, 0)),
                pl.BlockSpec((1, rows, width), lambda i, o: (i, 0, 0)),
                pl.BlockSpec((rows, nstate), lambda i, o: (o[i], 0)),
                pl.BlockSpec((1, width, nstate), lambda i, o: (o[i], 0, 0)),
                pl.BlockSpec((1, heads, nstate), lambda i, o: (o[i], 0, 0)),
                pl.BlockSpec((width, nstate), lambda i, o: (0, 0)),
            ],
            out_specs=[pl.BlockSpec((rows, width), lambda i, o: (0, 0))] * count,
        ),
        out_shape=[jax.ShapeDtypeStruct((rows, width), BF16)] * count,
        name="gated_blocks",
    )(order, base, slope, out_keys, starts, before, incoming)


def project_kernel(core_ref, *refs, count):
    gs = refs[:count]
    firsts = refs[count : 2 * count]
    seconds = refs[2 * count : 3 * count]
    out_ref = refs[-1]
    half = firsts[0].shape[0]
    mine = pl.multiple_of(core_ref[0] * half, half)
    other = pl.multiple_of((1 - core_ref[0]) * half, half)
    acc = None
    for g, a, b in zip(gs, firsts, seconds):
        part = jnp.dot(g[:, pl.ds(mine, half)], a[...], preferred_element_type=F32)
        part = part + jnp.dot(g[:, pl.ds(other, half)], b[...], preferred_element_type=F32)
        acc = part if acc is None else acc + part
    out_ref[...] = acc.astype(out_ref.dtype)


def project(core, gs, firsts, seconds, dtype):
    count = len(gs)
    rows, width = gs[0].shape
    half, cols = firsts[0].shape
    tile = min(cols, 512)
    in_specs = [pl.BlockSpec((rows, width), lambda j, c: (0, 0))] * count
    in_specs += [pl.BlockSpec((half, tile), lambda j, c: (0, j))] * (2 * count)
    return pl.pallas_call(
        functools.partial(project_kernel, count=count),
        grid_spec=pltpu.PrefetchScalarGridSpec(
            num_scalar_prefetch=1,
            grid=(cols // tile,),
            in_specs=in_specs,
            out_specs=pl.BlockSpec((rows, tile), lambda j, c: (0, j)),
        ),
        out_shape=jax.ShapeDtypeStruct((rows, cols), dtype),
        name="project",
    )(core, *gs, *firsts, *seconds)


def send_kernel(chan_ref, pos_ref, near_ref, across_ref, latent_ref, *outs):
    slots, dim = outs[0].shape
    groups, rows = pos_ref.shape
    latent = (near_ref[...] + across_ref[...].astype(F32)).astype(BF16)
    latent_ref[...] = latent
    slot = lax.broadcasted_iota(jnp.int32, (slots, rows), 0)
    for k, out_ref in enumerate(outs):
        here = slot + (chan_ref[0] ^ k) * slots
        acc = None
        for g in range(groups):
            pick = jnp.where(here == pos_ref[g : g + 1, :], 1.0, 0.0).astype(BF16)
            part = jnp.dot(pick, latent[:, g * dim : (g + 1) * dim], preferred_element_type=F32)
            acc = part if acc is None else acc + part
        out_ref[...] = acc.astype(BF16)


def sent_rows(chan, pos, near, across, count, slots, dim):
    rows, cols = near.shape
    return pl.pallas_call(
        send_kernel,
        grid_spec=pltpu.PrefetchScalarGridSpec(
            num_scalar_prefetch=1,
            grid=(1,),
            in_specs=[
                pl.BlockSpec(pos.shape, lambda i, c: (0, 0)),
                pl.BlockSpec(near.shape, lambda i, c: (0, 0)),
                pl.BlockSpec(across.shape, lambda i, c: (0, 0)),
            ],
            out_specs=[pl.BlockSpec((rows, cols), lambda i, c: (0, 0))]
            + [pl.BlockSpec((slots, dim), lambda i, c: (0, 0))] * count,
        ),
        out_shape=[jax.ShapeDtypeStruct((rows, cols), BF16)]
        + [jax.ShapeDtypeStruct((slots, dim), BF16)] * count,
        name="sent_rows",
    )(chan, pos, near, across)


def norm_of(v):
    return jnp.sqrt(jnp.sum(v * v, axis=-1, keepdims=True) + 1e-06)


def grad_kernel(pos_ref, latent_ref, up_ref, q_ref, out_ref):
    entries, dim = q_ref.shape
    rows = latent_ref.shape[0]
    groups = latent_ref.shape[1] // dim
    slot = lax.broadcasted_iota(jnp.int32, (rows, entries), 1)
    for n in range(groups):
        cols = slice(n * dim, (n + 1) * dim)
        pick = jnp.where(slot == pos_ref[:, n : n + 1], 1.0, 0.0).astype(BF16)
        q = jnp.dot(pick, q_ref[...], preferred_element_type=F32)
        e = latent_ref[:, cols].astype(F32)
        g = up_ref[:, cols].astype(F32)
        ne = norm_of(e)
        nq = norm_of(q)
        eh = e / ne
        qh = q / nq
        summed = eh + qh
        unit = summed / norm_of(summed)
        along = jnp.sum(unit * g, axis=-1, keepdims=True)
        toward = jnp.sum(qh * g, axis=-1, keepdims=True)
        out_ref[:, cols] = (nq / ne) * (g - 2.0 * unit * along + 2.0 * eh * toward) + (
            2.0 * COMMIT
        ) * (e - q)


def latent_grads(pos_cols, latent, upstream, q):
    rows, width = latent.shape
    groups = pos_cols.shape[1]
    tile = min(rows, 128)
    return pl.pallas_call(
        grad_kernel,
        grid=(rows // tile,),
        in_specs=[
            pl.BlockSpec((tile, groups), lambda i: (i, 0)),
            pl.BlockSpec((tile, width), lambda i: (i, 0)),
            pl.BlockSpec((tile, width), lambda i: (i, 0)),
            pl.BlockSpec(q.shape, lambda i: (0, 0)),
        ],
        out_specs=pl.BlockSpec((tile, width), lambda i: (i, 0)),
        out_shape=jax.ShapeDtypeStruct((rows, width), F32),
        name="latent_grads",
    )(pos_cols, latent, upstream, q)


def order_kernel(chan_ref, place_ref, picked_ref, *refs):
    chunks = refs[:-1]
    out_ref = refs[-1]
    tile = out_ref.shape[0]
    slots = chunks[0].shape[0]
    joined = max(1, min(len(chunks), 256 // slots))
    slot = lax.broadcasted_iota(jnp.int32, (tile, joined * slots), 0) + pl.program_id(0) * tile
    acc = None
    for n in range(0, len(chunks), joined):
        here = []
        values = []
        for k in range(n, n + joined):
            source = chan_ref[0] ^ k
            here.append(place_ref[source])
            q = picked_ref[source].astype(F32)
            values.append((q - chunks[k][...].astype(F32)).astype(BF16))
        pick = jnp.where(slot == jnp.concatenate(here, axis=1), 1.0, 0.0).astype(BF16)
        part = jnp.dot(pick, jnp.concatenate(values, axis=0), preferred_element_type=F32)
        acc = part if acc is None else acc + part
    out_ref[...] = acc.astype(BF16)


def ordered(chan, place, picked, chunks):
    slots, dim = chunks[0].shape
    total = slots * len(chunks)
    tile = min(total, 512)
    return pl.pallas_call(
        order_kernel,
        grid_spec=pltpu.PrefetchScalarGridSpec(
            num_scalar_prefetch=1,
            grid=(total // tile,),
            in_specs=[
                pl.BlockSpec(place.shape, lambda i, c: (0, 0, 0)),
                pl.BlockSpec(picked.shape, lambda i, c: (0, 0, 0)),
            ]
            + [pl.BlockSpec((slots, dim), lambda i, c: (0, 0))] * len(chunks),
            out_specs=pl.BlockSpec((tile, dim), lambda i, c: (i, 0)),
        ),
        out_shape=jax.ShapeDtypeStruct((total, dim), BF16),
        name="ordered",
    )(chan, place, picked, *chunks)


def table_kernel(bounds_ref, codes_ref, *refs, window, codes):
    runs = refs[:-1]
    out_ref = refs[-1]
    length = runs[0].shape[0]
    parts = out_ref.shape[0] // codes

    def gathered(part, turn):
        block = pl.program_id(0) * parts + part
        code = lax.broadcasted_iota(jnp.int32, (codes, window * len(runs)), 0) + block * codes
        picks = []
        rows = []
        for r, run in enumerate(runs):
            first = (bounds_ref[r, block] // 16) * 16 + turn * window
            at = pl.multiple_of(jnp.minimum(first, length - window), 16)
            lane = pl.multiple_of((at // 128) * 128, 128)
            near = codes_ref[r : r + 1, pl.ds(lane, 256)]
            near = pltpu.roll(jnp.broadcast_to(near, (8, 256)), (lane - at) % 256, 1)
            near = near[0:1, :window]
            col = lax.broadcasted_iota(jnp.int32, (1, window), 1) + at
            picks.append(jnp.where(col >= first, near, -1))
            rows.append(run[pl.ds(at, window), :])
        pick = jnp.where(jnp.concatenate(picks, axis=1) == code, 2.0, 0.0).astype(BF16)
        return jnp.dot(pick, jnp.concatenate(rows, axis=0), preferred_element_type=F32)

    for part in range(parts):
        out_ref[part * codes : (part + 1) * codes, :] = gathered(part, 0)
    for part in range(parts):
        block = pl.program_id(0) * parts + part
        turns = 0
        for r in range(len(runs)):
            lo = (bounds_ref[r, block] // 16) * 16
            turns = jnp.maximum(turns, (bounds_ref[r, block + 1] - lo + window - 1) // window)

        def more(turn, carry):
            out_ref[part * codes : (part + 1) * codes, :] += gathered(part, turn)
            return carry

        lax.fori_loop(1, turns, more, 0)


def table(bounds, codes, runs, codes_dev):
    length, dim = runs[0].shape
    block = min(CODE_BLOCK, codes_dev)
    blocks = codes_dev // block
    parts = 4
    while blocks % parts:
        parts //= 2
    window = 16
    while window < 128 and window < length and window < 2 * length // blocks:
        window *= 2
    return pl.pallas_call(
        functools.partial(table_kernel, window=window, codes=block),
        grid_spec=pltpu.PrefetchScalarGridSpec(
            num_scalar_prefetch=1,
            grid=(blocks // parts,),
            in_specs=[pl.BlockSpec(codes.shape, lambda i, b: (0, 0))]
            + [pl.BlockSpec((length, dim), lambda i, b: (0, 0))] * len(runs),
            out_specs=pl.BlockSpec((parts * block, dim), lambda i, b: (i, 0)),
        ),
        out_shape=jax.ShapeDtypeStruct((codes_dev, dim), F32),
        name="table",
    )(bounds, codes, *runs)


def layer(
    frames_in,
    gate_in,
    in_keys,
    out_keys,
    step_size,
    decay_rate,
    skip_gain,
    out_weight,
    codebook,
    code_index,
    upstream,
):
    chans = lax.axis_size("chan")
    seqs = lax.axis_size("seq")
    chan = lax.axis_index("chan").astype(jnp.int32)
    seq = lax.axis_index("seq").astype(jnp.int32)
    half = chans // 2
    core = seq % 2
    frames, width = frames_in.shape
    rows = frames // chans
    codes_dev, dim = codebook.shape
    groups = code_index.shape[1]
    heads = decay_rate.shape[0]
    head_dim = width // heads

    entries = rows * groups
    slots = max(1, (entries + chans - 1) // chans)
    flat = code_index.T.reshape(entries)
    owner = flat // codes_dev
    within = flat - owner * codes_dev
    hot = (owner[:, None] == jnp.arange(chans, dtype=jnp.int32)[None, :]).astype(BF16)
    entry = jnp.arange(entries, dtype=jnp.int32)
    earlier = (entry[:, None] > entry[None, :]).astype(BF16)
    counts = jnp.dot(earlier, hot, preferred_element_type=F32)
    rank = jnp.sum(counts * hot.astype(F32), axis=1).astype(jnp.int32)
    slot_of = owner * slots + rank
    pos = slot_of.reshape(groups, rows)
    wanted = jnp.sum(
        jnp.where(slot_of[None, :] == entry[:, None], within[None, :] + 1, 0), axis=1
    )
    wanted = jnp.where(wanted == 0, codes_dev, wanted - 1).reshape(chans, slots)
    wrows = out_weight.shape[0] // 2
    mine = lax.dynamic_slice_in_dim(out_weight, core * wrows, wrows, 0)
    other = lax.dynamic_slice_in_dim(out_weight, (1 - core) * wrows, wrows, 0)
    firsts = [mine] + [flip(mine, "chan", k) for k in range(1, half)]
    seconds = [other] + [flip(firsts[k], "seq", 1) for k in range(1, half)]

    step_t = step_size.T
    rate = decay_rate.reshape(heads, 1)
    starts, cums, before, held, sent = block_states(frames_in, in_keys, step_t, rate, rows)
    held_log = -jnp.sum(step_t * rate, axis=1)
    lower_log = jnp.zeros_like(held_log)

    def rows_of(logs, use, otherwise):
        return jnp.repeat(jnp.where(use, jnp.exp(logs), otherwise), head_dim)[:, None]

    factors = []
    bit = 1
    while bit < seqs:
        got_log = flip(held_log, "seq", bit)
        after = (seq & bit) != 0
        factors.append(
            (
                rows_of(lower_log, after, 0.0),
                rows_of(held_log, after, 1.0),
                rows_of(got_log, ~after, 1.0),
            )
        )
        lower_log = jnp.where(after, lower_log + got_log, lower_log)
        held_log = held_log + got_log
        bit *= 2
    incoming = jnp.zeros_like(held)
    bit = 1
    for to_incoming, to_got, to_held in factors:
        got = flip(sent, "seq", bit).astype(F32)
        incoming = incoming + to_incoming * got
        held = to_got * got + to_held * held
        sent = held.astype(BF16)
        bit *= 2

    top = chan // half
    low = chan % half
    turn = jnp.arange(half, dtype=jnp.int32)
    near = jnp.concatenate([top * half + (low ^ turn), core[None]])
    far = jnp.concatenate([(1 - top) * half + (low ^ turn), core[None]])
    skip = jnp.repeat(skip_gain, head_dim)[None, :]

    def gated_for(which):
        base, slope = intra_block(
            which, half, frames_in, gate_in, in_keys, out_keys, step_t, cums, skip, rows
        )
        return gated_blocks(which, base, slope, out_keys, starts, before, incoming)

    def exchanged(out):
        return [out[0]] + [flip(out[k], "chan", k) for k in range(1, half)]

    far_out = gated_for(far)
    far_blocks = exchanged(far_out)
    near, _ = lax.optimization_barrier((near, far_out))
    near_out = gated_for(near)
    near_blocks = exchanged(near_out)
    wanted, _ = lax.optimization_barrier((wanted, near_out))
    received = lax.all_to_all(wanted, "chan", split_axis=0, concat_axis=0, tiled=True)
    far_sums = project(core[None], far_blocks, firsts, seconds, BF16)
    across = flip(far_sums, "chan", half)
    near_sums = project(core[None], near_blocks, firsts, seconds, F32)

    asked = received.reshape(1, entries)
    bit = seqs // 2
    while bit > 1:
        asked = jnp.concatenate([asked, flip(asked, "seq", bit)])
        bit //= 2
    picked = jnp.take(
        codebook, jnp.minimum(asked, codes_dev - 1).reshape(-1, slots), axis=0
    ).reshape(-1, chans, slots, dim)
    keys = asked * entries + entry[None, :]
    ranks = jnp.sum((keys[:, None, :] < keys[:, :, None]).astype(jnp.int32), axis=2)
    run_codes = jnp.sum(
        jnp.where(ranks[:, None, :] == entry[None, :, None], asked[:, None, :], 0), axis=2
    )
    if seqs > 1:
        run_codes = jnp.concatenate([run_codes, flip(run_codes, "seq", 1)])
    block = min(CODE_BLOCK, codes_dev)
    edges = jnp.arange(codes_dev // block + 1, dtype=jnp.int32) * block
    bounds = jnp.sum((run_codes[:, None, :] < edges[None, :, None]).astype(jnp.int32), axis=2)
    run_codes = jnp.pad(run_codes, ((0, 0), (0, 256)), constant_values=-1)

    near_sums, ranks, run_codes, bounds, picked = lax.optimization_barrier(
        (near_sums, ranks, run_codes, bounds, picked)
    )
    latent, *sends = sent_rows(chan[None], pos, near_sums, across, chans, slots, dim)
    arrived = {0: sends[0]}
    for k in range(1, chans):
        arrived[k] = flip(sends[k], "chan", k)
    back, _ = lax.optimization_barrier((picked[0], sends[0]))
    q = lax.all_to_all(back, "chan", split_axis=0, concat_axis=0, tiled=True)
    chunks = []
    for k in range(chans):
        got = [arrived[k]]
        bit = seqs // 2
        while bit > 1:
            got = got + [flip(a, "seq", bit) for a in got]
            bit //= 2
        chunks.append(got)
    runs = [
        ordered(
            chan[None],
            ranks[r].reshape(chans, 1, slots),
            picked[r],
            [chunks[k][r] for k in range(chans)],
        )
        for r in range(max(1, seqs // 2))
    ]
    if seqs > 1:
        runs = runs + [flip(a, "seq", 1) for a in runs]
    codebook_grad = table(bounds, run_codes, runs, codes_dev)
    latent_grad = latent_grads(pos.T, latent, upstream, q.reshape(entries, dim))
    return (latent, latent_grad, codebook_grad)


def solution(mesh):
    placed = (
        P("seq", "chan"),
        P("seq", "chan"),
        P("seq", None),
        P("seq", None),
        P("seq", "chan"),
        P("chan"),
        P("chan"),
        P("chan", None),
        P("chan", None),
        P(("seq", "chan"), None),
        P(("seq", "chan"), None),
    )
    return jax.shard_map(
        layer,
        mesh=mesh,
        in_specs=placed,
        out_specs=(P(("seq", "chan"), None), P(("seq", "chan"), None), P("chan", None)),
        check_vma=False,
    )
```

time: 274 us -> 259 us (0.945)
  waiting for transfers between devices: 65.2 us -> 87.5 us
  Pallas kernels: 94.3 us -> 78.9 us
  starting transfers between devices: 65.8 us -> 52.6 us
  local copies, waits for them, and re-layouts: 35.4 us -> 25.9 us
    ppermute x42 -> x35, waiting for transfers between devices: 56 us -> 81.1 us  [flip(): return lax.ppermute(x, axis, [(i, i ^ bit) for i in range(n)])]
    ppermute x42 -> x35, starting transfers between devices: 59.6 us -> 43.8 us  [flip(): return lax.ppermute(x, axis, [(i, i ^ bit) for i in range(n)])]
    pallas_call x7 -> x8, Pallas kernels: 63.7 us -> 54.8 us  [the longest x2 16.7 us: intra_block(): pl.pallas_call(intra_kernel, grid_spec=pltpu.PrefetchScalarGridSpec(num_s...]
    unnamed x80 -> x76, local copies, waits for them, and re-layouts: 9.63 us -> 4.19 us
    broadcast_in_dim x8 -> x4, local copies, waits for them, and re-layouts: 5.34 us -> 0.28 us  [the longest x3 0.21 us: rows_of(): jnp.repeat(jnp.where(use, jnp.exp(logs), otherwise), head_dim)[:, None]]
    squeeze x4 -> x1, local copies, waits for them, and re-layouts: 6.15 us -> 1.53 us  [layer(): picked[r]]
    gather x1, local copies, waits for them, and re-layouts: 8.49 us -> 12.1 us  [layer(): jnp.take(codebook, jnp.minimum(asked, codes_dev - 1).reshape(-1, slots),...]
    pallas_call x1, Pallas kernels: 11.1 us -> 7.65 us  [block_states(): pl.pallas_call(states_kernel, grid=(nb,), in_specs=[pl.BlockSpec((rows, w...]
  transfers between devices with their start and end apart: 43 -> 37, of which waited for: 15 -> 16; matrix products, arithmetic and copies ran while one was open for 14% -> 12% of each run, Pallas kernels for 27% -> 27%
where the time goes in v2:
time: 259 us; the launch traced here: 258 us
  waiting for transfers between devices  87.5 us (34%)
  Pallas kernels  78.9 us (30%)
  starting transfers between devices  52.6 us (20%)
  local copies, waits for them, and re-layouts  25.9 us (10%)
  other arithmetic  11.3 us (4%)
    ppermute x35, waiting for transfers between devices, flip(): return lax.ppermute(x, axis, [(i, i ^ bit) for i in range(n)])  81.1 us
    ppermute x35, starting transfers between devices, flip(): return lax.ppermute(x, axis, [(i, i ^ bit) for i in range(n)])  43.8 us
    pallas_call x2, Pallas kernels, intra_block(): pl.pallas_call(intra_kernel, grid_spec=pltpu.PrefetchScalarGridSpec(num_s...  16.7 us
    pallas_call x2, Pallas kernels, project(): pl.pallas_call(functools.partial(project_kernel, count=count), grid_spec=...  14 us
    pallas_call x1, Pallas kernels, table(): pl.pallas_call(functools.partial(table_kernel, window=window, codes=block...  12.4 us
    gather x1, local copies, waits for them, and re-layouts, layer(): jnp.take(codebook, jnp.minimum(asked, codes_dev - 1).reshape(-1, slots),...  12.1 us
    pallas_call x2, Pallas kernels, gated_blocks(): pl.pallas_call(gate_kernel, grid_spec=pltpu.PrefetchScalarGridSpec(num_sc...  10.5 us
    pallas_call x2, Pallas kernels, ordered(): pl.pallas_call(order_kernel, grid_spec=pltpu.PrefetchScalarGridSpec(num_s...  7.87 us
  transfers between devices with their start and end apart: 37, of which 16 were waited for; matrix products, arithmetic and copies ran while one was open for 12% of the time, Pallas kernels for 27%

profile of v2, /device:TPU:0, one launch (start us, length us, event | category | flops | bytes accessed | tf_op | source)
XLA Modules:
  0.0 257.7 jit_solution(701135813003732934)
XLA Ops:
  9.0 7.7 %block_states.1 = (bf16[8,512,128]{2,1,0:T(8,128)(2,1)}, f32[8,2048]{1,0:T(8,128)}, f32[8,8,128]{2,1,0:T(8,128)}, f32[512,128]{1,0:T(8,128)}, bf16[512,128]{1,0:T(8,128)(2,1)}) custom-call(bf16[2048,512]{1,0:T(8,128)(2,1)} %x_ref.5, bf16[2048,128]{1,0:T(8,128)(2,1)} %b_ref.5, f32[8,2048]{1,0:T(8,128)} %bitcast.34, f32[8,1]{1,0:T(8,128)} %copy.37.rate_ref), custom_call_target="tpu_custom_call" | custom-call | tf_op jit(solution)/shard_map/block_states/pallas_call | solution.py:94
  24.7 8.4 %intra_block.2 = (f32[4,256,512]{2,1,0:T(8,128)}, bf16[4,256,512]{2,1,0:T(8,128)(2,1)}) custom-call(s32[5]{0:T(128)} %pad_add_fusion.3.order_ref, bf16[2048,512]{1,0:T(8,128)(2,1)} %x_ref.5, bf16[2048,512]{1,0:T(8,128)(2,1)} %gate_ref.3, bf16[2048,128]{1,0:T(8,128)(2,1)} %b_ref.5, bf16[2048,128]{1,0:T(8,128)(2,1)} %c_ref.7, f32[8,2048]{1,0:T(8,128)} %bitcast.35, ...), custom_call_target="tpu_custom_call" | custom-call | tf_op jit(solution)/shard_map/intra_block/pallas_call | solution.py:166
  33.8 19.6 %collective-permute-done.8.refs_7_ = bf16[256,2048]{1,0:T(8,128)(2,1)S(1)} collective-permute-done((bf16[256,2048]{1,0:T(8,128)(2,1)S(1)}, bf16[256,2048]{1,0:T(8,128)(2,1)S(1)}, u32[]{:S(2)}, u32[]{:S(2)}) %collective-permute-start.8) | collective-permute-done | bytes 1048608 | tf_op jit(solution)/shard_map/ppermute | solution.py:19
  56.6 5.3 %gated_blocks.2 = (bf16[256,512]{1,0:T(8,128)(2,1)}, bf16[256,512]{1,0:T(8,128)(2,1)}, bf16[256,512]{1,0:T(8,128)(2,1)}, bf16[256,512]{1,0:T(8,128)(2,1)}) custom-call(s32[5]{0:T(128)} %pad_add_fusion.3.order_ref, f32[4,256,512]{2,1,0:T(8,128)} %get-tuple-element.38.base_ref, bf16[4,256,512]{2,1,0:T(8,128)(2,1)} %get-tuple-element.39.slope_ref, ...), custom_call_target="tpu_custom_call" | custom-call | tf_op jit(solution)/shard_map/gated_blocks/pallas_call | solution.py:213
  61.9 8.4 %intra_block.3 = (f32[4,256,512]{2,1,0:T(8,128)}, bf16[4,256,512]{2,1,0:T(8,128)(2,1)}) custom-call(s32[5]{0:T(128)} %pad_add_fusion.2.order_ref, bf16[2048,512]{1,0:T(8,128)(2,1)} %x_ref.5, bf16[2048,512]{1,0:T(8,128)(2,1)} %gate_ref.3, bf16[2048,128]{1,0:T(8,128)(2,1)} %b_ref.5, bf16[2048,128]{1,0:T(8,128)(2,1)} %c_ref.7, f32[8,2048]{1,0:T(8,128)} %bitcast.36, ...), custom_call_target="tpu_custom_call" | custom-call | tf_op jit(solution)/shard_map/intra_block/pallas_call | solution.py:166
  70.2 5.2 %gated_blocks.3 = (bf16[256,512]{1,0:T(8,128)(2,1)}, bf16[256,512]{1,0:T(8,128)(2,1)}, bf16[256,512]{1,0:T(8,128)(2,1)}, bf16[256,512]{1,0:T(8,128)(2,1)}) custom-call(s32[5]{0:T(128)} %pad_add_fusion.2.order_ref, f32[4,256,512]{2,1,0:T(8,128)} %get-tuple-element.49.base_ref, bf16[4,256,512]{2,1,0:T(8,128)(2,1)} %get-tuple-element.50.slope_ref, ...), custom_call_target="tpu_custom_call" | custom-call | tf_op jit(solution)/shard_map/gated_blocks/pallas_call | solution.py:213
  75.4 4.9 %all-to-all-start = ((s32[8,1,128]{2,1,0:T(1,128)}), s32[8,1,128]{2,1,0:T(1,128)S(1)}, u32[]{:S(2)}, u32[]{:S(2)}) async-start(s32[8,1,128]{2,1,0:T(1,128)} %bitcast.6), calls=%async_computation | async-start | bytes 8192 | tf_op jit(solution)/shard_map/all_to_all | solution.py:563
  80.4 6.4 %all-to-all-done = s32[8,1,128]{2,1,0:T(1,128)S(1)} async-done(((s32[8,1,128]{2,1,0:T(1,128)}), s32[8,1,128]{2,1,0:T(1,128)S(1)}, u32[]{:S(2)}, u32[]{:S(2)}) %all-to-all-start) | async-done | bytes 4128 | tf_op jit(solution)/shard_map/all_to_all | solution.py:563
  92.0 4.3 %collective-permute-done.14.refs_1_ = bf16[256,512]{1,0:T(8,128)(2,1)} collective-permute-done((bf16[256,512]{1,0:T(8,128)(2,1)}, bf16[256,512]{1,0:T(8,128)(2,1)}, u32[]{:S(2)}, u32[]{:S(2)}) %collective-permute-start.14) | collective-permute-done | bytes 262176 | tf_op jit(solution)/shard_map/ppermute | solution.py:19
  99.4 4.7 %collective-permute-done.16.refs_3_ = bf16[256,512]{1,0:T(8,128)(2,1)S(1)} collective-permute-done((bf16[256,512]{1,0:T(8,128)(2,1)}, bf16[256,512]{1,0:T(8,128)(2,1)S(1)}, u32[]{:S(2)}, u32[]{:S(2)}) %collective-permute-start.16) | collective-permute-done | bytes 262176 | tf_op jit(solution)/shard_map/ppermute | solution.py:19
  106.8 6.8 %project.3 = bf16[256,2048]{1,0:T(8,128)(2,1)} custom-call(s32[1]{0:T(128)} %bitcast.2.core_ref, bf16[256,512]{1,0:T(8,128)(2,1)} %get-tuple-element.44.refs_0_, bf16[256,512]{1,0:T(8,128)(2,1)} %collective-permute-done.14.refs_1_, bf16[256,512]{1,0:T(8,128)(2,1)} %collective-permute-done.15.refs_2_, bf16[256,512]{1,0:T(8,128)(2,1)} %copy-done.11, ...), custom_call_target="tpu_custom_call" | custom-call | tf_op jit(solution)/shard_map/project/pallas_call | solution.py:256
  114.2 12.1 %gather_fusion = bf16[2048,512]{1,0:T(8,128)(2,1)S(1)} fusion(bf16[8192,512]{1,0:T(8,128)(2,1)} %param.19, s32[2048]{0:T(1024)S(1)} %fusion.13), kind=kCustom, calls=%fused_computation | custom fusion | bytes 4202496 | tf_op jit(solution)/shard_map/jit(_take)/gather | solution.py:573
  129.8 7.2 %project.2.near_ref = f32[256,2048]{1,0:T(8,128)} custom-call(s32[1]{0:T(128)} %bitcast.2.core_ref, bf16[256,512]{1,0:T(8,128)(2,1)} %get-tuple-element.51.refs_0_, bf16[256,512]{1,0:T(8,128)(2,1)} %collective-permute-done.3.refs_1_, bf16[256,512]{1,0:T(8,128)(2,1)} %collective-permute-done.4.refs_2_, bf16[256,512]{1,0:T(8,128)(2,1)} %collective-permute-done.5.refs_3_, ...), custom_call_target="tpu_custom_call" | custom-call | tf_op jit(solution)/shard_map/project/pallas_call | solution.py:256
  138.5 20.1 %collective-permute-done.17.across_ref = bf16[256,2048]{1,0:T(8,128)(2,1)S(1)} collective-permute-done((bf16[256,2048]{1,0:T(8,128)(2,1)}, bf16[256,2048]{1,0:T(8,128)(2,1)S(1)}, u32[]{:S(2)}, u32[]{:S(2)}) %collective-permute-start.17) | collective-permute-done | bytes 1048608 | tf_op jit(solution)/shard_map/ppermute | solution.py:19
  159.6 3.9 %sent_rows.1 = (bf16[256,2048]{1,0:T(8,128)(2,1)}, bf16[128,512]{1,0:T(8,128)(2,1)}, bf16[128,512]{1,0:T(8,128)(2,1)}, bf16[128,512]{1,0:T(8,128)(2,1)}, bf16[12...) custom-call(s32[1]{0:T(128)} %bitcast.chan_ref, ...), custom_call_target="tpu_custom_call" | custom-call | tf_op jit(solution)/shard_map/sent_rows/pallas_call | solution.py:287
  163.5 3.9 %all-to-all-start.1 = ((bf16[8,128,512]{2,1,0:T(8,128)(2,1)}), bf16[8,128,512]{2,1,0:T(8,128)(2,1)S(1)}, u32[]{:S(2)}, u32[]{:S(2)}) async-start(bf16[8,128,512]{2,1,0:T(8,128)(2,1)} %get-tuple-element.60.picked_ref), calls=%async_computation.1 | async-start | bytes 2097152 | tf_op jit(solution)/shard_map/all_to_all | solution.py:596
  175.0 5.3 %collective-permute-done.18.refs_1_ = bf16[128,512]{1,0:T(8,128)(2,1)S(1)} collective-permute-done((bf16[128,512]{1,0:T(8,128)(2,1)S(1)}, bf16[128,512]{1,0:T(8,128)(2,1)S(1)}, u32[]{:S(2)}, u32[]{:S(2)}) %collective-permute-start.18) | collective-permute-done | bytes 131104 | tf_op jit(solution)/shard_map/ppermute | solution.py:19
  184.0 4.3 %collective-permute-done.19.refs_2_ = bf16[128,512]{1,0:T(8,128)(2,1)S(1)} collective-permute-done((bf16[128,512]{1,0:T(8,128)(2,1)S(1)}, bf16[128,512]{1,0:T(8,128)(2,1)S(1)}, u32[]{:S(2)}, u32[]{:S(2)}) %collective-permute-start.19) | collective-permute-done | bytes 131104 | tf_op jit(solution)/shard_map/ppermute | solution.py:19
  188.3 4.6 %collective-permute-start.24 = (bf16[128,512]{1,0:T(8,128)(2,1)S(1)}, bf16[128,512]{1,0:T(8,128)(2,1)S(1)}, u32[]{:S(2)}, u32[]{:S(2)}) collective-permute-start(bf16[128,512]{1,0:T(8,128)(2,1)S(1)} %copy-done.30), channel_id=1, source_target_pairs={{0,7},{1,6},{2,5},{3,4},{4,3},{5,2},{6,1},{7,0},{8,15},{9,14},{10,... | collective-permute-start | bytes 393224 | tf_op jit(solution)/shard_map/ppermute | solution.py:19
  195.2 13.1 %collective-permute-done.21.refs_4_ = bf16[128,512]{1,0:T(8,128)(2,1)S(1)} collective-permute-done((bf16[128,512]{1,0:T(8,128)(2,1)S(1)}, bf16[128,512]{1,0:T(8,128)(2,1)S(1)}, u32[]{:S(2)}, u32[]{:S(2)}) %collective-permute-start.21) | collective-permute-done | bytes 131104 | tf_op jit(solution)/shard_map/ppermute | solution.py:19
  221.3 3.9 %ordered.2.refs_0_ = bf16[1024,512]{1,0:T(8,128)(2,1)} custom-call(s32[1]{0:T(128)} %bitcast.chan_ref, s32[8,1,128]{2,1,0:T(1,128)} %get-tuple-element.76.place_ref, bf16[8,128,512]{2,1,0:T(8,128)(2,1)} %get-tuple-element.60.picked_ref, bf16[128,512]{1,0:T(8,128)(2,1)} %get-tuple-element.59.refs_0_, bf16[128,512]{1,0:T(8,128)(2,1)} %copy-done.13, ...), custom_call_target="tpu_custom_call" | custom-call | tf_op jit(solution)/shard_map/ordered/pallas_call | solution.py:379
  230.5 3.9 %ordered.3.refs_1_ = bf16[1024,512]{1,0:T(8,128)(2,1)} custom-call(s32[1]{0:T(128)} %bitcast.chan_ref, s32[8,1,128]{2,1,0:T(1,128)} %get-tuple-element.75.place_ref, bf16[8,128,512]{2,1,0:T(8,128)(2,1)} %get-tuple-element.71.picked_ref, bf16[128,512]{1,0:T(8,128)(2,1)} %copy-done.19, bf16[128,512]{1,0:T(8,128)(2,1)} %copy-done.21, ...), custom_call_target="tpu_custom_call" | custom-call | tf_op jit(solution)/shard_map/ordered/pallas_call | solution.py:379
  238.3 12.4 %table.1 = f32[8192,512]{1,0:T(8,128)} custom-call(s32[4,33]{1,0:T(4,128)} %copy.39.bounds_ref, s32[4,1280]{1,0:T(4,128)} %pad.4.codes_ref, bf16[1024,512]{1,0:T(8,128)(2,1)} %ordered.2.refs_0_, bf16[1024,512]{1,0:T(8,128)(2,1)} %ordered.3.refs_1_, bf16[1024,512]{1,0:T(8,128)(2,1)} %copy-done.9, bf16[1024,512]{1,0:T(8,128)(2,1)} %copy-done.10), custom_call_target="tpu_custom_call" | custom-call | tf_op jit(solution)/shard_map/table/pallas_call | solution.py:446
  251.7 6.0 %latent_grads.1 = f32[256,2048]{1,0:T(8,128)} custom-call(s32[256,4]{1,0:T(8,128)} %bitcast.33, bf16[256,2048]{1,0:T(8,128)(2,1)} %get-tuple-element.34.latent_ref, bf16[256,2048]{1,0:T(8,128)(2,1)} %up_ref.1, bf16[1024,512]{1,0:T(8,128)(2,1)} %bitcast.31), custom_call_target="tpu_custom_call" | custom-call | tf_op jit(solution)/shard_map/latent_grads/pallas_call | solution.py:338
  (182 shorter events, 74.6 us)
Async XLA Ops:
  3.5 30.3 %collective-permute-start.7 = (bf16[256,2048]{1,0:T(8,128)(2,1)S(1)}, bf16[256,2048]{1,0:T(8,128)(2,1)S(1)}, u32[]{:S(2)}, u32[]{:S(2)}) collective-permute-start(bf16[256,2048]{1,0:T(8,128)(2,1)S(1)} %get-tuple-element.74.refs_4_), channel_id=1, source_target_pairs={{0,2},{1,3},{2,0},{3,1},{4,6},{5,7},{6,4},{7,5},{8,10},{9,11},{10,... | collective-permute-start | bytes 3145736 | tf_op jit(solution)/shard_map/ppermute | solution.py:19
  6.5 46.8 %collective-permute-start.8 = (bf16[256,2048]{1,0:T(8,128)(2,1)S(1)}, bf16[256,2048]{1,0:T(8,128)(2,1)S(1)}, u32[]{:S(2)}, u32[]{:S(2)}) collective-permute-start(bf16[256,2048]{1,0:T(8,128)(2,1)S(1)} %get-tuple-element.74.refs_4_), channel_id=1, source_target_pairs={{0,3},{1,2},{2,1},{3,0},{4,7},{5,6},{6,5},{7,4},{8,11},{9,10},{10,... | collective-permute-start | bytes 3145736 | tf_op jit(solution)/shard_map/ppermute | solution.py:19
  7.9 46.9 %collective-permute-start.6 = (bf16[256,2048]{1,0:T(8,128)(2,1)S(1)}, bf16[256,2048]{1,0:T(8,128)(2,1)}, u32[]{:S(2)}, u32[]{:S(2)}) collective-permute-start(bf16[256,2048]{1,0:T(8,128)(2,1)S(1)} %get-tuple-element.74.refs_4_), channel_id=1, source_target_pairs={{0,1},{1,0},{2,3},{3,2},{4,5},{5,4},{6,7},{7,6},{8,9},{9,8},{10,11... | collective-permute-start | bytes 3145736 | tf_op jit(solution)/shard_map/ppermute | solution.py:19
  21.3 33.6 %collective-permute-start.2 = (bf16[512,128]{1,0:T(8,128)(2,1)}, bf16[512,128]{1,0:T(8,128)(2,1)}, u32[]{:S(2)}, u32[]{:S(2)}) collective-permute-start(bf16[512,128]{1,0:T(8,128)(2,1)} %fusion.5), channel_id=1, source_target_pairs={{0,16},{8,24},{16,0},{24,8},{1,17},{9,25},{17,1},{25,9},{2,18},{10... | collective-permute-start | bytes 393224 | tf_op jit(solution)/shard_map/ppermute | solution.py:19
  33.8 70.9 %collective-permute-start.10 = (bf16[256,2048]{1,0:T(8,128)(2,1)S(1)}, bf16[256,2048]{1,0:T(8,128)(2,1)}, u32[]{:S(2)}, u32[]{:S(2)}) collective-permute-start(bf16[256,2048]{1,0:T(8,128)(2,1)S(1)} %collective-permute-done.7.refs_6_), channel_id=1, source_target_pairs={{0,8},{8,0},{16,24},{24,16},{1,9},{9,1},{17,25},{25,17},{2,10},{10... | collective-permute-start | bytes 3145736 | tf_op jit(solution)/shard_map/ppermute | solution.py:19
  53.4 52.4 %collective-permute-start.11 = (bf16[256,2048]{1,0:T(8,128)(2,1)S(1)}, bf16[256,2048]{1,0:T(8,128)(2,1)}, u32[]{:S(2)}, u32[]{:S(2)}) collective-permute-start(bf16[256,2048]{1,0:T(8,128)(2,1)S(1)} %collective-permute-done.8.refs_7_), channel_id=1, source_target_pairs={{0,8},{8,0},{16,24},{24,16},{1,9},{9,1},{17,25},{25,17},{2,10},{10... | collective-permute-start | bytes 3145736 | tf_op jit(solution)/shard_map/ppermute | solution.py:19
  54.8 50.9 %collective-permute-start.9 = (bf16[256,2048]{1,0:T(8,128)(2,1)}, bf16[256,2048]{1,0:T(8,128)(2,1)S(1)}, u32[]{:S(2)}, u32[]{:S(2)}) collective-permute-start(bf16[256,2048]{1,0:T(8,128)(2,1)} %collective-permute-done.6.refs_5_), channel_id=1, source_target_pairs={{0,8},{8,0},{16,24},{24,16},{1,9},{9,1},{17,25},{25,17},{2,10},{10... | collective-permute-start | bytes 3145736 | tf_op jit(solution)/shard_map/ppermute | solution.py:19
  75.4 11.3 %all-to-all-start = ((s32[8,1,128]{2,1,0:T(1,128)}), s32[8,1,128]{2,1,0:T(1,128)S(1)}, u32[]{:S(2)}, u32[]{:S(2)}) async-start(s32[8,1,128]{2,1,0:T(1,128)} %bitcast.6), calls=%async_computation | async-start | bytes 8192 | tf_op jit(solution)/shard_map/all_to_all | solution.py:563
  97.9 31.9 %collective-permute-start.3 = (bf16[256,512]{1,0:T(8,128)(2,1)}, bf16[256,512]{1,0:T(8,128)(2,1)}, u32[]{:S(2)}, u32[]{:S(2)}) collective-permute-start(bf16[256,512]{1,0:T(8,128)(2,1)} %get-tuple-element.52), channel_id=1, source_target_pairs={{0,1},{1,0},{2,3},{3,2},{4,5},{5,4},{6,7},{7,6},{8,9},{9,8},{10,11... | collective-permute-start | bytes 786440 | tf_op jit(solution)/shard_map/ppermute | solution.py:19
  104.1 25.7 %collective-permute-start.4 = (bf16[256,512]{1,0:T(8,128)(2,1)}, bf16[256,512]{1,0:T(8,128)(2,1)}, u32[]{:S(2)}, u32[]{:S(2)}) collective-permute-start(bf16[256,512]{1,0:T(8,128)(2,1)} %get-tuple-element.53), channel_id=1, source_target_pairs={{0,2},{1,3},{2,0},{3,1},{4,6},{5,7},{6,4},{7,5},{8,10},{9,11},{10,... | collective-permute-start | bytes 786440 | tf_op jit(solution)/shard_map/ppermute | solution.py:19
  104.6 25.2 %collective-permute-start.5 = (bf16[256,512]{1,0:T(8,128)(2,1)}, bf16[256,512]{1,0:T(8,128)(2,1)}, u32[]{:S(2)}, u32[]{:S(2)}) collective-permute-start(bf16[256,512]{1,0:T(8,128)(2,1)} %get-tuple-element.54), channel_id=1, source_target_pairs={{0,3},{1,2},{2,1},{3,0},{4,7},{5,6},{6,5},{7,4},{8,11},{9,10},{10,... | collective-permute-start | bytes 786440 | tf_op jit(solution)/shard_map/ppermute | solution.py:19
  113.6 45.0 %collective-permute-start.17 = (bf16[256,2048]{1,0:T(8,128)(2,1)}, bf16[256,2048]{1,0:T(8,128)(2,1)S(1)}, u32[]{:S(2)}, u32[]{:S(2)}) collective-permute-start(bf16[256,2048]{1,0:T(8,128)(2,1)} %project.3), channel_id=1, source_target_pairs={{0,4},{1,5},{2,6},{3,7},{4,0},{5,1},{6,2},{7,3},{8,12},{9,13},{10,... | collective-permute-start | bytes 3145736 | tf_op jit(solution)/shard_map/ppermute | solution.py:19
  114.2 13.6 %collective-permute-start.13 = (s32[2,1024]{1,0:T(2,128)S(1)}, s32[2,1024]{1,0:T(2,128)S(1)}, u32[]{:S(2)}, u32[]{:S(2)}) collective-permute-start(s32[2,1024]{1,0:T(2,128)S(1)} %select_reduce_fusion), channel_id=1, source_target_pairs={{0,8},{8,0},{16,24},{24,16},{1,9},{9,1},{17,25},{25,17},{2,10},{10... | collective-permute-start | bytes 24584 | tf_op jit(solution)/shard_map/ppermute | solution.py:19
  163.5 87.2 %all-to-all-start.1 = ((bf16[8,128,512]{2,1,0:T(8,128)(2,1)}), bf16[8,128,512]{2,1,0:T(8,128)(2,1)S(1)}, u32[]{:S(2)}, u32[]{:S(2)}) async-start(bf16[8,128,512]{2,1,0:T(8,128)(2,1)} %get-tuple-element.60.picked_ref), calls=%async_computation.1 | async-start | bytes 2097152 | tf_op jit(solution)/shard_map/all_to_all | solution.py:596
  167.4 12.8 %collective-permute-start.18 = (bf16[128,512]{1,0:T(8,128)(2,1)S(1)}, bf16[128,512]{1,0:T(8,128)(2,1)S(1)}, u32[]{:S(2)}, u32[]{:S(2)}) collective-permute-start(bf16[128,512]{1,0:T(8,128)(2,1)S(1)} %copy-done.36), channel_id=1, source_target_pairs={{0,1},{1,0},{2,3},{3,2},{4,5},{5,4},{6,7},{7,6},{8,9},{9,8},{10,11... | collective-permute-start | bytes 393224 | tf_op jit(solution)/shard_map/ppermute | solution.py:19
  169.1 19.2 %collective-permute-start.19 = (bf16[128,512]{1,0:T(8,128)(2,1)S(1)}, bf16[128,512]{1,0:T(8,128)(2,1)S(1)}, u32[]{:S(2)}, u32[]{:S(2)}) collective-permute-start(bf16[128,512]{1,0:T(8,128)(2,1)S(1)} %copy-done.35), channel_id=1, source_target_pairs={{0,2},{1,3},{2,0},{3,1},{4,6},{5,7},{6,4},{7,5},{8,10},{9,11},{10,... | collective-permute-start | bytes 393224 | tf_op jit(solution)/shard_map/ppermute | solution.py:19
  170.6 22.3 %collective-permute-start.20 = (bf16[128,512]{1,0:T(8,128)(2,1)S(1)}, bf16[128,512]{1,0:T(8,128)(2,1)S(1)}, u32[]{:S(2)}, u32[]{:S(2)}) collective-permute-start(bf16[128,512]{1,0:T(8,128)(2,1)S(1)} %copy-done.34), channel_id=1, source_target_pairs={{0,3},{1,2},{2,1},{3,0},{4,7},{5,6},{6,5},{7,4},{8,11},{9,10},{10,... | collective-permute-start | bytes 393224 | tf_op jit(solution)/shard_map/ppermute | solution.py:19
  171.0 37.3 %collective-permute-start.21 = (bf16[128,512]{1,0:T(8,128)(2,1)S(1)}, bf16[128,512]{1,0:T(8,128)(2,1)S(1)}, u32[]{:S(2)}, u32[]{:S(2)}) collective-permute-start(bf16[128,512]{1,0:T(8,128)(2,1)S(1)} %copy-done.33), channel_id=1, source_target_pairs={{0,4},{1,5},{2,6},{3,7},{4,0},{5,1},{6,2},{7,3},{8,12},{9,13},{10,... | collective-permute-start | bytes 393224 | tf_op jit(solution)/shard_map/ppermute | solution.py:19
  173.6 37.5 %collective-permute-start.22 = (bf16[128,512]{1,0:T(8,128)(2,1)S(1)}, bf16[128,512]{1,0:T(8,128)(2,1)S(1)}, u32[]{:S(2)}, u32[]{:S(2)}) collective-permute-start(bf16[128,512]{1,0:T(8,128)(2,1)S(1)} %copy-done.32), channel_id=1, source_target_pairs={{0,5},{1,4},{2,7},{3,6},{4,1},{5,0},{6,3},{7,2},{8,13},{9,12},{10,... | collective-permute-start | bytes 393224 | tf_op jit(solution)/shard_map/ppermute | solution.py:19
  180.3 34.0 %collective-permute-start.23 = (bf16[128,512]{1,0:T(8,128)(2,1)S(1)}, bf16[128,512]{1,0:T(8,128)(2,1)S(1)}, u32[]{:S(2)}, u32[]{:S(2)}) collective-permute-start(bf16[128,512]{1,0:T(8,128)(2,1)S(1)} %copy-done.31), channel_id=1, source_target_pairs={{0,6},{1,7},{2,4},{3,5},{4,2},{5,3},{6,0},{7,1},{8,14},{9,15},{10,... | collective-permute-start | bytes 393224 | tf_op jit(solution)/shard_map/ppermute | solution.py:19
  188.3 26.0 %collective-permute-start.24 = (bf16[128,512]{1,0:T(8,128)(2,1)S(1)}, bf16[128,512]{1,0:T(8,128)(2,1)S(1)}, u32[]{:S(2)}, u32[]{:S(2)}) collective-permute-start(bf16[128,512]{1,0:T(8,128)(2,1)S(1)} %copy-done.30), channel_id=1, source_target_pairs={{0,7},{1,6},{2,5},{3,4},{4,3},{5,2},{6,1},{7,0},{8,15},{9,14},{10,... | collective-permute-start | bytes 393224 | tf_op jit(solution)/shard_map/ppermute | solution.py:19
  192.9 23.4 %collective-permute-start.25 = (bf16[128,512]{1,0:T(8,128)(2,1)S(1)}, bf16[128,512]{1,0:T(8,128)(2,1)S(1)}, u32[]{:S(2)}, u32[]{:S(2)}) collective-permute-start(bf16[128,512]{1,0:T(8,128)(2,1)S(1)} %copy-done.12), channel_id=1, source_target_pairs={{0,16},{8,24},{16,0},{24,8},{1,17},{9,25},{17,1},{25,9},{2,18},{10... | collective-permute-start | bytes 393224 | tf_op jit(solution)/shard_map/ppermute | solution.py:19
  216.4 12.6 %collective-permute-start.31 = (bf16[128,512]{1,0:T(8,128)(2,1)S(1)}, bf16[128,512]{1,0:T(8,128)(2,1)S(1)}, u32[]{:S(2)}, u32[]{:S(2)}) collective-permute-start(bf16[128,512]{1,0:T(8,128)(2,1)S(1)} %collective-permute-done.23.refs_6_), channel_id=1, source_target_pairs={{0,16},{8,24},{16,0},{24,8},{1,17},{9,25},{17,1},{25,9},{2,18},{10... | collective-permute-start | bytes 393224 | tf_op jit(solution)/shard_map/ppermute | solution.py:19
  218.6 11.9 %collective-permute-start.32 = (bf16[128,512]{1,0:T(8,128)(2,1)S(1)}, bf16[128,512]{1,0:T(8,128)(2,1)}, u32[]{:S(2)}, u32[]{:S(2)}) collective-permute-start(bf16[128,512]{1,0:T(8,128)(2,1)S(1)} %collective-permute-done.24.refs_7_), channel_id=1, source_target_pairs={{0,16},{8,24},{16,0},{24,8},{1,17},{9,25},{17,1},{25,9},{2,18},{10... | collective-permute-start | bytes 393224 | tf_op jit(solution)/shard_map/ppermute | solution.py:19
  (50 other events, 544.9 us)

commit v3 on v2

--- a/solution.py
+++ b/solution.py
@@ -10,6 +10,8 @@
 
 COMMIT = 0.25
 CODE_BLOCK = 256
+TERM_ROWS = 16
+GRANT = 16 * 1024 * 1024
 F32 = jnp.float32
 BF16 = jnp.bfloat16
 
@@ -30,8 +32,14 @@
     )
 
 
+def three_terms(value):
+    one = value.astype(BF16).astype(F32)
+    two = (value - one).astype(BF16).astype(F32)
+    return one, two, value - one - two
+
+
 def states_kernel(
-    x_ref, b_ref, dt_ref, rate_ref, starts_ref, cums_ref, before_ref, final_ref, sent_ref,
+    x_ref, b_ref, dt_ref, rate_ref, starts_ref, cums_ref, before_ref, sent_ref,
     state, seen, upper,
 ):
     step = pl.program_id(0)
@@ -51,10 +59,12 @@
         ).astype(BF16)
 
     dt = dt_ref[...]
-    logs = -dt * rate_ref[...]
-    one = logs.astype(BF16).astype(F32)
-    two = (logs - one).astype(BF16).astype(F32)
-    three = logs - one - two
+    same = lax.broadcasted_iota(jnp.int32, (heads, heads), 0) == lax.broadcasted_iota(
+        jnp.int32, (heads, heads), 1
+    )
+    rate = jnp.sum(jnp.where(same, rate_ref[...], 0.0), axis=1, keepdims=True)
+    logs = -dt * rate
+    one, two, three = three_terms(logs)
     terms = jnp.concatenate([one, two, three, jnp.zeros_like(one)], axis=0).astype(BF16)
     sums = jnp.dot(terms, upper[...], preferred_element_type=F32)
     cums = sums[:heads] + sums[heads : 2 * heads] + sums[2 * heads : 3 * heads]
@@ -82,8 +92,11 @@
 
     @pl.when(step == pl.num_programs(0) - 1)
     def _():
-        final_ref[...] = state[...]
-        sent_ref[...] = state[...].astype(BF16)
+        sent_ref[:width, :] = state[...].astype(BF16)
+        for n, term in enumerate(three_terms(seen[...])):
+            at = width + n * TERM_ROWS
+            fill = jnp.zeros((TERM_ROWS - heads, term.shape[1]), F32)
+            sent_ref[at : at + TERM_ROWS, :] = jnp.concatenate([term, fill], axis=0).astype(BF16)
 
 
 def block_states(frames_in, in_keys, step_t, rate, rows):
@@ -98,21 +111,19 @@
             pl.BlockSpec((rows, width), lambda i: (i, 0)),
             pl.BlockSpec((rows, nstate), lambda i: (i, 0)),
             pl.BlockSpec((heads, rows), lambda i: (0, i)),
-            pl.BlockSpec((heads, 1), lambda i: (0, 0)),
+            pl.BlockSpec((1, heads), lambda i: (0, 0)),
         ],
         out_specs=[
             pl.BlockSpec((1, width, nstate), lambda i: (i, 0, 0)),
             pl.BlockSpec((heads, rows), lambda i: (0, i)),
             pl.BlockSpec((1, heads, nstate), lambda i: (i, 0, 0)),
-            pl.BlockSpec((width, nstate), lambda i: (0, 0)),
-            pl.BlockSpec((width, nstate), lambda i: (0, 0)),
+            pl.BlockSpec((width + 3 * TERM_ROWS, nstate), lambda i: (0, 0)),
         ],
         out_shape=[
             jax.ShapeDtypeStruct((nb, width, nstate), BF16),
             jax.ShapeDtypeStruct((heads, frames), F32),
             jax.ShapeDtypeStruct((nb, heads, nstate), F32),
-            jax.ShapeDtypeStruct((width, nstate), F32),
-            jax.ShapeDtypeStruct((width, nstate), BF16),
+            jax.ShapeDtypeStruct((width + 3 * TERM_ROWS, nstate), BF16),
         ],
         scratch_shapes=[
             pltpu.VMEM((width, nstate), F32),
@@ -120,6 +131,7 @@
             pltpu.VMEM((rows, rows), BF16),
         ],
         name="block_states",
+        compiler_params=pltpu.CompilerParams(vmem_limit_bytes=GRANT),
     )(frames_in, in_keys, step_t, rate)
 
 
@@ -133,6 +145,7 @@
     cums_t = cums_ref[...]
     cums = cums_t.T
     dt = dt_ref[...]
+    skip = per_head(skip_ref[...], heads, head_dim)
     for t in range(rows // tile):
         rs = slice(t * tile, (t + 1) * tile)
         n = (t + 1) * tile
@@ -154,7 +167,7 @@
             )
         gate = gate_ref[rs, :].astype(F32)
         gate = gate / (1.0 + jnp.exp(-gate))
-        mixed = jnp.concatenate(parts, axis=1) + x_ref[rs, :].astype(F32) * skip_ref[...]
+        mixed = jnp.concatenate(parts, axis=1) + x_ref[rs, :].astype(F32) * skip
         base_ref[0, rs, :] = mixed * gate
         slope_ref[0, rs, :] = (gate * per_head(jnp.exp(cums[rs, :]), heads, head_dim)).astype(BF16)
 
@@ -169,13 +182,13 @@
             num_scalar_prefetch=1,
             grid=(count,),
             in_specs=[
-                pl.BlockSpec((rows, width), lambda i, o: (o[i], 0)),
-                pl.BlockSpec((rows, width), lambda i, o: (o[i], 0)),
-                pl.BlockSpec((rows, nstate), lambda i, o: (o[i], 0)),
-                pl.BlockSpec((rows, nstate), lambda i, o: (o[i], 0)),
-                pl.BlockSpec((heads, rows), lambda i, o: (0, o[i])),
-                pl.BlockSpec((heads, rows), lambda i, o: (0, o[i])),
-                pl.BlockSpec((1, width), lambda i, o: (0, 0)),
+                pl.BlockSpec((rows, width), lambda i, o: (o[0] ^ i, 0)),
+                pl.BlockSpec((rows, width), lambda i, o: (o[0] ^ i, 0)),
+                pl.BlockSpec((rows, nstate), lambda i, o: (o[0] ^ i, 0)),
+                pl.BlockSpec((rows, nstate), lambda i, o: (o[0] ^ i, 0)),
+                pl.BlockSpec((heads, rows), lambda i, o: (0, o[0] ^ i)),
+                pl.BlockSpec((heads, rows), lambda i, o: (0, o[0] ^ i)),
+                pl.BlockSpec((1, heads), lambda i, o: (0, 0)),
             ],
             out_specs=[pl.BlockSpec((1, rows, width), lambda i, o: (i, 0, 0))] * 2,
         ),
@@ -184,18 +197,49 @@
             jax.ShapeDtypeStruct((count, rows, width), BF16),
         ],
         name="intra_block",
+        compiler_params=pltpu.CompilerParams(vmem_limit_bytes=GRANT),
     )(order, frames_in, gate_in, in_keys, out_keys, step_t, cums, skip)
 
 
-def gate_kernel(order_ref, base_ref, slope_ref, c_ref, starts_ref, before_ref, incoming_ref, *outs):
+def gate_kernel(
+    order_ref, base_ref, slope_ref, c_ref, starts_ref, before_ref, *refs, peers
+):
+    states = refs[:peers]
+    outs = refs[peers:-1]
+    incoming = refs[-1]
     width = base_ref.shape[2]
     heads = before_ref.shape[1]
     head_dim = width // heads
+    runs = [slice(h * head_dim, (h + 1) * head_dim) for h in range(heads)]
+
+    @pl.when(pl.program_id(0) == 0)
+    def _():
+        seq = order_ref[1]
+        logs = [
+            sum(
+                s[width + n * TERM_ROWS : width + (n + 1) * TERM_ROWS, :].astype(F32)
+                for n in range(3)
+            )
+            for s in states
+        ]
+        factors = []
+        for j in range(1, peers + 1):
+            log = jnp.zeros_like(logs[0])
+            for i in range(1, peers + 1):
+                between = ((seq ^ j) < (seq ^ i)) & ((seq ^ i) < seq)
+                log = log + jnp.where(between, logs[i - 1], 0.0)
+            factors.append(jnp.where((seq ^ j) < seq, jnp.exp(log), 0.0))
+        for h, rs in enumerate(runs):
+            total = jnp.zeros((head_dim, incoming.shape[1]), F32)
+            for factor, state in zip(factors, states):
+                total = total + factor[h : h + 1, :] * state[rs, :].astype(F32)
+            incoming[rs, :] = total
+
     carry = jnp.exp(before_ref[0])
-    parts = []
-    for h in range(heads):
-        rs = slice(h * head_dim, (h + 1) * head_dim)
-        parts.append(starts_ref[0, rs, :].astype(F32) + incoming_ref[rs, :] * carry[h : h + 1, :])
+    parts = [
+        starts_ref[0, rs, :].astype(F32) + incoming[rs, :] * carry[h : h + 1, :]
+        for h, rs in enumerate(runs)
+    ]
     start = jnp.concatenate(parts, axis=0).astype(BF16)
     inter = dot_nt(c_ref[...], start)
     gated = (base_ref[0] + inter * slope_ref[0].astype(F32)).astype(BF16)
@@ -206,70 +250,110 @@
             out_ref[...] = gated
 
 
-def gated_blocks(order, base, slope, out_keys, starts, before, incoming):
+def gated_blocks(order, base, slope, out_keys, starts, before, states):
     count, rows, width = base.shape
     nstate = out_keys.shape[1]
     heads = before.shape[1]
     return pl.pallas_call(
-        gate_kernel,
+        functools.partial(gate_kernel, peers=len(states)),
         grid_spec=pltpu.PrefetchScalarGridSpec(
             num_scalar_prefetch=1,
             grid=(count,),
             in_specs=[
                 pl.BlockSpec((1, rows, width), lambda i, o: (i, 0, 0)),
                 pl.BlockSpec((1, rows, width), lambda i, o: (i, 0, 0)),
-                pl.BlockSpec((rows, nstate), lambda i, o: (o[i], 0)),
-                pl.BlockSpec((1, width, nstate), lambda i, o: (o[i], 0, 0)),
-                pl.BlockSpec((1, heads, nstate), lambda i, o: (o[i], 0, 0)),
-                pl.BlockSpec((width, nstate), lambda i, o: (0, 0)),
-            ],
+                pl.BlockSpec((rows, nstate), lambda i, o: (o[0] ^ i, 0)),
+                pl.BlockSpec((1, width, nstate), lambda i, o: (o[0] ^ i, 0, 0)),
+                pl.BlockSpec((1, heads, nstate), lambda i, o: (o[0] ^ i, 0, 0)),
+            ]
+            + [pl.BlockSpec(s.shape, lambda i, o: (0, 0)) for s in states],
             out_specs=[pl.BlockSpec((rows, width), lambda i, o: (0, 0))] * count,
+            scratch_shapes=[pltpu.VMEM((width, nstate), F32)],
         ),
         out_shape=[jax.ShapeDtypeStruct((rows, width), BF16)] * count,
         name="gated_blocks",
-    )(order, base, slope, out_keys, starts, before, incoming)
-
-
-def project_kernel(core_ref, *refs, count):
+        compiler_params=pltpu.CompilerParams(vmem_limit_bytes=GRANT),
+    )(order, base, slope, out_keys, starts, before, *states)
+
+
+def project_kernel(place_ref, *refs, count, shares):
     gs = refs[:count]
-    firsts = refs[count : 2 * count]
-    seconds = refs[2 * count : 3 * count]
-    out_ref = refs[-1]
-    half = firsts[0].shape[0]
-    mine = pl.multiple_of(core_ref[0] * half, half)
-    other = pl.multiple_of((1 - core_ref[0]) * half, half)
+    ws = list(refs[count : count + 2 * sum(shares)])
+    outs = refs[count + 2 * sum(shares) :]
+    half = gs[0].shape[1] // 2
     acc = None
-    for g, a, b in zip(gs, firsts, seconds):
-        part = jnp.dot(g[:, pl.ds(mine, half)], a[...], preferred_element_type=F32)
-        part = part + jnp.dot(g[:, pl.ds(other, half)], b[...], preferred_element_type=F32)
-        acc = part if acc is None else acc + part
-    out_ref[...] = acc.astype(out_ref.dtype)
-
-
-def project(core, gs, firsts, seconds, dtype):
+    for side in range(2):
+        start = (place_ref[0] ^ side) * half
+        for g, share in zip(gs, shares):
+            pieces = [ws.pop(0) for _ in range(share)]
+            width = half // share
+            values = [
+                g[:, pl.ds(pl.multiple_of(start + (place_ref[1] * (share - 1) ^ n) * width, width), width)]
+                for n in range(share)
+            ]
+            part = jnp.dot(
+                values[0] if share == 1 else jnp.concatenate(values, axis=1),
+                pieces[0][...]
+                if share == 1
+                else jnp.concatenate([piece[...] for piece in pieces], axis=0),
+                preferred_element_type=F32,
+            )
+            acc = part if acc is None else acc + part
+    if len(outs) == 1:
+        outs[0][...] = acc.astype(outs[0].dtype)
+    else:
+        per = pl.num_programs(0) // len(outs)
+        for n, out_ref in enumerate(outs):
+
+            @pl.when(pl.program_id(0) // per == n)
+            def _():
+                out_ref[...] = acc.astype(out_ref.dtype)
+
+
+def project(place, gs, weight, firsts, seconds, dtype, pieces):
     count = len(gs)
     rows, width = gs[0].shape
-    half, cols = firsts[0].shape
-    tile = min(cols, 512)
+    half, cols = width // 2, weight.shape[1]
+    tile = min(cols // pieces, 512)
+    per = cols // tile // pieces
+
+    def piece(n):
+        return pl.BlockSpec((rows, tile), lambda j, c: (0, jnp.clip(j - n * per, 0, per - 1)))
+
+    def specs(parts):
+        return [pl.BlockSpec((w.shape[0], tile), lambda j, c: (0, j)) for ws in parts for w in ws]
+
     in_specs = [pl.BlockSpec((rows, width), lambda j, c: (0, 0))] * count
-    in_specs += [pl.BlockSpec((half, tile), lambda j, c: (0, j))] * (2 * count)
+    in_specs += [pl.BlockSpec((half, tile), lambda j, c: (c[0], j))] + specs(firsts)
+    in_specs += [pl.BlockSpec((half, tile), lambda j, c: (1 - c[0], j))] + specs(seconds)
     return pl.pallas_call(
-        functools.partial(project_kernel, count=count),
+        functools.partial(
+            project_kernel, count=count, shares=[1] + [len(ws) for ws in firsts]
+        ),
         grid_spec=pltpu.PrefetchScalarGridSpec(
             num_scalar_prefetch=1,
             grid=(cols // tile,),
             in_specs=in_specs,
-            out_specs=pl.BlockSpec((rows, tile), lambda j, c: (0, j)),
+            out_specs=[piece(n) for n in range(pieces)],
         ),
-        out_shape=jax.ShapeDtypeStruct((rows, cols), dtype),
+        out_shape=[jax.ShapeDtypeStruct((rows, cols // pieces), dtype)] * pieces,
         name="project",
-    )(core, *gs, *firsts, *seconds)
-
-
-def send_kernel(chan_ref, pos_ref, near_ref, across_ref, latent_ref, *outs):
+        compiler_params=pltpu.CompilerParams(vmem_limit_bytes=GRANT),
+    )(
+        place,
+        *gs,
+        weight,
+        *[w for ws in firsts for w in ws],
+        weight,
+        *[w for ws in seconds for w in ws],
+    )
+
+
+def send_kernel(chan_ref, pos_ref, near_ref, across_ref, later_ref, latent_ref, *outs):
     slots, dim = outs[0].shape
     groups, rows = pos_ref.shape
-    latent = (near_ref[...] + across_ref[...].astype(F32)).astype(BF16)
+    across = jnp.concatenate([across_ref[...], later_ref[...]], axis=1).astype(F32)
+    latent = (near_ref[...] + across).astype(BF16)
     latent_ref[...] = latent
     slot = lax.broadcasted_iota(jnp.int32, (slots, rows), 0)
     for k, out_ref in enumerate(outs):
@@ -292,7 +376,8 @@
             in_specs=[
                 pl.BlockSpec(pos.shape, lambda i, c: (0, 0)),
                 pl.BlockSpec(near.shape, lambda i, c: (0, 0)),
-                pl.BlockSpec(across.shape, lambda i, c: (0, 0)),
+                pl.BlockSpec(across[0].shape, lambda i, c: (0, 0)),
+                pl.BlockSpec(across[1].shape, lambda i, c: (0, 0)),
             ],
             out_specs=[pl.BlockSpec((rows, cols), lambda i, c: (0, 0))]
             + [pl.BlockSpec((slots, dim), lambda i, c: (0, 0))] * count,
@@ -300,7 +385,8 @@
         out_shape=[jax.ShapeDtypeStruct((rows, cols), BF16)]
         + [jax.ShapeDtypeStruct((slots, dim), BF16)] * count,
         name="sent_rows",
-    )(chan, pos, near, across)
+        compiler_params=pltpu.CompilerParams(vmem_limit_bytes=GRANT),
+    )(chan, pos, near, *across)
 
 
 def norm_of(v):
@@ -347,6 +433,7 @@
         out_specs=pl.BlockSpec((tile, width), lambda i: (i, 0)),
         out_shape=jax.ShapeDtypeStruct((rows, width), F32),
         name="latent_grads",
+        compiler_params=pltpu.CompilerParams(vmem_limit_bytes=GRANT),
     )(pos_cols, latent, upstream, q)
 
 
@@ -390,6 +477,7 @@
         ),
         out_shape=jax.ShapeDtypeStruct((total, dim), BF16),
         name="ordered",
+        compiler_params=pltpu.CompilerParams(vmem_limit_bytes=GRANT),
     )(chan, place, picked, *chunks)
 
 
@@ -454,6 +542,7 @@
         ),
         out_shape=jax.ShapeDtypeStruct((codes_dev, dim), F32),
         name="table",
+        compiler_params=pltpu.CompilerParams(vmem_limit_bytes=GRANT),
     )(bounds, codes, *runs)
 
 
@@ -476,13 +565,51 @@
     seq = lax.axis_index("seq").astype(jnp.int32)
     half = chans // 2
     core = seq % 2
-    frames, width = frames_in.shape
+    frames, _ = frames_in.shape
     rows = frames // chans
     codes_dev, dim = codebook.shape
     groups = code_index.shape[1]
     heads = decay_rate.shape[0]
-    head_dim = width // heads
-
+
+    wrows = out_weight.shape[0] // 2
+    share = (seq // 2) % 2
+    split = seqs >= 4 and wrows % 256 == 0
+    mine = lax.dynamic_slice_in_dim(out_weight, core * wrows, wrows, 0)
+    firsts = [None] * half
+    for k in sorted(range(1, half), key=lambda k: (k & (k - 1) == 0, k)):
+        if k & (k - 1) and split:
+            part = lax.dynamic_slice_in_dim(
+                out_weight, core * wrows + share * (wrows // 2), wrows // 2, 0
+            )
+            part = flip(part, "chan", k)
+            firsts[k] = [part, flip(part, "seq", 2)]
+        else:
+            firsts[k] = [flip(mine, "chan", k)]
+    firsts = firsts[1:]
+    seconds = [[flip(w, "seq", 1) for w in ws] for ws in firsts]
+
+    step_t = step_size.T
+    starts, cums, before, sent = block_states(
+        frames_in, in_keys, step_t, decay_rate.reshape(1, heads), rows
+    )
+    states = {k: flip(sent, "seq", k) for k in list(range(2, seqs)) + [1]}
+    states = [states[k] for k in range(1, seqs)]
+    skip = skip_gain.reshape(1, heads)
+
+    def gated_for(which):
+        base, slope = intra_block(
+            which, half, frames_in, gate_in, in_keys, out_keys, step_t, cums, skip, rows
+        )
+        return gated_blocks(which, base, slope, out_keys, starts, before, states)
+
+    def exchanged(out):
+        return [out[0]] + [flip(out[k], "chan", k) for k in range(1, half)]
+
+    far_out = gated_for(jnp.stack([chan ^ half, seq]))
+    far_blocks = exchanged(far_out)
+    near, _ = lax.optimization_barrier((jnp.stack([chan, seq]), far_out))
+    near_out = gated_for(near)
+    near_blocks = exchanged(near_out)
     entries = rows * groups
     slots = max(1, (entries + chans - 1) // chans)
     flat = code_index.T.reshape(entries)
@@ -499,71 +626,12 @@
         jnp.where(slot_of[None, :] == entry[:, None], within[None, :] + 1, 0), axis=1
     )
     wanted = jnp.where(wanted == 0, codes_dev, wanted - 1).reshape(chans, slots)
-    wrows = out_weight.shape[0] // 2
-    mine = lax.dynamic_slice_in_dim(out_weight, core * wrows, wrows, 0)
-    other = lax.dynamic_slice_in_dim(out_weight, (1 - core) * wrows, wrows, 0)
-    firsts = [mine] + [flip(mine, "chan", k) for k in range(1, half)]
-    seconds = [other] + [flip(firsts[k], "seq", 1) for k in range(1, half)]
-
-    step_t = step_size.T
-    rate = decay_rate.reshape(heads, 1)
-    starts, cums, before, held, sent = block_states(frames_in, in_keys, step_t, rate, rows)
-    held_log = -jnp.sum(step_t * rate, axis=1)
-    lower_log = jnp.zeros_like(held_log)
-
-    def rows_of(logs, use, otherwise):
-        return jnp.repeat(jnp.where(use, jnp.exp(logs), otherwise), head_dim)[:, None]
-
-    factors = []
-    bit = 1
-    while bit < seqs:
-        got_log = flip(held_log, "seq", bit)
-        after = (seq & bit) != 0
-        factors.append(
-            (
-                rows_of(lower_log, after, 0.0),
-                rows_of(held_log, after, 1.0),
-                rows_of(got_log, ~after, 1.0),
-            )
-        )
-        lower_log = jnp.where(after, lower_log + got_log, lower_log)
-        held_log = held_log + got_log
-        bit *= 2
-    incoming = jnp.zeros_like(held)
-    bit = 1
-    for to_incoming, to_got, to_held in factors:
-        got = flip(sent, "seq", bit).astype(F32)
-        incoming = incoming + to_incoming * got
-        held = to_got * got + to_held * held
-        sent = held.astype(BF16)
-        bit *= 2
-
-    top = chan // half
-    low = chan % half
-    turn = jnp.arange(half, dtype=jnp.int32)
-    near = jnp.concatenate([top * half + (low ^ turn), core[None]])
-    far = jnp.concatenate([(1 - top) * half + (low ^ turn), core[None]])
-    skip = jnp.repeat(skip_gain, head_dim)[None, :]
-
-    def gated_for(which):
-        base, slope = intra_block(
-            which, half, frames_in, gate_in, in_keys, out_keys, step_t, cums, skip, rows
-        )
-        return gated_blocks(which, base, slope, out_keys, starts, before, incoming)
-
-    def exchanged(out):
-        return [out[0]] + [flip(out[k], "chan", k) for k in range(1, half)]
-
-    far_out = gated_for(far)
-    far_blocks = exchanged(far_out)
-    near, _ = lax.optimization_barrier((near, far_out))
-    near_out = gated_for(near)
-    near_blocks = exchanged(near_out)
-    wanted, _ = lax.optimization_barrier((wanted, near_out))
     received = lax.all_to_all(wanted, "chan", split_axis=0, concat_axis=0, tiled=True)
-    far_sums = project(core[None], far_blocks, firsts, seconds, BF16)
-    across = flip(far_sums, "chan", half)
-    near_sums = project(core[None], near_blocks, firsts, seconds, F32)
+
+    far_sums = project(jnp.stack([core, share]), far_blocks, out_weight, firsts, seconds, BF16, 2)
+    across = [flip(far_sums[0], "chan", half)]
+    across.append(flip(far_sums[1], "chan", half))
+    (near_sums,) = project(jnp.stack([core, share]), near_blocks, out_weight, firsts, seconds, F32, 1)
 
     asked = received.reshape(1, entries)
     bit = seqs // 2
@@ -585,14 +653,14 @@
     bounds = jnp.sum((run_codes[:, None, :] < edges[None, :, None]).astype(jnp.int32), axis=2)
     run_codes = jnp.pad(run_codes, ((0, 0), (0, 256)), constant_values=-1)
 
-    near_sums, ranks, run_codes, bounds, picked = lax.optimization_barrier(
-        (near_sums, ranks, run_codes, bounds, picked)
+    near_sums, ranks, run_codes, bounds, picked, back = lax.optimization_barrier(
+        (near_sums, ranks, run_codes, bounds, picked, picked[0])
     )
     latent, *sends = sent_rows(chan[None], pos, near_sums, across, chans, slots, dim)
     arrived = {0: sends[0]}
     for k in range(1, chans):
         arrived[k] = flip(sends[k], "chan", k)
-    back, _ = lax.optimization_barrier((picked[0], sends[0]))
+    back, _ = lax.optimization_barrier((back, sends[0]))
     q = lax.all_to_all(back, "chan", split_axis=0, concat_axis=0, tiled=True)
     chunks = []
     for k in range(chans):

time: 259 us -> 262 us (1.012)
  Pallas kernels: 78.9 us -> 56.7 us
  local copies, waits for them, and re-layouts: 25.9 us -> 45 us
  starting transfers between devices: 52.6 us -> 58.6 us
  waiting for transfers between devices: 87.5 us -> 83.3 us
  other arithmetic: 11.3 us -> 15 us
    unnamed x76 -> x84, local copies, waits for them, and re-layouts: 4.19 us -> 21.2 us
    ppermute x35 -> x38, waiting for transfers between devices: 81.1 us -> 67.9 us  [flip(): return lax.ppermute(x, axis, [(i, i ^ bit) for i in range(n)])]
    all_to_all x1, waiting for transfers between devices: 6.39 us -> 15.4 us  [layer(): lax.all_to_all(wanted, 'chan', split_axis=0, concat_axis=0, tiled=True)]
    all_to_all x1, starting transfers between devices: 3.92 us -> 10 us  [layer(): q = lax.all_to_all(back, 'chan', split_axis=0, concat_axis=0, tiled=True)]
    pallas_call x4, Pallas kernels: 24.4 us -> 18.4 us  [the longest x2 11.9 us: project(): pl.pallas_call(functools.partial(project_kernel, count=count, shares=[1]...]
    pallas_call x2, Pallas kernels: 7.87 us -> 3.15 us  [ordered(): pl.pallas_call(order_kernel, grid_spec=pltpu.PrefetchScalarGridSpec(num_s...]
    pallas_call x2, Pallas kernels: 16.7 us -> 12.3 us  [intra_block(): pl.pallas_call(intra_kernel, grid_spec=pltpu.PrefetchScalarGridSpec(num_s...]
    pallas_call x1, Pallas kernels: 7.65 us -> 4.79 us  [block_states(): pl.pallas_call(states_kernel, grid=(nb,), in_specs=[pl.BlockSpec((rows, w...]
  transfers between devices with their start and end apart: 37 -> 40, of which waited for: 16 -> 16; matrix products, arithmetic and copies ran while one was open for 12% -> 14% of each run, Pallas kernels for 27% -> 19%
where the time goes in v3:
time: 262 us; the launch traced here: 260 us
  waiting for transfers between devices  83.3 us (32%)
  starting transfers between devices  58.6 us (22%)
  Pallas kernels  56.7 us (22%)
  local copies, waits for them, and re-layouts  45 us (17%)
  other arithmetic  15 us (6%)
    ppermute x38, waiting for transfers between devices, flip(): return lax.ppermute(x, axis, [(i, i ^ bit) for i in range(n)])  67.9 us
    ppermute x38, starting transfers between devices, flip(): return lax.ppermute(x, axis, [(i, i ^ bit) for i in range(n)])  42.4 us
    unnamed x84, local copies, waits for them, and re-layouts  21.2 us
    all_to_all x1, waiting for transfers between devices, layer(): lax.all_to_all(wanted, 'chan', split_axis=0, concat_axis=0, tiled=True)  15.4 us
    gather x1, local copies, waits for them, and re-layouts, layer(): jnp.take(codebook, jnp.minimum(asked, codes_dev - 1).reshape(-1, slots),...  14.4 us
    pallas_call x2, Pallas kernels, intra_block(): pl.pallas_call(intra_kernel, grid_spec=pltpu.PrefetchScalarGridSpec(num_s...  12.3 us
    pallas_call x2, Pallas kernels, project(): pl.pallas_call(functools.partial(project_kernel, count=count, shares=[1]...  11.9 us
    pallas_call x1, Pallas kernels, table(): pl.pallas_call(functools.partial(table_kernel, window=window, codes=block...  11.6 us
  transfers between devices with their start and end apart: 40, of which 16 were waited for; matrix products, arithmetic and copies ran while one was open for 14% of the time, Pallas kernels for 19%

profile of v3, /device:TPU:0, one launch (start us, length us, event | category | flops | bytes accessed | tf_op | source)
XLA Modules:
  0.0 260.3 jit_solution(3605825076234371579)
XLA Ops:
  3.2 3.0 %collective-permute-start.6 = (bf16[256,2048]{1,0:T(8,128)(2,1)}, bf16[256,2048]{1,0:T(8,128)(2,1)}, u32[]{:S(2)}, u32[]{:S(2)}) collective-permute-start(bf16[256,2048]{1,0:T(8,128)(2,1)} %constant_dynamic-slice_fusion.1), channel_id=1, source_target_pairs={{0,1},{1,0},{2,3},{3,2},{4,5},{5,4},{6,7},{7,6},{8,9},{9,8},{10,11... | collective-permute-start | bytes 3145736 | tf_op jit(solution)/shard_map/ppermute | solution.py:21
  10.2 4.8 %block_states.1 = (bf16[8,512,128]{2,1,0:T(8,128)(2,1)S(1)}, f32[8,2048]{1,0:T(8,128)S(1)}, f32[8,8,128]{2,1,0:T(8,128)S(1)}, bf16[560,128]{1,0:T(8,128)(2,1)}) custom-call(bf16[2048,512]{1,0:T(8,128)(2,1)S(1)} %copy-done.1, bf16[2048,128]{1,0:T(8,128)(2,1)S(1)} %copy-done.7, f32[8,2048]{1,0:T(8,128)S(1)} %bitcast.34, f32[1,8]{1,0:T(1,128)S(1)} %bitcast.39), custom_call_target="tpu_custom_call" | custom-call | tf_op jit(solution)/shard_map/block_states/pallas_call | solution.py:107
  18.4 6.2 %all-to-all-start = ((s32[8,1,128]{2,1,0:T(1,128)}), s32[8,1,128]{2,1,0:T(1,128)}, u32[]{:S(2)}, u32[]{:S(2)}) async-start(s32[8,1,128]{2,1,0:T(1,128)} %bitcast.9), calls=%async_computation | async-start | bytes 8192 | tf_op jit(solution)/shard_map/all_to_all | solution.py:629
  28.9 15.4 %all-to-all-done = s32[8,1,128]{2,1,0:T(1,128)} async-done(((s32[8,1,128]{2,1,0:T(1,128)}), s32[8,1,128]{2,1,0:T(1,128)}, u32[]{:S(2)}, u32[]{:S(2)}) %all-to-all-start) | async-done | bytes 4128 | tf_op jit(solution)/shard_map/all_to_all | solution.py:629
  51.1 6.1 %intra_block.2 = (f32[4,256,512]{2,1,0:T(8,128)S(1)}, bf16[4,256,512]{2,1,0:T(8,128)(2,1)S(1)}) custom-call(s32[2]{0:T(128)S(1)} %copy-done.24, bf16[2048,512]{1,0:T(8,128)(2,1)S(1)} %copy-done.2, bf16[2048,512]{1,0:T(8,128)(2,1)S(1)} %copy-done.5, bf16[2048,128]{1,0:T(8,128)(2,1)S(1)} %copy-done.7, bf16[2048,128]{1,0:T(8,128)(2,1)S(1)} %copy-done.4, ...), custom_call_target="tpu_custom_call" | custom-call | tf_op jit(solution)/shard_map/intra_block/pallas_call | solution.py:179
  66.1 14.4 %gather_fusion = bf16[2048,512]{1,0:T(8,128)(2,1)} fusion(bf16[8192,512]{1,0:T(8,128)(2,1)} %param.19, s32[2048]{0:T(1024)} %fusion.10), kind=kCustom, calls=%fused_computation | custom fusion | bytes 4202496 | tf_op jit(solution)/shard_map/jit(_take)/gather | solution.py:641
  86.7 3.6 %gated_blocks.2 = (bf16[256,512]{1,0:T(8,128)(2,1)S(1)}, bf16[256,512]{1,0:T(8,128)(2,1)}, bf16[256,512]{1,0:T(8,128)(2,1)}, bf16[256,512]{1,0:T(8,128)(2,1)S(1)}) custom-call(s32[2]{0:T(128)S(1)} %copy-done.25, f32[4,256,512]{2,1,0:T(8,128)S(1)} %copy-done.12, bf16[4,256,512]{2,1,0:T(8,128)(2,1)S(1)} %copy-done.16, bf16[2048,128]{1,0:T(8,128)(2,1)S(1)} %copy-done.4, ...), custom_call_target="tpu_custom_call" | custom-call | tf_op jit(solution)/shard_map/gated_blocks/pallas_call | solution.py:257
  96.6 4.1 %collective-permute-done.16.refs_1_ = bf16[256,512]{1,0:T(8,128)(2,1)} collective-permute-done((bf16[256,512]{1,0:T(8,128)(2,1)}, bf16[256,512]{1,0:T(8,128)(2,1)}, u32[]{:S(2)}, u32[]{:S(2)}) %collective-permute-start.16) | collective-permute-done | bytes 262176 | tf_op jit(solution)/shard_map/ppermute | solution.py:21
  106.2 6.2 %collective-permute-done.18.refs_3_ = bf16[256,512]{1,0:T(8,128)(2,1)S(1)} collective-permute-done((bf16[256,512]{1,0:T(8,128)(2,1)}, bf16[256,512]{1,0:T(8,128)(2,1)S(1)}, u32[]{:S(2)}, u32[]{:S(2)}) %collective-permute-start.18) | collective-permute-done | bytes 262176 | tf_op jit(solution)/shard_map/ppermute | solution.py:21
  114.2 6.3 %project.3 = (bf16[256,1024]{1,0:T(8,128)(2,1)S(1)}, bf16[256,1024]{1,0:T(8,128)(2,1)S(1)}) custom-call(s32[2]{0:T(128)S(1)} %copy-done.28, bf16[256,512]{1,0:T(8,128)(2,1)S(1)} %copy-done.19, bf16[256,512]{1,0:T(8,128)(2,1)} %collective-permute-done.16.refs_1_, bf16[256,512]{1,0:T(8,128)(2,1)} %collective-permute-done.17.refs_2_, ...), custom_call_target="tpu_custom_call" | custom-call | tf_op jit(solution)/shard_map/project/pallas_call | solution.py:329
  123.5 6.2 %intra_block.3 = (f32[4,256,512]{2,1,0:T(8,128)S(1)}, bf16[4,256,512]{2,1,0:T(8,128)(2,1)S(1)}) custom-call(s32[2]{0:T(128)S(1)} %copy-done.23, bf16[2048,512]{1,0:T(8,128)(2,1)S(1)} %copy-done.3, bf16[2048,512]{1,0:T(8,128)(2,1)S(1)} %copy-done.6, bf16[2048,128]{1,0:T(8,128)(2,1)S(1)} %copy-done.7, bf16[2048,128]{1,0:T(8,128)(2,1)S(1)} %copy-done.4, ...), custom_call_target="tpu_custom_call" | custom-call | tf_op jit(solution)/shard_map/intra_block/pallas_call | solution.py:179
  129.7 2.9 %gated_blocks.3 = (bf16[256,512]{1,0:T(8,128)(2,1)S(1)}, bf16[256,512]{1,0:T(8,128)(2,1)S(1)}, bf16[256,512]{1,0:T(8,128)(2,1)S(1)}, bf16[256,512]{1,0:T(8,128)(2,1)S(1)}) custom-call(s32[2]{0:T(128)S(1)} %copy-done.23, f32[4,256,512]{2,1,0:T(8,128)S(1)} %get-tuple-element.49.base_ref, bf16[4,256,512]{2,1,0:T(8,128)(2,1)S(1)} %get-tuple-element.50.slope_ref, ...), custom_call_target="tpu_custom_call" | custom-call | tf_op jit(solution)/shard_map/gated_blocks/pallas_call | solution.py:257
  141.0 9.4 %collective-permute-done.4.refs_2_ = bf16[256,512]{1,0:T(8,128)(2,1)S(1)} collective-permute-done((bf16[256,512]{1,0:T(8,128)(2,1)S(1)}, bf16[256,512]{1,0:T(8,128)(2,1)S(1)}, u32[]{:S(2)}, u32[]{:S(2)}) %collective-permute-start.4) | collective-permute-done | bytes 262176 | tf_op jit(solution)/shard_map/ppermute | solution.py:21
  150.4 5.2 %collective-permute-done.5.refs_3_ = bf16[256,512]{1,0:T(8,128)(2,1)S(1)} collective-permute-done((bf16[256,512]{1,0:T(8,128)(2,1)S(1)}, bf16[256,512]{1,0:T(8,128)(2,1)S(1)}, u32[]{:S(2)}, u32[]{:S(2)}) %collective-permute-start.5) | collective-permute-done | bytes 262176 | tf_op jit(solution)/shard_map/ppermute | solution.py:21
  155.5 5.7 %project.2.near_ref = f32[256,2048]{1,0:T(8,128)S(1)} custom-call(s32[2]{0:T(128)S(1)} %copy-done.29, bf16[256,512]{1,0:T(8,128)(2,1)S(1)} %get-tuple-element.51.refs_0_, bf16[256,512]{1,0:T(8,128)(2,1)S(1)} %collective-permute-done.3.refs_1_, bf16[256,512]{1,0:T(8,128)(2,1)S(1)} %collective-permute-done.4.refs_2_, ...), custom_call_target="tpu_custom_call" | custom-call | tf_op jit(solution)/shard_map/project/pallas_call | solution.py:329
  161.2 8.3 %collective-permute-done.20.later_ref = bf16[256,1024]{1,0:T(8,128)(2,1)S(1)} collective-permute-done((bf16[256,1024]{1,0:T(8,128)(2,1)S(1)}, bf16[256,1024]{1,0:T(8,128)(2,1)S(1)}, u32[]{:S(2)}, u32[]{:S(2)}) %collective-permute-start.20) | collective-permute-done | bytes 524320 | tf_op jit(solution)/shard_map/ppermute | solution.py:21
  171.8 10.0 %all-to-all-start.1 = ((bf16[8,128,512]{2,1,0:T(8,128)(2,1)}), bf16[8,128,512]{2,1,0:T(8,128)(2,1)S(1)}, u32[]{:S(2)}, u32[]{:S(2)}) async-start(bf16[8,128,512]{2,1,0:T(8,128)(2,1)} %slice_select_fusion), calls=%async_computation.1 | async-start | bytes 2097152 | tf_op jit(solution)/shard_map/all_to_all | solution.py:664
  185.3 2.9 %collective-permute-start.24 = (bf16[128,512]{1,0:T(8,128)(2,1)S(1)}, bf16[128,512]{1,0:T(8,128)(2,1)S(1)}, u32[]{:S(2)}, u32[]{:S(2)}) collective-permute-start(bf16[128,512]{1,0:T(8,128)(2,1)S(1)} %get-tuple-element.69), channel_id=1, source_target_pairs={{0,4},{1,5},{2,6},{3,7},{4,0},{5,1},{6,2},{7,3},{8,12},{9,13},{10,... | collective-permute-start | bytes 393224 | tf_op jit(solution)/shard_map/ppermute | solution.py:21
  189.7 3.7 %collective-permute-done.21.refs_1_ = bf16[128,512]{1,0:T(8,128)(2,1)S(1)} collective-permute-done((bf16[128,512]{1,0:T(8,128)(2,1)S(1)}, bf16[128,512]{1,0:T(8,128)(2,1)S(1)}, u32[]{:S(2)}, u32[]{:S(2)}) %collective-permute-start.21) | collective-permute-done | bytes 131104 | tf_op jit(solution)/shard_map/ppermute | solution.py:21
  194.9 7.9 %collective-permute-done.22.refs_2_ = bf16[128,512]{1,0:T(8,128)(2,1)S(1)} collective-permute-done((bf16[128,512]{1,0:T(8,128)(2,1)S(1)}, bf16[128,512]{1,0:T(8,128)(2,1)S(1)}, u32[]{:S(2)}, u32[]{:S(2)}) %collective-permute-start.22) | collective-permute-done | bytes 131104 | tf_op jit(solution)/shard_map/ppermute | solution.py:21
  202.9 3.4 %collective-permute-start.26 = (bf16[128,512]{1,0:T(8,128)(2,1)S(1)}, bf16[128,512]{1,0:T(8,128)(2,1)S(1)}, u32[]{:S(2)}, u32[]{:S(2)}) collective-permute-start(bf16[128,512]{1,0:T(8,128)(2,1)S(1)} %get-tuple-element.71), channel_id=1, source_target_pairs={{0,6},{1,7},{2,4},{3,5},{4,2},{5,3},{6,0},{7,1},{8,14},{9,15},{10,... | collective-permute-start | bytes 393224 | tf_op jit(solution)/shard_map/ppermute | solution.py:21
  208.7 10.7 %collective-permute-done.24.refs_4_ = bf16[128,512]{1,0:T(8,128)(2,1)S(1)} collective-permute-done((bf16[128,512]{1,0:T(8,128)(2,1)S(1)}, bf16[128,512]{1,0:T(8,128)(2,1)S(1)}, u32[]{:S(2)}, u32[]{:S(2)}) %collective-permute-start.24) | collective-permute-done | bytes 131104 | tf_op jit(solution)/shard_map/ppermute | solution.py:21
  242.0 11.6 %table.1 = f32[8192,512]{1,0:T(8,128)} custom-call(s32[4,33]{1,0:T(4,128)S(1)} %copy.34.bounds_ref, s32[4,1280]{1,0:T(4,128)S(1)} %pad.4.codes_ref, bf16[1024,512]{1,0:T(8,128)(2,1)S(1)} %ordered.2.refs_0_, bf16[1024,512]{1,0:T(8,128)(2,1)S(1)} %ordered.3.refs_1_, bf16[1024,512]{1,0:T(8,128)(2,1)} %collective-permute-done.36.refs_2_, ...), custom_call_target="tpu_custom_call" | custom-call | tf_op jit(solution)/shard_map/table/pallas_call | solution.py:534
  256.0 4.2 %latent_grads.1 = f32[256,2048]{1,0:T(8,128)} custom-call(s32[256,4]{1,0:T(8,128)S(1)} %bitcast.33, bf16[256,2048]{1,0:T(8,128)(2,1)S(1)} %copy-done.14, bf16[256,2048]{1,0:T(8,128)(2,1)S(1)} %copy-done.13, bf16[1024,512]{1,0:T(8,128)(2,1)S(1)} %bitcast.32), custom_call_target="tpu_custom_call" | custom-call | tf_op jit(solution)/shard_map/latent_grads/pallas_call | solution.py:424
  (187 shorter events, 96.8 us)
Async XLA Ops:
  3.2 61.1 %collective-permute-start.6 = (bf16[256,2048]{1,0:T(8,128)(2,1)}, bf16[256,2048]{1,0:T(8,128)(2,1)}, u32[]{:S(2)}, u32[]{:S(2)}) collective-permute-start(bf16[256,2048]{1,0:T(8,128)(2,1)} %constant_dynamic-slice_fusion.1), channel_id=1, source_target_pairs={{0,1},{1,0},{2,3},{3,2},{4,5},{5,4},{6,7},{7,6},{8,9},{9,8},{10,11... | collective-permute-start | bytes 3145736 | tf_op jit(solution)/shard_map/ppermute | solution.py:21
  6.2 58.4 %collective-permute-start.7 = (bf16[256,2048]{1,0:T(8,128)(2,1)}, bf16[256,2048]{1,0:T(8,128)(2,1)}, u32[]{:S(2)}, u32[]{:S(2)}) collective-permute-start(bf16[256,2048]{1,0:T(8,128)(2,1)} %constant_dynamic-slice_fusion.1), channel_id=1, source_target_pairs={{0,2},{1,3},{2,0},{3,1},{4,6},{5,7},{6,4},{7,5},{8,10},{9,11},{10,... | collective-permute-start | bytes 3145736 | tf_op jit(solution)/shard_map/ppermute | solution.py:21
  8.6 54.2 %collective-permute-start.8 = (bf16[128,2048]{1,0:T(8,128)(2,1)}, bf16[128,2048]{1,0:T(8,128)(2,1)}, u32[]{:S(2)}, u32[]{:S(2)}) collective-permute-start(bf16[128,2048]{1,0:T(8,128)(2,1)} %constant_dynamic-slice_fusion), channel_id=1, source_target_pairs={{0,3},{1,2},{2,1},{3,0},{4,7},{5,6},{6,5},{7,4},{8,11},{9,10},{10,... | collective-permute-start | bytes 1572872 | tf_op jit(solution)/shard_map/ppermute | solution.py:21
  16.6 46.2 %collective-permute-start = (bf16[560,128]{1,0:T(8,128)(2,1)}, bf16[560,128]{1,0:T(8,128)(2,1)S(1)}, u32[]{:S(2)}, u32[]{:S(2)}) collective-permute-start(bf16[560,128]{1,0:T(8,128)(2,1)} %get-tuple-element.43), channel_id=1, source_target_pairs={{0,8},{8,0},{16,24},{24,16},{1,9},{9,1},{17,25},{25,17},{2,10},{10... | collective-permute-start | bytes 430088 | tf_op jit(solution)/shard_map/ppermute | solution.py:21
  18.4 25.9 %all-to-all-start = ((s32[8,1,128]{2,1,0:T(1,128)}), s32[8,1,128]{2,1,0:T(1,128)}, u32[]{:S(2)}, u32[]{:S(2)}) async-start(s32[8,1,128]{2,1,0:T(1,128)} %bitcast.9), calls=%async_computation | async-start | bytes 8192 | tf_op jit(solution)/shard_map/all_to_all | solution.py:629
  44.3 15.2 %collective-permute-start.14 = (s32[1,1024]{1,0:T(1,128)}, s32[1,1024]{1,0:T(1,128)}, u32[]{:S(2)}, u32[]{:S(2)}) collective-permute-start(s32[1,1024]{1,0:T(1,128)} %bitcast.10), channel_id=1, source_target_pairs={{0,16},{8,24},{16,0},{24,8},{1,17},{9,25},{17,1},{25,9},{2,18},{10... | collective-permute-start | bytes 12296 | tf_op jit(solution)/shard_map/ppermute | solution.py:21
  59.6 21.7 %collective-permute-start.1 = (bf16[560,128]{1,0:T(8,128)(2,1)}, bf16[560,128]{1,0:T(8,128)(2,1)}, u32[]{:S(2)}, u32[]{:S(2)}) collective-permute-start(bf16[560,128]{1,0:T(8,128)(2,1)} %get-tuple-element.43), channel_id=1, source_target_pairs={{0,16},{8,24},{16,0},{24,8},{1,17},{9,25},{17,1},{25,9},{2,18},{10... | collective-permute-start | bytes 430088 | tf_op jit(solution)/shard_map/ppermute | solution.py:21
  62.7 18.5 %collective-permute-start.2 = (bf16[560,128]{1,0:T(8,128)(2,1)}, bf16[560,128]{1,0:T(8,128)(2,1)}, u32[]{:S(2)}, u32[]{:S(2)}) collective-permute-start(bf16[560,128]{1,0:T(8,128)(2,1)} %get-tuple-element.43), channel_id=1, source_target_pairs={{0,24},{8,16},{16,8},{24,0},{1,25},{9,17},{17,9},{25,1},{2,26},{10... | collective-permute-start | bytes 430088 | tf_op jit(solution)/shard_map/ppermute | solution.py:21
  62.7 37.9 %collective-permute-start.9 = (bf16[128,2048]{1,0:T(8,128)(2,1)}, bf16[128,2048]{1,0:T(8,128)(2,1)}, u32[]{:S(2)}, u32[]{:S(2)}) collective-permute-start(bf16[128,2048]{1,0:T(8,128)(2,1)} %collective-permute-done.8.refs_7_), channel_id=1, source_target_pairs={{0,16},{8,24},{16,0},{24,8},{1,17},{9,25},{17,1},{25,9},{2,18},{10... | collective-permute-start | bytes 1572872 | tf_op jit(solution)/shard_map/ppermute | solution.py:21
  64.3 48.2 %collective-permute-start.10 = (bf16[256,2048]{1,0:T(8,128)(2,1)}, bf16[256,2048]{1,0:T(8,128)(2,1)}, u32[]{:S(2)}, u32[]{:S(2)}) collective-permute-start(bf16[256,2048]{1,0:T(8,128)(2,1)} %collective-permute-done.6.refs_5_), channel_id=1, source_target_pairs={{0,8},{8,0},{16,24},{24,16},{1,9},{9,1},{17,25},{25,17},{2,10},{10... | collective-permute-start | bytes 3145736 | tf_op jit(solution)/shard_map/ppermute | solution.py:21
  64.6 47.9 %collective-permute-start.11 = (bf16[256,2048]{1,0:T(8,128)(2,1)}, bf16[256,2048]{1,0:T(8,128)(2,1)}, u32[]{:S(2)}, u32[]{:S(2)}) collective-permute-start(bf16[256,2048]{1,0:T(8,128)(2,1)} %collective-permute-done.7.refs_6_), channel_id=1, source_target_pairs={{0,8},{8,0},{16,24},{24,16},{1,9},{9,1},{17,25},{25,17},{2,10},{10... | collective-permute-start | bytes 3145736 | tf_op jit(solution)/shard_map/ppermute | solution.py:21
  112.5 22.1 %collective-permute-start.15 = (s32[2,1024]{1,0:T(2,128)S(1)}, s32[2,1024]{1,0:T(2,128)S(1)}, u32[]{:S(2)}, u32[]{:S(2)}) collective-permute-start(s32[2,1024]{1,0:T(2,128)S(1)} %select_reduce_fusion), channel_id=1, source_target_pairs={{0,8},{8,0},{16,24},{24,16},{1,9},{9,1},{17,25},{25,17},{2,10},{10... | collective-permute-start | bytes 24584 | tf_op jit(solution)/shard_map/ppermute | solution.py:21
  120.4 40.7 %collective-permute-start.19 = (bf16[256,1024]{1,0:T(8,128)(2,1)S(1)}, bf16[256,1024]{1,0:T(8,128)(2,1)S(1)}, u32[]{:S(2)}, u32[]{:S(2)}) collective-permute-start(bf16[256,1024]{1,0:T(8,128)(2,1)S(1)} %get-tuple-element.56), channel_id=1, source_target_pairs={{0,4},{1,5},{2,6},{3,7},{4,0},{5,1},{6,2},{7,3},{8,12},{9,13},{10,... | collective-permute-start | bytes 1572872 | tf_op jit(solution)/shard_map/ppermute | solution.py:21
  121.2 48.4 %collective-permute-start.20 = (bf16[256,1024]{1,0:T(8,128)(2,1)S(1)}, bf16[256,1024]{1,0:T(8,128)(2,1)S(1)}, u32[]{:S(2)}, u32[]{:S(2)}) collective-permute-start(bf16[256,1024]{1,0:T(8,128)(2,1)S(1)} %get-tuple-element.57), channel_id=1, source_target_pairs={{0,4},{1,5},{2,6},{3,7},{4,0},{5,1},{6,2},{7,3},{8,12},{9,13},{10,... | collective-permute-start | bytes 1572872 | tf_op jit(solution)/shard_map/ppermute | solution.py:21
  134.0 16.3 %collective-permute-start.4 = (bf16[256,512]{1,0:T(8,128)(2,1)S(1)}, bf16[256,512]{1,0:T(8,128)(2,1)S(1)}, u32[]{:S(2)}, u32[]{:S(2)}) collective-permute-start(bf16[256,512]{1,0:T(8,128)(2,1)S(1)} %get-tuple-element.53), channel_id=1, source_target_pairs={{0,2},{1,3},{2,0},{3,1},{4,6},{5,7},{6,4},{7,5},{8,10},{9,11},{10,... | collective-permute-start | bytes 786440 | tf_op jit(solution)/shard_map/ppermute | solution.py:21
  134.6 20.9 %collective-permute-start.5 = (bf16[256,512]{1,0:T(8,128)(2,1)S(1)}, bf16[256,512]{1,0:T(8,128)(2,1)S(1)}, u32[]{:S(2)}, u32[]{:S(2)}) collective-permute-start(bf16[256,512]{1,0:T(8,128)(2,1)S(1)} %get-tuple-element.54), channel_id=1, source_target_pairs={{0,3},{1,2},{2,1},{3,0},{4,7},{5,6},{6,5},{7,4},{8,11},{9,10},{10,... | collective-permute-start | bytes 786440 | tf_op jit(solution)/shard_map/ppermute | solution.py:21
  171.8 81.8 %all-to-all-start.1 = ((bf16[8,128,512]{2,1,0:T(8,128)(2,1)}), bf16[8,128,512]{2,1,0:T(8,128)(2,1)S(1)}, u32[]{:S(2)}, u32[]{:S(2)}) async-start(bf16[8,128,512]{2,1,0:T(8,128)(2,1)} %slice_select_fusion), calls=%async_computation.1 | async-start | bytes 2097152 | tf_op jit(solution)/shard_map/all_to_all | solution.py:664
  183.8 19.0 %collective-permute-start.22 = (bf16[128,512]{1,0:T(8,128)(2,1)S(1)}, bf16[128,512]{1,0:T(8,128)(2,1)S(1)}, u32[]{:S(2)}, u32[]{:S(2)}) collective-permute-start(bf16[128,512]{1,0:T(8,128)(2,1)S(1)} %get-tuple-element.67), channel_id=1, source_target_pairs={{0,2},{1,3},{2,0},{3,1},{4,6},{5,7},{6,4},{7,5},{8,10},{9,11},{10,... | collective-permute-start | bytes 393224 | tf_op jit(solution)/shard_map/ppermute | solution.py:21
  185.3 21.0 %collective-permute-start.23 = (bf16[128,512]{1,0:T(8,128)(2,1)S(1)}, bf16[128,512]{1,0:T(8,128)(2,1)S(1)}, u32[]{:S(2)}, u32[]{:S(2)}) collective-permute-start(bf16[128,512]{1,0:T(8,128)(2,1)S(1)} %get-tuple-element.68), channel_id=1, source_target_pairs={{0,3},{1,2},{2,1},{3,0},{4,7},{5,6},{6,5},{7,4},{8,11},{9,10},{10,... | collective-permute-start | bytes 393224 | tf_op jit(solution)/shard_map/ppermute | solution.py:21
  185.3 34.1 %collective-permute-start.24 = (bf16[128,512]{1,0:T(8,128)(2,1)S(1)}, bf16[128,512]{1,0:T(8,128)(2,1)S(1)}, u32[]{:S(2)}, u32[]{:S(2)}) collective-permute-start(bf16[128,512]{1,0:T(8,128)(2,1)S(1)} %get-tuple-element.69), channel_id=1, source_target_pairs={{0,4},{1,5},{2,6},{3,7},{4,0},{5,1},{6,2},{7,3},{8,12},{9,13},{10,... | collective-permute-start | bytes 393224 | tf_op jit(solution)/shard_map/ppermute | solution.py:21
  188.2 33.8 %collective-permute-start.25 = (bf16[128,512]{1,0:T(8,128)(2,1)S(1)}, bf16[128,512]{1,0:T(8,128)(2,1)S(1)}, u32[]{:S(2)}, u32[]{:S(2)}) collective-permute-start(bf16[128,512]{1,0:T(8,128)(2,1)S(1)} %get-tuple-element.70), channel_id=1, source_target_pairs={{0,5},{1,4},{2,7},{3,6},{4,1},{5,0},{6,3},{7,2},{8,13},{9,12},{10,... | collective-permute-start | bytes 393224 | tf_op jit(solution)/shard_map/ppermute | solution.py:21
  193.3 34.0 %collective-permute-start.28 = (bf16[128,512]{1,0:T(8,128)(2,1)S(1)}, bf16[128,512]{1,0:T(8,128)(2,1)S(1)}, u32[]{:S(2)}, u32[]{:S(2)}) collective-permute-start(bf16[128,512]{1,0:T(8,128)(2,1)S(1)} %get-tuple-element.60.refs_0_), channel_id=1, source_target_pairs={{0,16},{8,24},{16,0},{24,8},{1,17},{9,25},{17,1},{25,9},{2,18},{10... | collective-permute-start | bytes 393224 | tf_op jit(solution)/shard_map/ppermute | solution.py:21
  202.9 22.4 %collective-permute-start.26 = (bf16[128,512]{1,0:T(8,128)(2,1)S(1)}, bf16[128,512]{1,0:T(8,128)(2,1)S(1)}, u32[]{:S(2)}, u32[]{:S(2)}) collective-permute-start(bf16[128,512]{1,0:T(8,128)(2,1)S(1)} %get-tuple-element.71), channel_id=1, source_target_pairs={{0,6},{1,7},{2,4},{3,5},{4,2},{5,3},{6,0},{7,1},{8,14},{9,15},{10,... | collective-permute-start | bytes 393224 | tf_op jit(solution)/shard_map/ppermute | solution.py:21
  206.3 19.6 %collective-permute-start.27 = (bf16[128,512]{1,0:T(8,128)(2,1)S(1)}, bf16[128,512]{1,0:T(8,128)(2,1)S(1)}, u32[]{:S(2)}, u32[]{:S(2)}) collective-permute-start(bf16[128,512]{1,0:T(8,128)(2,1)S(1)} %get-tuple-element.72), channel_id=1, source_target_pairs={{0,7},{1,6},{2,5},{3,4},{4,3},{5,2},{6,1},{7,0},{8,15},{9,14},{10,... | collective-permute-start | bytes 393224 | tf_op jit(solution)/shard_map/ppermute | solution.py:21
  (58 other events, 393.7 us)

commit v4 on v3

--- a/solution.py
+++ b/solution.py
@@ -420,6 +420,9 @@
 def latent_grads(pos_cols, latent, upstream, q):
     rows, width = latent.shape
     groups = pos_cols.shape[1]
+    latent, upstream = [
+        pltpu.with_memory_space_constraint(x, pltpu.HBM) for x in (latent, upstream)
+    ]
     tile = min(rows, 128)
     return pl.pallas_call(
         grad_kernel,
@@ -607,9 +610,8 @@
 
     far_out = gated_for(jnp.stack([chan ^ half, seq]))
     far_blocks = exchanged(far_out)
-    near, _ = lax.optimization_barrier((jnp.stack([chan, seq]), far_out))
-    near_out = gated_for(near)
-    near_blocks = exchanged(near_out)
+    code_index, _ = lax.optimization_barrier((code_index, far_out))
+
     entries = rows * groups
     slots = max(1, (entries + chans - 1) // chans)
     flat = code_index.T.reshape(entries)
@@ -630,6 +632,9 @@
 
     far_sums = project(jnp.stack([core, share]), far_blocks, out_weight, firsts, seconds, BF16, 2)
     across = [flip(far_sums[0], "chan", half)]
+    near, _ = lax.optimization_barrier((jnp.stack([chan, seq]), far_sums))
+    near_out = gated_for(near)
+    near_blocks = exchanged(near_out)
     across.append(flip(far_sums[1], "chan", half))
     (near_sums,) = project(jnp.stack([core, share]), near_blocks, out_weight, firsts, seconds, F32, 1)
 
@@ -638,11 +643,14 @@
     while bit > 1:
         asked = jnp.concatenate([asked, flip(asked, "seq", bit)])
         bit //= 2
-    picked = jnp.take(
-        codebook, jnp.minimum(asked, codes_dev - 1).reshape(-1, slots), axis=0
-    ).reshape(-1, chans, slots, dim)
+    picked = jnp.take(codebook, asked.reshape(-1, slots), axis=0, mode="clip").reshape(
+        -1, chans, slots, dim
+    )
     keys = asked * entries + entry[None, :]
     ranks = jnp.sum((keys[:, None, :] < keys[:, :, None]).astype(jnp.int32), axis=2)
+    near_sums, asked, ranks, picked, back = lax.optimization_barrier(
+        (near_sums, asked, ranks, picked, picked[0])
+    )
     run_codes = jnp.sum(
         jnp.where(ranks[:, None, :] == entry[None, :, None], asked[:, None, :], 0), axis=2
     )
@@ -652,10 +660,6 @@
     edges = jnp.arange(codes_dev // block + 1, dtype=jnp.int32) * block
     bounds = jnp.sum((run_codes[:, None, :] < edges[None, :, None]).astype(jnp.int32), axis=2)
     run_codes = jnp.pad(run_codes, ((0, 0), (0, 256)), constant_values=-1)
-
-    near_sums, ranks, run_codes, bounds, picked, back = lax.optimization_barrier(
-        (near_sums, ranks, run_codes, bounds, picked, picked[0])
-    )
     latent, *sends = sent_rows(chan[None], pos, near_sums, across, chans, slots, dim)
     arrived = {0: sends[0]}
     for k in range(1, chans):

time: 262 us -> 218 us (0.83)
  waiting for transfers between devices: 83.3 us -> 59.5 us
  other arithmetic: 15 us -> 6.7 us
  local copies, waits for them, and re-layouts: 45 us -> 36.7 us
  starting transfers between devices: 58.6 us -> 51.6 us
  Pallas kernels: 56.7 us -> 60.5 us
    ppermute x38, waiting for transfers between devices: 67.9 us -> 53.9 us  [flip(): return lax.ppermute(x, axis, [(i, i ^ bit) for i in range(n)])]
    all_to_all x1, waiting for transfers between devices: 15.4 us -> 5.52 us  [layer(): lax.all_to_all(wanted, 'chan', split_axis=0, concat_axis=0, tiled=True)]
    unnamed x84 -> x59, local copies, waits for them, and re-layouts: 21.2 us -> 14.4 us
    all_to_all x1, starting transfers between devices: 10 us -> 3.74 us  [layer(): q = lax.all_to_all(back, 'chan', split_axis=0, concat_axis=0, tiled=True)]
    select_n x2 -> x0, other arithmetic: 2.74 us -> none  [layer(): jnp.take(codebook, jnp.minimum(asked, codes_dev - 1).reshape(-1, slots),...]
  transfers between devices with their start and end apart: 40 -> 40, of which waited for: 16 -> 15; matrix products, arithmetic and copies ran while one was open for 14% -> 12% of each run, Pallas kernels for 19% -> 24%
where the time goes in v4:
time: 218 us; the launch traced here: 217 us
  Pallas kernels  60.5 us (28%)
  waiting for transfers between devices  59.5 us (27%)
  starting transfers between devices  51.6 us (24%)
  local copies, waits for them, and re-layouts  36.7 us (17%)
  other arithmetic  6.7 us (3%)
    ppermute x38, waiting for transfers between devices, flip(): return lax.ppermute(x, axis, [(i, i ^ bit) for i in range(n)])  53.9 us
    ppermute x38, starting transfers between devices, flip(): return lax.ppermute(x, axis, [(i, i ^ bit) for i in range(n)])  42.4 us
    unnamed x59, local copies, waits for them, and re-layouts  14.4 us
    gather x1, local copies, waits for them, and re-layouts, layer(): jnp.take(codebook, asked.reshape(-1, slots), axis=0, mode='clip')  13.8 us
    pallas_call x2, Pallas kernels, project(): pl.pallas_call(functools.partial(project_kernel, count=count, shares=[1]...  12.7 us
    pallas_call x2, Pallas kernels, intra_block(): pl.pallas_call(intra_kernel, grid_spec=pltpu.PrefetchScalarGridSpec(num_s...  12.3 us
    pallas_call x1, Pallas kernels, table(): pl.pallas_call(functools.partial(table_kernel, window=window, codes=block...  11.6 us
    pallas_call x2, Pallas kernels, gated_blocks(): pl.pallas_call(functools.partial(gate_kernel, peers=len(states)), grid_sp...  7.13 us
  transfers between devices with their start and end apart: 40, of which 15 were waited for; matrix products, arithmetic and copies ran while one was open for 12% of the time, Pallas kernels for 24%

profile of v4, /device:TPU:0, one launch (start us, length us, event | category | flops | bytes accessed | tf_op | source)
XLA Modules:
  0.0 216.6 jit_solution(17892796735577349290)
XLA Ops:
  0.7 2.4 %constant_dynamic-slice_fusion.1 = bf16[256,2048]{1,0:T(8,128)(2,1)} fusion(bf16[512,2048]{1,0:T(8,128)(2,1)} %refs_9_.3, s32[]{:T(128)S(6)} %select_n.68), kind=kLoop, calls=%fused_computation.46 | loop fusion | bytes 2097156 | tf_op jit(solution)/shard_map/dynamic_slice | solution.py:580
  3.1 3.0 %collective-permute-start.6 = (bf16[256,2048]{1,0:T(8,128)(2,1)}, bf16[256,2048]{1,0:T(8,128)(2,1)}, u32[]{:S(2)}, u32[]{:S(2)}) collective-permute-start(bf16[256,2048]{1,0:T(8,128)(2,1)} %constant_dynamic-slice_fusion.1), channel_id=1, source_target_pairs={{0,1},{1,0},{2,3},{3,2},{4,5},{5,4},{6,7},{7,6},{8,9},{9,8},{10,11... | collective-permute-start | bytes 3145736 | tf_op jit(solution)/shard_map/ppermute | solution.py:21
  11.8 4.8 %block_states.1 = (bf16[8,512,128]{2,1,0:T(8,128)(2,1)S(1)}, f32[8,2048]{1,0:T(8,128)S(1)}, f32[8,8,128]{2,1,0:T(8,128)S(1)}, bf16[560,128]{1,0:T(8,128)(2,1)}) custom-call(bf16[2048,512]{1,0:T(8,128)(2,1)S(1)} %copy-done.1, bf16[2048,128]{1,0:T(8,128)(2,1)S(1)} %copy-done.8, f32[8,2048]{1,0:T(8,128)S(1)} %bitcast.32, f32[1,8]{1,0:T(1,128)S(1)} %bitcast.37), custom_call_target="tpu_custom_call" | custom-call | tf_op jit(solution)/shard_map/block_states/pallas_call | solution.py:107
  26.6 6.1 %intra_block.2 = (f32[4,256,512]{2,1,0:T(8,128)S(1)}, bf16[4,256,512]{2,1,0:T(8,128)(2,1)S(1)}) custom-call(s32[2]{0:T(128)S(1)} %pad_add_fusion.2.order_ref, bf16[2048,512]{1,0:T(8,128)(2,1)S(1)} %copy-done.2, bf16[2048,512]{1,0:T(8,128)(2,1)S(1)} %copy-done.6, bf16[2048,128]{1,0:T(8,128)(2,1)S(1)} %copy-done.9, bf16[2048,128]{1,0:T(8,128)(2,1)S(1)} %copy-done.4, ...), custom_call_target="tpu_custom_call" | custom-call | tf_op jit(solution)/shard_map/intra_block/pallas_call | solution.py:179
  32.8 3.5 %gated_blocks.2 = (bf16[256,512]{1,0:T(8,128)(2,1)S(1)}, bf16[256,512]{1,0:T(8,128)(2,1)}, bf16[256,512]{1,0:T(8,128)(2,1)}, bf16[256,512]{1,0:T(8,128)(2,1)S(1)}) custom-call(s32[2]{0:T(128)S(1)} %pad_add_fusion.2.order_ref, f32[4,256,512]{2,1,0:T(8,128)S(1)} %get-tuple-element.39.base_ref, bf16[4,256,512]{2,1,0:T(8,128)(2,1)S(1)} %get-tuple-element.40.slope_ref, ...), custom_call_target="tpu_custom_call" | custom-call | tf_op jit(solution)/shard_map/gated_blocks/pallas_call | solution.py:257
  45.2 2.5 %collective-permute-done.3.refs_1_ = bf16[256,512]{1,0:T(8,128)(2,1)} collective-permute-done((bf16[256,512]{1,0:T(8,128)(2,1)}, bf16[256,512]{1,0:T(8,128)(2,1)}, u32[]{:S(2)}, u32[]{:S(2)}) %collective-permute-start.3) | collective-permute-done | bytes 262176 | tf_op jit(solution)/shard_map/ppermute | solution.py:21
  47.7 2.7 %collective-permute-start.5 = (bf16[256,512]{1,0:T(8,128)(2,1)}, bf16[256,512]{1,0:T(8,128)(2,1)}, u32[]{:S(2)}, u32[]{:S(2)}) collective-permute-start(bf16[256,512]{1,0:T(8,128)(2,1)} %copy-done.25), channel_id=1, source_target_pairs={{0,3},{1,2},{2,1},{3,0},{4,7},{5,6},{6,5},{7,4},{8,11},{9,10},{10,... | collective-permute-start | bytes 786440 | tf_op jit(solution)/shard_map/ppermute | solution.py:21
  50.4 4.7 %collective-permute-done.9.refs_8_ = bf16[128,2048]{1,0:T(8,128)(2,1)} collective-permute-done((bf16[128,2048]{1,0:T(8,128)(2,1)S(1)}, bf16[128,2048]{1,0:T(8,128)(2,1)}, u32[]{:S(2)}, u32[]{:S(2)}) %collective-permute-start.9) | collective-permute-done | bytes 524320 | tf_op jit(solution)/shard_map/ppermute | solution.py:21
  55.7 5.5 %all-to-all-start = ((s32[8,1,128]{2,1,0:T(1,128)}), s32[8,1,128]{2,1,0:T(1,128)S(1)}, u32[]{:S(2)}, u32[]{:S(2)}) async-start(s32[8,1,128]{2,1,0:T(1,128)} %bitcast.9), calls=%async_computation | async-start | bytes 8192 | tf_op jit(solution)/shard_map/all_to_all | solution.py:631
  62.1 5.5 %all-to-all-done = s32[8,1,128]{2,1,0:T(1,128)S(1)} async-done(((s32[8,1,128]{2,1,0:T(1,128)}), s32[8,1,128]{2,1,0:T(1,128)S(1)}, u32[]{:S(2)}, u32[]{:S(2)}) %all-to-all-start) | async-done | bytes 4128 | tf_op jit(solution)/shard_map/all_to_all | solution.py:631
  71.4 6.8 %project.2 = (bf16[256,1024]{1,0:T(8,128)(2,1)}, bf16[256,1024]{1,0:T(8,128)(2,1)}) custom-call(s32[2]{0:T(128)S(1)} %pad_add_fusion.3.place_ref, bf16[256,512]{1,0:T(8,128)(2,1)S(1)} %copy-done.20, bf16[256,512]{1,0:T(8,128)(2,1)} %collective-permute-done.3.refs_1_, bf16[256,512]{1,0:T(8,128)(2,1)} %collective-permute-done.4.refs_2_, ...), custom_call_target="tpu_custom_call" | custom-call | tf_op jit(solution)/shard_map/project/pallas_call | solution.py:329
  81.9 6.2 %intra_block.3 = (f32[4,256,512]{2,1,0:T(8,128)S(1)}, bf16[4,256,512]{2,1,0:T(8,128)(2,1)S(1)}) custom-call(s32[2]{0:T(128)S(1)} %pad_add_fusion.4.order_ref, bf16[2048,512]{1,0:T(8,128)(2,1)S(1)} %copy-done.3, bf16[2048,512]{1,0:T(8,128)(2,1)S(1)} %copy-done.7, bf16[2048,128]{1,0:T(8,128)(2,1)S(1)} %copy-done.10, bf16[2048,128]{1,0:T(8,128)(2,1)S(1)} %copy-done.5, ...), custom_call_target="tpu_custom_call" | custom-call | tf_op jit(solution)/shard_map/intra_block/pallas_call | solution.py:179
  88.1 3.6 %gated_blocks.3 = (bf16[256,512]{1,0:T(8,128)(2,1)S(1)}, bf16[256,512]{1,0:T(8,128)(2,1)}, bf16[256,512]{1,0:T(8,128)(2,1)}, bf16[256,512]{1,0:T(8,128)(2,1)}) custom-call(s32[2]{0:T(128)S(1)} %pad_add_fusion.4.order_ref, f32[4,256,512]{2,1,0:T(8,128)S(1)} %get-tuple-element.52.base_ref, bf16[4,256,512]{2,1,0:T(8,128)(2,1)S(1)} %get-tuple-element.53.slope_ref, ...), custom_call_target="tpu_custom_call" | custom-call | tf_op jit(solution)/shard_map/gated_blocks/pallas_call | solution.py:257
  95.9 13.8 %gather_fusion = bf16[2048,512]{1,0:T(8,128)(2,1)} fusion(bf16[8192,512]{1,0:T(8,128)(2,1)} %param.19, s32[2048]{0:T(1024)S(1)} %bitcast_clamp_fusion), kind=kCustom, calls=%fused_computation | custom fusion | bytes 4202496 | tf_op jit(solution)/shard_map/jit(_take)/gather | solution.py:646
  113.9 14.4 %collective-permute-done.16.refs_3_ = bf16[256,512]{1,0:T(8,128)(2,1)} collective-permute-done((bf16[256,512]{1,0:T(8,128)(2,1)}, bf16[256,512]{1,0:T(8,128)(2,1)}, u32[]{:S(2)}, u32[]{:S(2)}) %collective-permute-start.16) | collective-permute-done | bytes 262176 | tf_op jit(solution)/shard_map/ppermute | solution.py:21
  128.3 5.8 %project.3.near_ref = f32[256,2048]{1,0:T(8,128)S(1)} custom-call(s32[2]{0:T(128)S(1)} %pad_add_fusion.3.place_ref, bf16[256,512]{1,0:T(8,128)(2,1)S(1)} %copy-done.22, bf16[256,512]{1,0:T(8,128)(2,1)S(1)} %collective-permute-done.14.refs_1_, bf16[256,512]{1,0:T(8,128)(2,1)S(1)} %collective-permute-done.15.refs_2_, ...), custom_call_target="tpu_custom_call" | custom-call | tf_op jit(solution)/shard_map/project/pallas_call | solution.py:329
  134.2 3.5 %sent_rows.1 = (bf16[256,2048]{1,0:T(8,128)(2,1)}, bf16[128,512]{1,0:T(8,128)(2,1)S(1)}, bf16[128,512]{1,0:T(8,128)(2,1)S(1)}, bf16[128,512]{1,0:T(8,128)(2,1)S(...) custom-call(s32[1]{0:T(128)} %bitcast.chan_ref, ...), custom_call_target="tpu_custom_call" | custom-call | tf_op jit(solution)/shard_map/sent_rows/pallas_call | solution.py:371
  137.7 3.7 %all-to-all-start.1 = ((bf16[8,128,512]{2,1,0:T(8,128)(2,1)}), bf16[8,128,512]{2,1,0:T(8,128)(2,1)S(1)}, u32[]{:S(2)}, u32[]{:S(2)}) async-start(bf16[8,128,512]{2,1,0:T(8,128)(2,1)} %bitcast.39), calls=%async_computation.1 | async-start | bytes 2097152 | tf_op jit(solution)/shard_map/all_to_all | solution.py:668
  145.0 2.6 %collective-permute-start.24 = (bf16[128,512]{1,0:T(8,128)(2,1)S(1)}, bf16[128,512]{1,0:T(8,128)(2,1)S(1)}, u32[]{:S(2)}, u32[]{:S(2)}) collective-permute-start(bf16[128,512]{1,0:T(8,128)(2,1)S(1)} %get-tuple-element.69), channel_id=1, source_target_pairs={{0,4},{1,5},{2,6},{3,7},{4,0},{5,1},{6,2},{7,3},{8,12},{9,13},{10,... | collective-permute-start | bytes 393224 | tf_op jit(solution)/shard_map/ppermute | solution.py:21
  149.0 2.8 %collective-permute-done.21.refs_1_ = bf16[128,512]{1,0:T(8,128)(2,1)S(1)} collective-permute-done((bf16[128,512]{1,0:T(8,128)(2,1)S(1)}, bf16[128,512]{1,0:T(8,128)(2,1)S(1)}, u32[]{:S(2)}, u32[]{:S(2)}) %collective-permute-start.21) | collective-permute-done | bytes 131104 | tf_op jit(solution)/shard_map/ppermute | solution.py:21
  152.4 9.4 %collective-permute-done.22.refs_2_ = bf16[128,512]{1,0:T(8,128)(2,1)S(1)} collective-permute-done((bf16[128,512]{1,0:T(8,128)(2,1)S(1)}, bf16[128,512]{1,0:T(8,128)(2,1)S(1)}, u32[]{:S(2)}, u32[]{:S(2)}) %collective-permute-start.22) | collective-permute-done | bytes 131104 | tf_op jit(solution)/shard_map/ppermute | solution.py:21
  166.4 10.6 %collective-permute-done.24.refs_4_ = bf16[128,512]{1,0:T(8,128)(2,1)S(1)} collective-permute-done((bf16[128,512]{1,0:T(8,128)(2,1)S(1)}, bf16[128,512]{1,0:T(8,128)(2,1)S(1)}, u32[]{:S(2)}, u32[]{:S(2)}) %collective-permute-start.24) | collective-permute-done | bytes 131104 | tf_op jit(solution)/shard_map/ppermute | solution.py:21
  199.5 11.6 %table.1 = f32[8192,512]{1,0:T(8,128)} custom-call(s32[4,33]{1,0:T(4,128)S(1)} %copy.35.bounds_ref, s32[4,1280]{1,0:T(4,128)S(1)} %pad.4.codes_ref, bf16[1024,512]{1,0:T(8,128)(2,1)S(1)} %ordered.2.refs_0_, bf16[1024,512]{1,0:T(8,128)(2,1)S(1)} %ordered.3.refs_1_, bf16[1024,512]{1,0:T(8,128)(2,1)} %collective-permute-done.36.refs_2_, ...), custom_call_target="tpu_custom_call" | custom-call | tf_op jit(solution)/shard_map/table/pallas_call | solution.py:537
  211.1 5.5 %latent_grads.1 = f32[256,2048]{1,0:T(8,128)} custom-call(s32[256,4]{1,0:T(8,128)S(1)} %bitcast.31, bf16[256,2048]{1,0:T(8,128)(2,1)} %get-tuple-element.35.latent_ref, bf16[256,2048]{1,0:T(8,128)(2,1)} %up_ref.1, bf16[1024,512]{1,0:T(8,128)(2,1)S(1)} %bitcast.30), custom_call_target="tpu_custom_call" | custom-call | tf_op jit(solution)/shard_map/latent_grads/pallas_call | solution.py:427
  (157 shorter events, 74.4 us)
Async XLA Ops:
  3.1 40.6 %collective-permute-start.6 = (bf16[256,2048]{1,0:T(8,128)(2,1)}, bf16[256,2048]{1,0:T(8,128)(2,1)}, u32[]{:S(2)}, u32[]{:S(2)}) collective-permute-start(bf16[256,2048]{1,0:T(8,128)(2,1)} %constant_dynamic-slice_fusion.1), channel_id=1, source_target_pairs={{0,1},{1,0},{2,3},{3,2},{4,5},{5,4},{6,7},{7,6},{8,9},{9,8},{10,11... | collective-permute-start | bytes 3145736 | tf_op jit(solution)/shard_map/ppermute | solution.py:21
  6.1 37.6 %collective-permute-start.7 = (bf16[256,2048]{1,0:T(8,128)(2,1)}, bf16[256,2048]{1,0:T(8,128)(2,1)}, u32[]{:S(2)}, u32[]{:S(2)}) collective-permute-start(bf16[256,2048]{1,0:T(8,128)(2,1)} %constant_dynamic-slice_fusion.1), channel_id=1, source_target_pairs={{0,2},{1,3},{2,0},{3,1},{4,6},{5,7},{6,4},{7,5},{8,10},{9,11},{10,... | collective-permute-start | bytes 3145736 | tf_op jit(solution)/shard_map/ppermute | solution.py:21
  18.4 23.7 %collective-permute-start.8 = (bf16[128,2048]{1,0:T(8,128)(2,1)}, bf16[128,2048]{1,0:T(8,128)(2,1)S(1)}, u32[]{:S(2)}, u32[]{:S(2)}) collective-permute-start(bf16[128,2048]{1,0:T(8,128)(2,1)} %constant_dynamic-slice_fusion), channel_id=1, source_target_pairs={{0,3},{1,2},{2,1},{3,0},{4,7},{5,6},{6,5},{7,4},{8,11},{9,10},{10,... | collective-permute-start | bytes 1572872 | tf_op jit(solution)/shard_map/ppermute | solution.py:21
  18.4 14.4 %collective-permute-start.1 = (bf16[560,128]{1,0:T(8,128)(2,1)}, bf16[560,128]{1,0:T(8,128)(2,1)}, u32[]{:S(2)}, u32[]{:S(2)}) collective-permute-start(bf16[560,128]{1,0:T(8,128)(2,1)} %get-tuple-element.43), channel_id=1, source_target_pairs={{0,16},{8,24},{16,0},{24,8},{1,17},{9,25},{17,1},{25,9},{2,18},{10... | collective-permute-start | bytes 430088 | tf_op jit(solution)/shard_map/ppermute | solution.py:21
  42.1 13.0 %collective-permute-start.9 = (bf16[128,2048]{1,0:T(8,128)(2,1)S(1)}, bf16[128,2048]{1,0:T(8,128)(2,1)}, u32[]{:S(2)}, u32[]{:S(2)}) collective-permute-start(bf16[128,2048]{1,0:T(8,128)(2,1)S(1)} %collective-permute-done.8.refs_7_), channel_id=1, source_target_pairs={{0,16},{8,24},{16,0},{24,8},{1,17},{9,25},{17,1},{25,9},{2,18},{10... | collective-permute-start | bytes 1572872 | tf_op jit(solution)/shard_map/ppermute | solution.py:21
  43.7 26.6 %collective-permute-start.10 = (bf16[256,2048]{1,0:T(8,128)(2,1)}, bf16[256,2048]{1,0:T(8,128)(2,1)}, u32[]{:S(2)}, u32[]{:S(2)}) collective-permute-start(bf16[256,2048]{1,0:T(8,128)(2,1)} %collective-permute-done.6.refs_5_), channel_id=1, source_target_pairs={{0,8},{8,0},{16,24},{24,16},{1,9},{9,1},{17,25},{25,17},{2,10},{10... | collective-permute-start | bytes 3145736 | tf_op jit(solution)/shard_map/ppermute | solution.py:21
  43.7 26.6 %collective-permute-start.11 = (bf16[256,2048]{1,0:T(8,128)(2,1)}, bf16[256,2048]{1,0:T(8,128)(2,1)}, u32[]{:S(2)}, u32[]{:S(2)}) collective-permute-start(bf16[256,2048]{1,0:T(8,128)(2,1)} %collective-permute-done.7.refs_6_), channel_id=1, source_target_pairs={{0,8},{8,0},{16,24},{24,16},{1,9},{9,1},{17,25},{25,17},{2,10},{10... | collective-permute-start | bytes 3145736 | tf_op jit(solution)/shard_map/ppermute | solution.py:21
  47.7 19.9 %collective-permute-start.5 = (bf16[256,512]{1,0:T(8,128)(2,1)}, bf16[256,512]{1,0:T(8,128)(2,1)}, u32[]{:S(2)}, u32[]{:S(2)}) collective-permute-start(bf16[256,512]{1,0:T(8,128)(2,1)} %copy-done.25), channel_id=1, source_target_pairs={{0,3},{1,2},{2,1},{3,0},{4,7},{5,6},{6,5},{7,4},{8,11},{9,10},{10,... | collective-permute-start | bytes 786440 | tf_op jit(solution)/shard_map/ppermute | solution.py:21
  50.4 19.9 %collective-permute-start.12 = (bf16[128,2048]{1,0:T(8,128)(2,1)S(1)}, bf16[128,2048]{1,0:T(8,128)(2,1)}, u32[]{:S(2)}, u32[]{:S(2)}) collective-permute-start(bf16[128,2048]{1,0:T(8,128)(2,1)S(1)} %collective-permute-done.8.refs_7_), channel_id=1, source_target_pairs={{0,8},{8,0},{16,24},{24,16},{1,9},{9,1},{17,25},{25,17},{2,10},{10... | collective-permute-start | bytes 1572872 | tf_op jit(solution)/shard_map/ppermute | solution.py:21
  55.1 15.2 %collective-permute-start.13 = (bf16[128,2048]{1,0:T(8,128)(2,1)}, bf16[128,2048]{1,0:T(8,128)(2,1)}, u32[]{:S(2)}, u32[]{:S(2)}) collective-permute-start(bf16[128,2048]{1,0:T(8,128)(2,1)} %collective-permute-done.9.refs_8_), channel_id=1, source_target_pairs={{0,8},{8,0},{16,24},{24,16},{1,9},{9,1},{17,25},{25,17},{2,10},{10... | collective-permute-start | bytes 1572872 | tf_op jit(solution)/shard_map/ppermute | solution.py:21
  67.6 13.6 %collective-permute-start.17 = (s32[1,1024]{1,0:T(1,128)S(1)}, s32[1,1024]{1,0:T(1,128)S(1)}, u32[]{:S(2)}, u32[]{:S(2)}) collective-permute-start(s32[1,1024]{1,0:T(1,128)S(1)} %bitcast.44), channel_id=1, source_target_pairs={{0,16},{8,24},{16,0},{24,8},{1,17},{9,25},{17,1},{25,9},{2,18},{10... | collective-permute-start | bytes 12296 | tf_op jit(solution)/shard_map/ppermute | solution.py:21
  78.2 55.9 %collective-permute-start.18 = (bf16[256,1024]{1,0:T(8,128)(2,1)}, bf16[256,1024]{1,0:T(8,128)(2,1)}, u32[]{:S(2)}, u32[]{:S(2)}) collective-permute-start(bf16[256,1024]{1,0:T(8,128)(2,1)} %get-tuple-element.49), channel_id=1, source_target_pairs={{0,4},{1,5},{2,6},{3,7},{4,0},{5,1},{6,2},{7,3},{8,12},{9,13},{10,... | collective-permute-start | bytes 1572872 | tf_op jit(solution)/shard_map/ppermute | solution.py:21
  78.9 55.3 %collective-permute-start.19 = (bf16[256,1024]{1,0:T(8,128)(2,1)}, bf16[256,1024]{1,0:T(8,128)(2,1)}, u32[]{:S(2)}, u32[]{:S(2)}) collective-permute-start(bf16[256,1024]{1,0:T(8,128)(2,1)} %get-tuple-element.50), channel_id=1, source_target_pairs={{0,4},{1,5},{2,6},{3,7},{4,0},{5,1},{6,2},{7,3},{8,12},{9,13},{10,... | collective-permute-start | bytes 1572872 | tf_op jit(solution)/shard_map/ppermute | solution.py:21
  92.4 21.5 %collective-permute-start.14 = (bf16[256,512]{1,0:T(8,128)(2,1)}, bf16[256,512]{1,0:T(8,128)(2,1)S(1)}, u32[]{:S(2)}, u32[]{:S(2)}) collective-permute-start(bf16[256,512]{1,0:T(8,128)(2,1)} %get-tuple-element.55), channel_id=1, source_target_pairs={{0,1},{1,0},{2,3},{3,2},{4,5},{5,4},{6,7},{7,6},{8,9},{9,8},{10,11... | collective-permute-start | bytes 786440 | tf_op jit(solution)/shard_map/ppermute | solution.py:21
  92.9 20.9 %collective-permute-start.15 = (bf16[256,512]{1,0:T(8,128)(2,1)}, bf16[256,512]{1,0:T(8,128)(2,1)S(1)}, u32[]{:S(2)}, u32[]{:S(2)}) collective-permute-start(bf16[256,512]{1,0:T(8,128)(2,1)} %get-tuple-element.56), channel_id=1, source_target_pairs={{0,2},{1,3},{2,0},{3,1},{4,6},{5,7},{6,4},{7,5},{8,10},{9,11},{10,... | collective-permute-start | bytes 786440 | tf_op jit(solution)/shard_map/ppermute | solution.py:21
  93.5 34.8 %collective-permute-start.16 = (bf16[256,512]{1,0:T(8,128)(2,1)}, bf16[256,512]{1,0:T(8,128)(2,1)}, u32[]{:S(2)}, u32[]{:S(2)}) collective-permute-start(bf16[256,512]{1,0:T(8,128)(2,1)} %get-tuple-element.57), channel_id=1, source_target_pairs={{0,3},{1,2},{2,1},{3,0},{4,7},{5,6},{6,5},{7,4},{8,11},{9,10},{10,... | collective-permute-start | bytes 786440 | tf_op jit(solution)/shard_map/ppermute | solution.py:21
  137.7 73.5 %all-to-all-start.1 = ((bf16[8,128,512]{2,1,0:T(8,128)(2,1)}), bf16[8,128,512]{2,1,0:T(8,128)(2,1)S(1)}, u32[]{:S(2)}, u32[]{:S(2)}) async-start(bf16[8,128,512]{2,1,0:T(8,128)(2,1)} %bitcast.39), calls=%async_computation.1 | async-start | bytes 2097152 | tf_op jit(solution)/shard_map/all_to_all | solution.py:668
  143.1 18.6 %collective-permute-start.22 = (bf16[128,512]{1,0:T(8,128)(2,1)S(1)}, bf16[128,512]{1,0:T(8,128)(2,1)S(1)}, u32[]{:S(2)}, u32[]{:S(2)}) collective-permute-start(bf16[128,512]{1,0:T(8,128)(2,1)S(1)} %get-tuple-element.67), channel_id=1, source_target_pairs={{0,2},{1,3},{2,0},{3,1},{4,6},{5,7},{6,4},{7,5},{8,10},{9,11},{10,... | collective-permute-start | bytes 393224 | tf_op jit(solution)/shard_map/ppermute | solution.py:21
  144.6 19.4 %collective-permute-start.23 = (bf16[128,512]{1,0:T(8,128)(2,1)S(1)}, bf16[128,512]{1,0:T(8,128)(2,1)S(1)}, u32[]{:S(2)}, u32[]{:S(2)}) collective-permute-start(bf16[128,512]{1,0:T(8,128)(2,1)S(1)} %get-tuple-element.68), channel_id=1, source_target_pairs={{0,3},{1,2},{2,1},{3,0},{4,7},{5,6},{6,5},{7,4},{8,11},{9,10},{10,... | collective-permute-start | bytes 393224 | tf_op jit(solution)/shard_map/ppermute | solution.py:21
  145.0 32.0 %collective-permute-start.24 = (bf16[128,512]{1,0:T(8,128)(2,1)S(1)}, bf16[128,512]{1,0:T(8,128)(2,1)S(1)}, u32[]{:S(2)}, u32[]{:S(2)}) collective-permute-start(bf16[128,512]{1,0:T(8,128)(2,1)S(1)} %get-tuple-element.69), channel_id=1, source_target_pairs={{0,4},{1,5},{2,6},{3,7},{4,0},{5,1},{6,2},{7,3},{8,12},{9,13},{10,... | collective-permute-start | bytes 393224 | tf_op jit(solution)/shard_map/ppermute | solution.py:21
  147.5 32.0 %collective-permute-start.25 = (bf16[128,512]{1,0:T(8,128)(2,1)S(1)}, bf16[128,512]{1,0:T(8,128)(2,1)S(1)}, u32[]{:S(2)}, u32[]{:S(2)}) collective-permute-start(bf16[128,512]{1,0:T(8,128)(2,1)S(1)} %get-tuple-element.70), channel_id=1, source_target_pairs={{0,5},{1,4},{2,7},{3,6},{4,1},{5,0},{6,3},{7,2},{8,13},{9,12},{10,... | collective-permute-start | bytes 393224 | tf_op jit(solution)/shard_map/ppermute | solution.py:21
  151.8 32.2 %collective-permute-start.28 = (bf16[128,512]{1,0:T(8,128)(2,1)S(1)}, bf16[128,512]{1,0:T(8,128)(2,1)S(1)}, u32[]{:S(2)}, u32[]{:S(2)}) collective-permute-start(bf16[128,512]{1,0:T(8,128)(2,1)S(1)} %get-tuple-element.61.refs_0_), channel_id=1, source_target_pairs={{0,16},{8,24},{16,0},{24,8},{1,17},{9,25},{17,1},{25,9},{2,18},{10... | collective-permute-start | bytes 393224 | tf_op jit(solution)/shard_map/ppermute | solution.py:21
  161.8 20.1 %collective-permute-start.26 = (bf16[128,512]{1,0:T(8,128)(2,1)S(1)}, bf16[128,512]{1,0:T(8,128)(2,1)S(1)}, u32[]{:S(2)}, u32[]{:S(2)}) collective-permute-start(bf16[128,512]{1,0:T(8,128)(2,1)S(1)} %get-tuple-element.71), channel_id=1, source_target_pairs={{0,6},{1,7},{2,4},{3,5},{4,2},{5,3},{6,0},{7,1},{8,14},{9,15},{10,... | collective-permute-start | bytes 393224 | tf_op jit(solution)/shard_map/ppermute | solution.py:21
  164.0 19.4 %collective-permute-start.27 = (bf16[128,512]{1,0:T(8,128)(2,1)S(1)}, bf16[128,512]{1,0:T(8,128)(2,1)S(1)}, u32[]{:S(2)}, u32[]{:S(2)}) collective-permute-start(bf16[128,512]{1,0:T(8,128)(2,1)S(1)} %get-tuple-element.72), channel_id=1, source_target_pairs={{0,7},{1,6},{2,5},{3,4},{4,3},{5,2},{6,1},{7,0},{8,15},{9,14},{10,... | collective-permute-start | bytes 393224 | tf_op jit(solution)/shard_map/ppermute | solution.py:21
  (45 other events, 361.5 us)
